TPU v7x, 32 devices: a whole 2x2x4 slice. The times are simulated.
32 devices in a mesh: section: 2 (over y), tensor: 4 (over z), fsdp: 4 (over x, core).
Axes of the slice: x: 2, y: 2, z: 4, core: 2. Of those that a mesh axis runs over, the one named last changes fastest.
Arguments:
- images: bfloat16 [2, 4, 729, 1152], P(None, 'fsdp'), may hold values from -6 to 6
- cotangent: bfloat16 [2, 4, 729, 1152], P(None, 'fsdp'), may hold values from -6 to 6
- qkv_weight: bfloat16 [2, 3, 1152, 1152], P('section', None, 'fsdp', 'tensor'), may hold values from -1 to 1
- qv_bias: bfloat16 [2, 2, 1152], P('section', None, 'tensor'), may hold values from -3 to 3
- out_weight: bfloat16 [2, 1152, 1152], P('section', 'tensor', 'fsdp'), may hold values from -0.75 to 0.75
- up_weight: bfloat16 [2, 1152, 4304], P('section', 'fsdp', 'tensor'), may hold values from -0.1875 to 0.1875
- up_bias: bfloat16 [2, 4304], P('section', 'tensor'), may hold values from -3 to 3
- down_weight: bfloat16 [2, 4304, 1152], P('section', 'tensor', 'fsdp'), may hold values from -0.09375 to 0.09375
- gains: bfloat16 [2, 2, 1152], P('section', None, 'fsdp'), may hold values from 0.099609375 to 1.8984375
- shifts: bfloat16 [2, 4, 1152], P('section', None, 'fsdp'), may hold values from -3 to 3
Outputs:
- section_outputs: bfloat16 [2, 2, 4, 729, 1152], P('section', None, 'fsdp')
- input_grads: bfloat16 [2, 2, 4, 729, 1152], P('section', None, 'fsdp')
- grad_qkv: float32 [2, 3, 1152, 1152], P('section', None, 'fsdp', 'tensor')
- grad_qv_bias: float32 [2, 2, 1152], P('section', None, 'tensor')
- grad_out: float32 [2, 1152, 1152], P('section', 'tensor', 'fsdp')
- grad_up: float32 [2, 1152, 4304], P('section', 'fsdp', 'tensor')
- grad_up_bias: float32 [2, 4304], P('section', 'tensor')
- grad_down: float32 [2, 4304, 1152], P('section', 'tensor', 'fsdp')
- grad_gains: float32 [2, 2, 1152], P('section', None, 'fsdp')
- grad_shifts: float32 [2, 4, 1152], P('section', None, 'fsdp')
All inputs are finite; a program needn't handle non-finite values.
Results may differ from a plain program's by a relative error of at most 0.013.
Values may be sent and summed in bfloat16 or wider, within the bound.
A program may use at most 256 MiB of HBM per device.

v0:
```python
import jax
import jax.numpy as jnp
from jax import lax
from jax.sharding import PartitionSpec as P

HD = 72


NORM_EPS = 1e-06
GELU_ROOT = 0.7978845608028654
GELU_CUBIC = 0.044715


def from_behind(value, axis, steps):
    count = lax.axis_size(axis)
    leading, last = (max(0, -steps), min(count, count - steps))
    return lax.ppermute(value, axis, [(source, source + steps) for source in range(leading, last)])


def gelu_value(value):
    return 0.5 * value * (1.0 + jnp.tanh(GELU_ROOT * (value + GELU_CUBIC * value * value * value)))


def gelu_slope(value):
    inner = jnp.tanh(GELU_ROOT * (value + GELU_CUBIC * value * value * value))
    return 0.5 * (1.0 + inner) + 0.5 * value * (1.0 - inner * inner) * GELU_ROOT * (
        1.0 + 3.0 * GELU_CUBIC * value * value
    )


def norm_forward(token_rows, gain, shift):
    mean_row = jnp.mean(token_rows, axis=-1, keepdims=True)
    centred = token_rows - mean_row
    inverse = lax.rsqrt(jnp.mean(centred * centred, axis=-1, keepdims=True) + NORM_EPS)
    normed = centred * inverse
    return (normed * gain + shift, normed, inverse)


def norm_backward(grad_normed, normed, inverse, gain):
    scaled = grad_normed * gain
    inner = (
        scaled
        - jnp.mean(scaled, axis=-1, keepdims=True)
        - normed * jnp.mean(scaled * normed, axis=-1, keepdims=True)
    )
    return (inverse * inner, jnp.sum(grad_normed * normed, axis=0), jnp.sum(grad_normed, axis=0))


def layer_forward(layer_input, weights, qv_bias, up_bias):
    qkv_weight, out_weight, up_weight, down_weight, gains, shifts = weights
    image_count, seq_len, model_width = layer_input.shape
    local_heads = qkv_weight.shape[2] // HD
    score_scale = HD ** (-0.5)
    gain_rows = gains.astype(jnp.float32)
    shift_rows = shifts.astype(jnp.float32)
    token_rows = layer_input.astype(jnp.float32).reshape(-1, model_width)
    normed_one = norm_forward(token_rows, gain_rows[0], shift_rows[0])[0].astype(jnp.bfloat16)
    projected = jnp.einsum(
        "td,cde->cte", normed_one, qkv_weight, preferred_element_type=jnp.float32
    )
    bias_rows = qv_bias.astype(jnp.float32)
    queries = (projected[0] + bias_rows[0]).astype(jnp.bfloat16)
    key_rows = projected[1].astype(jnp.bfloat16)
    values = (projected[2] + bias_rows[1]).astype(jnp.bfloat16)
    head_shape = (image_count, seq_len, local_heads, HD)
    scores = (
        jnp.einsum(
            "bqhd,bkhd->bhqk",
            queries.reshape(head_shape),
            key_rows.reshape(head_shape),
            preferred_element_type=jnp.float32,
        )
        * score_scale
    )
    row_max = jnp.max(scores, axis=-1, keepdims=True)
    exp_scores = jnp.exp(scores - row_max)
    row_total = jnp.sum(exp_scores, axis=-1, keepdims=True)
    attn_probs = (exp_scores / row_total).astype(jnp.bfloat16)
    log_total = row_max + jnp.log(row_total)
    context = jnp.einsum(
        "bhqk,bkhd->bqhd",
        attn_probs,
        values.reshape(head_shape),
        preferred_element_type=jnp.float32,
    )
    context = context.astype(jnp.bfloat16).reshape(-1, local_heads * HD)
    attn_term = jnp.dot(context, out_weight, preferred_element_type=jnp.float32)
    hidden = token_rows + lax.psum(attn_term, "tensor") + shift_rows[1]
    normed_two = norm_forward(hidden, gain_rows[1], shift_rows[2])[0].astype(jnp.bfloat16)
    pre_act = jnp.dot(normed_two, up_weight, preferred_element_type=jnp.float32) + up_bias.astype(
        jnp.float32
    )
    active = gelu_value(pre_act).astype(jnp.bfloat16)
    mlp_term = jnp.dot(active, down_weight, preferred_element_type=jnp.float32)
    output_low = (hidden + lax.psum(mlp_term, "tensor") + shift_rows[3]).astype(jnp.bfloat16)
    stored = (
        layer_input,
        normed_one,
        queries,
        key_rows,
        values,
        log_total,
        context,
        hidden,
        normed_two,
        pre_act,
        active,
    )
    return (output_low, stored)


def layer_backward(grad_output, stored, weights):
    qkv_weight, out_weight, up_weight, down_weight, gains, shifts = weights
    (
        layer_input,
        normed_one,
        queries,
        key_rows,
        values,
        log_total,
        context,
        hidden,
        normed_two,
        pre_act,
        active,
    ) = stored
    image_count, seq_len, model_width = layer_input.shape
    local_heads = qkv_weight.shape[2] // HD
    score_scale = HD ** (-0.5)
    gain_rows = gains.astype(jnp.float32)
    shift_rows = shifts.astype(jnp.float32)
    grad_mix = grad_output.astype(jnp.bfloat16)
    grad_down = jnp.einsum("tf,td->fd", active, grad_mix, preferred_element_type=jnp.float32)
    grad_active = jnp.einsum("td,fd->tf", grad_mix, down_weight, preferred_element_type=jnp.float32)
    grad_pre = (grad_active * gelu_slope(pre_act)).astype(jnp.bfloat16)
    grad_up = jnp.einsum("td,tf->df", normed_two, grad_pre, preferred_element_type=jnp.float32)
    up_bias_grad = jnp.sum(grad_pre.astype(jnp.float32), axis=0)
    two_term = jnp.einsum("tf,df->td", grad_pre, up_weight, preferred_element_type=jnp.float32)
    centred_two, inverse_two = norm_forward(hidden, gain_rows[1], shift_rows[2])[1:]
    grad_normed_two = lax.psum(two_term, "tensor")
    from_two, gain_two_grad, shift_two_grad = norm_backward(
        grad_normed_two, centred_two, inverse_two, gain_rows[1]
    )
    grad_hidden = grad_output + from_two
    grad_attn = grad_hidden.astype(jnp.bfloat16)
    attn_shift_grad = jnp.sum(grad_attn.astype(jnp.float32), axis=0)
    mix_shift_grad = jnp.sum(grad_mix.astype(jnp.float32), axis=0)
    grad_out = jnp.einsum("te,td->ed", context, grad_attn, preferred_element_type=jnp.float32)
    grad_context = jnp.einsum(
        "td,ed->te", grad_attn, out_weight, preferred_element_type=jnp.float32
    ).astype(jnp.bfloat16)
    head_shape = (image_count, seq_len, local_heads, HD)
    query_heads = queries.reshape(head_shape)
    key_heads = key_rows.reshape(head_shape)
    value_heads = values.reshape(head_shape)
    context_grads = grad_context.reshape(head_shape)
    scores = (
        jnp.einsum("bqhd,bkhd->bhqk", query_heads, key_heads, preferred_element_type=jnp.float32)
        * score_scale
    )
    probs_full = jnp.exp(scores - log_total)
    mixed = jnp.einsum(
        "bqhd,bkhd->bhqk", context_grads, value_heads, preferred_element_type=jnp.float32
    )
    row_delta = jnp.sum(mixed * probs_full, axis=-1, keepdims=True)
    grad_scores = (probs_full * (mixed - row_delta)).astype(jnp.bfloat16)
    grad_values = jnp.einsum(
        "bhqk,bqhd->bkhd",
        probs_full.astype(jnp.bfloat16),
        context_grads,
        preferred_element_type=jnp.float32,
    ).astype(jnp.bfloat16)
    grad_queries = (
        jnp.einsum("bhqk,bkhd->bqhd", grad_scores, key_heads, preferred_element_type=jnp.float32)
        * score_scale
    ).astype(jnp.bfloat16)
    grad_keys = (
        jnp.einsum("bhqk,bqhd->bkhd", grad_scores, query_heads, preferred_element_type=jnp.float32)
        * score_scale
    ).astype(jnp.bfloat16)
    flat_shape = (-1, local_heads * HD)
    grad_proj = jnp.stack(
        [
            grad_queries.reshape(flat_shape),
            grad_keys.reshape(flat_shape),
            grad_values.reshape(flat_shape),
        ]
    )
    grad_qkv = jnp.einsum("td,cte->cde", normed_one, grad_proj, preferred_element_type=jnp.float32)
    qv_bias_grad = jnp.stack(
        [
            jnp.sum(grad_proj[0].astype(jnp.float32), axis=0),
            jnp.sum(grad_proj[2].astype(jnp.float32), axis=0),
        ]
    )
    one_term = jnp.einsum("cte,cde->td", grad_proj, qkv_weight, preferred_element_type=jnp.float32)
    token_rows = layer_input.astype(jnp.float32).reshape(-1, model_width)
    grad_normed_one = lax.psum(one_term, "tensor")
    centred_one, inverse_one = norm_forward(token_rows, gain_rows[0], shift_rows[0])[1:]
    from_one, gain_one_grad, shift_one_grad = norm_backward(
        grad_normed_one, centred_one, inverse_one, gain_rows[0]
    )
    grad_low = (grad_hidden + from_one).astype(jnp.bfloat16)
    grad_gains = jnp.stack([gain_one_grad, gain_two_grad])
    grad_shifts = jnp.stack([shift_one_grad, attn_shift_grad, shift_two_grad, mix_shift_grad])
    return (
        grad_low,
        (grad_qkv, grad_out, grad_up, grad_down, grad_gains, grad_shifts),
        (qv_bias_grad, up_bias_grad),
    )


def per_device(
    images,
    cotangent,
    qkv_weight,
    qv_bias,
    out_weight,
    up_weight,
    up_bias,
    down_weight,
    gains,
    shifts,
):
    micro_count, image_count, seq_len, model_width = images.shape
    section_index = lax.axis_index("section")
    local_qv = qv_bias[0]
    local_up = up_bias[0]
    weights = (
        lax.all_gather(qkv_weight[0], "fsdp", axis=1, tiled=True),
        lax.all_gather(out_weight[0], "fsdp", axis=1, tiled=True),
        lax.all_gather(up_weight[0], "fsdp", axis=0, tiled=True),
        lax.all_gather(down_weight[0], "fsdp", axis=1, tiled=True),
        lax.all_gather(gains[0], "fsdp", axis=1, tiled=True),
        lax.all_gather(shifts[0], "fsdp", axis=1, tiled=True),
    )

    def forward_tick(carried, tick_index):
        own_input = lax.dynamic_index_in_dim(
            images, jnp.minimum(tick_index, micro_count - 1), 0, keepdims=False
        )
        layer_input = jnp.where(section_index == 0, own_input, carried)
        output_low, stored = layer_forward(layer_input, weights, local_qv, local_up)
        output_low = output_low.reshape(image_count, seq_len, model_width)
        passed = from_behind(output_low, "section", 1)
        return (passed, (output_low, stored))

    ticks = jnp.arange(micro_count + 1, dtype=jnp.int32)
    output_all, stored_all = lax.scan(forward_tick, jnp.zeros_like(images[0]), ticks)[1]
    section_outputs = lax.dynamic_slice_in_dim(output_all, section_index, micro_count, 0)
    start_sums = tuple((jnp.zeros(item.shape, jnp.float32) for item in weights))
    start_biases = (jnp.zeros(local_qv.shape, jnp.float32), jnp.zeros(local_up.shape, jnp.float32))

    def backward_tick(carry, tick_index):
        received, grad_sums, bias_totals = carry
        micro_index = micro_count - tick_index - section_index
        is_valid = (micro_index >= 0) & (micro_index < micro_count)
        safe_index = jnp.clip(micro_index, 0, micro_count - 1)
        own_grad = (
            lax.dynamic_index_in_dim(cotangent, safe_index, 0, keepdims=False)
            .astype(jnp.float32)
            .reshape(-1, model_width)
        )
        grad_output = jnp.where(section_index == 1, own_grad, received)
        stored = tuple(
            (
                lax.dynamic_index_in_dim(item, safe_index + section_index, 0, keepdims=False)
                for item in stored_all
            )
        )
        grad_low, grads, biases = layer_backward(grad_output, stored, weights)
        grads = tuple((jnp.where(is_valid, item, 0.0) for item in grads))
        biases = tuple((jnp.where(is_valid, item, 0.0) for item in biases))
        grad_low = grad_low.reshape(image_count, seq_len, model_width)
        passed = from_behind(grad_low, "section", -1).astype(jnp.float32).reshape(-1, model_width)
        grad_sums = tuple((first + second for first, second in zip(grad_sums, grads)))
        bias_totals = tuple((first + second for first, second in zip(bias_totals, biases)))
        return ((passed, grad_sums, bias_totals), grad_low)

    start_grad = jnp.zeros((image_count * seq_len, model_width), jnp.float32)
    finished, grad_all = lax.scan(backward_tick, (start_grad, start_sums, start_biases), ticks)
    grad_sums, bias_totals = (finished[1], finished[2])
    final_grads = (
        lax.psum_scatter(
            grad_sums[0].astype(jnp.bfloat16), "fsdp", scatter_dimension=1, tiled=True
        ).astype(jnp.float32),
        lax.psum_scatter(
            grad_sums[1].astype(jnp.bfloat16), "fsdp", scatter_dimension=1, tiled=True
        ).astype(jnp.float32),
        lax.psum_scatter(
            grad_sums[2].astype(jnp.bfloat16), "fsdp", scatter_dimension=0, tiled=True
        ).astype(jnp.float32),
        lax.psum_scatter(
            grad_sums[3].astype(jnp.bfloat16), "fsdp", scatter_dimension=1, tiled=True
        ).astype(jnp.float32),
        lax.psum_scatter(
            grad_sums[4].astype(jnp.bfloat16), "fsdp", scatter_dimension=1, tiled=True
        ).astype(jnp.float32),
        lax.psum_scatter(
            grad_sums[5].astype(jnp.bfloat16), "fsdp", scatter_dimension=1, tiled=True
        ).astype(jnp.float32),
    )
    final_biases = lax.psum((bias_totals[0], bias_totals[1]), "fsdp")
    gain_grads, shift_grads = (final_grads[4], final_grads[5])
    input_grads = jnp.flip(lax.dynamic_slice_in_dim(grad_all, 1 - section_index, micro_count, 0), 0)
    return (
        section_outputs[None],
        input_grads[None],
        final_grads[0][None],
        final_biases[0][None],
        final_grads[1][None],
        final_grads[2][None],
        final_biases[1][None],
        final_grads[3][None],
        gain_grads[None],
        shift_grads[None],
    )


def solution(mesh):
    return jax.shard_map(
        per_device,
        mesh=mesh,
        in_specs=(
            P(None, "fsdp", None, None),
            P(None, "fsdp", None, None),
            P("section", None, "fsdp", "tensor"),
            P("section", None, "tensor"),
            P("section", "tensor", "fsdp"),
            P("section", "fsdp", "tensor"),
            P("section", "tensor"),
            P("section", "tensor", "fsdp"),
            P("section", None, "fsdp"),
            P("section", None, "fsdp"),
        ),
        out_specs=(
            P("section", None, "fsdp", None, None),
            P("section", None, "fsdp", None, None),
            P("section", None, "fsdp", "tensor"),
            P("section", None, "tensor"),
            P("section", "tensor", "fsdp"),
            P("section", "fsdp", "tensor"),
            P("section", "tensor"),
            P("section", "tensor", "fsdp"),
            P("section", None, "fsdp"),
            P("section", None, "fsdp"),
        ),
        check_vma=False,
    )
```

profile of v0, /device:TPU:0, one launch (start us, length us, event | category | flops | bytes accessed | tf_op | source)
XLA Modules:
  0.0 2444.3 jit_solution(16826438468239682339)
XLA Ops:
  83.8 22.2 all-gather.12.cloned.1.call-done
  112.5 1034.5 %while.66 = (s32[]{:T(128)}, bf16[1,729,1152]{2,1,0:T(8,128)(2,1)}, bf16[3,1,729,1152]{3,2,1,0:T(8,128)(2,1)}, bf16[3,1,729,1152]{3,2,1,0:T(8,128)(2,1)}, bf16[3...) while((s32[]{:T(128)}, bf16[1,729,1152]{2,1,0:T(8,128)(2,1)}, ...), condition=%wide.region_9.10_spmd, body=%wide.region_0.9_spmd.sunk | while | flops 6232035840 | bytes 263704656 | solution.py:249
  145.6 130.7 %all-reduce.6.cloned.1.call-done = f32[729,1152]{1,0:T(8,128)} async-done(((f32[729,1152]{1,0:T(8,128)}), f32[729,1152]{1,0:T(8,128)}) %all-reduce.6.cloned.1.call-update) | async-done | bytes 3359248 | tf_op jit(solution)/shard_map/while/body/eval_jaxpr/psum | solution.py:88
  297.6 124.3 %all-reduce.8.cloned.1.call-done = f32[729,1152]{1,0:T(8,128)} async-done(((f32[729,1152]{1,0:T(8,128)}), f32[729,1152]{1,0:T(8,128)}) %all-reduce.8.cloned.1.call-update) | async-done | bytes 3359248 | tf_op jit(solution)/shard_map/while/body/eval_jaxpr/psum | solution.py:95
  436.2 29.8 %collective-permute-done = bf16[1,729,1152]{2,1,0:T(8,128)(2,1)} collective-permute-done((bf16[1,729,1152]{2,1,0:T(8,128)(2,1)}, bf16[1,729,1152]{2,1,0:T(8,128)(2,1)}, u32[]{:S(2)}, u32[]{:S(2)}) %collective-permute-start) | collective-permute-done | bytes 1679648 | tf_op jit(solution)/shard_map/while/body/eval_jaxpr/ppermute | solution.py:17
  486.1 130.8 %all-reduce.6.cloned.1.call-done = f32[729,1152]{1,0:T(8,128)} async-done(((f32[729,1152]{1,0:T(8,128)}), f32[729,1152]{1,0:T(8,128)}) %all-reduce.6.cloned.1.call-update) | async-done | bytes 3359248 | tf_op jit(solution)/shard_map/while/body/eval_jaxpr/psum | solution.py:88
  638.1 124.4 %all-reduce.8.cloned.1.call-done = f32[729,1152]{1,0:T(8,128)} async-done(((f32[729,1152]{1,0:T(8,128)}), f32[729,1152]{1,0:T(8,128)}) %all-reduce.8.cloned.1.call-update) | async-done | bytes 3359248 | tf_op jit(solution)/shard_map/while/body/eval_jaxpr/psum | solution.py:95
  776.8 29.7 %collective-permute-done = bf16[1,729,1152]{2,1,0:T(8,128)(2,1)} collective-permute-done((bf16[1,729,1152]{2,1,0:T(8,128)(2,1)}, bf16[1,729,1152]{2,1,0:T(8,128)(2,1)}, u32[]{:S(2)}, u32[]{:S(2)}) %collective-permute-start) | collective-permute-done | bytes 1679648 | tf_op jit(solution)/shard_map/while/body/eval_jaxpr/ppermute | solution.py:17
  826.6 130.8 %all-reduce.6.cloned.1.call-done = f32[729,1152]{1,0:T(8,128)} async-done(((f32[729,1152]{1,0:T(8,128)}), f32[729,1152]{1,0:T(8,128)}) %all-reduce.6.cloned.1.call-update) | async-done | bytes 3359248 | tf_op jit(solution)/shard_map/while/body/eval_jaxpr/psum | solution.py:88
  978.7 124.3 %all-reduce.8.cloned.1.call-done = f32[729,1152]{1,0:T(8,128)} async-done(((f32[729,1152]{1,0:T(8,128)}), f32[729,1152]{1,0:T(8,128)}) %all-reduce.8.cloned.1.call-update) | async-done | bytes 3359248 | tf_op jit(solution)/shard_map/while/body/eval_jaxpr/psum | solution.py:95
  1117.1 29.7 %collective-permute-done = bf16[1,729,1152]{2,1,0:T(8,128)(2,1)} collective-permute-done((bf16[1,729,1152]{2,1,0:T(8,128)(2,1)}, bf16[1,729,1152]{2,1,0:T(8,128)(2,1)}, u32[]{:S(2)}, u32[]{:S(2)}) %collective-permute-start) | collective-permute-done | bytes 1679648 | tf_op jit(solution)/shard_map/while/body/eval_jaxpr/ppermute | solution.py:17
  1149.9 1104.1 %while.67 = (s32[]{:T(128)}, f32[729,1152]{1,0:T(8,128)S(1)}, f32[3,1152,288]{1,2,0:T(8,128)}, f32[288,1152]{1,0:T(8,128)}, f32[1152,1076]{0,1:T(8,128)}, /*inde...) while((s32[]{:T(128)}, f32[729,1152]{1,0:T(8,128)S(1)}, ...), condition=%wide.region_31.32_spmd.clone, body=%wide.region_10.31_spmd.clone.sunk | while | flops 12738733056 | bytes 490833920 | solution.py:281
  1200.5 115.7 %all-reduce.10.cloned.1.call-done = f32[729,1152]{1,0:T(8,128)} async-done(((f32[729,1152]{1,0:T(8,128)}), f32[729,1152]{1,0:T(8,128)}) %all-reduce.10.cloned.1.call-update) | async-done | bytes 3359248 | tf_op jit(solution)/shard_map/while/body/eval_jaxpr/psum | solution.py:140
  1378.7 106.2 %all-reduce.12.cloned.1.call-done = f32[729,1152]{1,0:T(8,128)} async-done(((f32[729,1152]{1,0:T(8,128)}), f32[729,1152]{1,0:T(8,128)}) %all-reduce.12.cloned.1.call-update) | async-done | bytes 3359248 | tf_op jit(solution)/shard_map/while/body/eval_jaxpr/psum | solution.py:198
  1498.5 34.7 %collective-permute-done.1 = bf16[1,729,1152]{2,1,0:T(8,128)(2,1)S(1)} collective-permute-done((bf16[1,729,1152]{2,1,0:T(8,128)(2,1)S(1)}, bf16[1,729,1152]{2,1,0:T(8,128)(2,1)S(1)}, u32[]{:S(2)}, u32[]{:S(2)}) %collective-permute-start.1) | collective-permute-done | bytes 1679648 | tf_op jit(solution)/shard_map/while/body/eval_jaxpr/ppermute | solution.py:17
  1562.8 113.6 %all-reduce.10.cloned.1.call-done = f32[729,1152]{1,0:T(8,128)} async-done(((f32[729,1152]{1,0:T(8,128)}), f32[729,1152]{1,0:T(8,128)}) %all-reduce.10.cloned.1.call-update) | async-done | bytes 3359248 | tf_op jit(solution)/shard_map/while/body/eval_jaxpr/psum | solution.py:140
  1740.9 104.2 %all-reduce.12.cloned.1.call-done = f32[729,1152]{1,0:T(8,128)} async-done(((f32[729,1152]{1,0:T(8,128)}), f32[729,1152]{1,0:T(8,128)}) %all-reduce.12.cloned.1.call-update) | async-done | bytes 3359248 | tf_op jit(solution)/shard_map/while/body/eval_jaxpr/psum | solution.py:198
  1858.7 34.7 %collective-permute-done.1 = bf16[1,729,1152]{2,1,0:T(8,128)(2,1)S(1)} collective-permute-done((bf16[1,729,1152]{2,1,0:T(8,128)(2,1)S(1)}, bf16[1,729,1152]{2,1,0:T(8,128)(2,1)S(1)}, u32[]{:S(2)}, u32[]{:S(2)}) %collective-permute-start.1) | collective-permute-done | bytes 1679648 | tf_op jit(solution)/shard_map/while/body/eval_jaxpr/ppermute | solution.py:17
  1922.9 113.6 %all-reduce.10.cloned.1.call-done = f32[729,1152]{1,0:T(8,128)} async-done(((f32[729,1152]{1,0:T(8,128)}), f32[729,1152]{1,0:T(8,128)}) %all-reduce.10.cloned.1.call-update) | async-done | bytes 3359248 | tf_op jit(solution)/shard_map/while/body/eval_jaxpr/psum | solution.py:140
  2100.9 104.2 %all-reduce.12.cloned.1.call-done = f32[729,1152]{1,0:T(8,128)} async-done(((f32[729,1152]{1,0:T(8,128)}), f32[729,1152]{1,0:T(8,128)}) %all-reduce.12.cloned.1.call-update) | async-done | bytes 3359248 | tf_op jit(solution)/shard_map/while/body/eval_jaxpr/psum | solution.py:198
  2218.7 34.7 %collective-permute-done.1 = bf16[1,729,1152]{2,1,0:T(8,128)(2,1)S(1)} collective-permute-done((bf16[1,729,1152]{2,1,0:T(8,128)(2,1)S(1)}, bf16[1,729,1152]{2,1,0:T(8,128)(2,1)S(1)}, u32[]{:S(2)}, u32[]{:S(2)}) %collective-permute-start.1) | collective-permute-done | bytes 1679648 | tf_op jit(solution)/shard_map/while/body/eval_jaxpr/ppermute | solution.py:17
  2296.5 31.6 %rev.4 = bf16[2,1,729,1152]{3,0,2,1:T(2,128)(2,1)} reverse(bf16[2,1,729,1152]{3,0,2,1:T(2,128)(2,1)} %constant_dynamic-slice_fusion.3), dimensions={0} | reverse | bytes 6718464 | tf_op jit(solution)/shard_map/jit(_flip)/rev | solution.py:305
  2364.7 32.0 %reduce-scatter.23.cloned.1.call-done = bf16[288,1076]{1,0:T(8,128)(2,1)} async-done(((bf16[1152,1076]{1,0:T(8,128)(2,1)}), bf16[288,1076]{1,0:T(8,128)(2,1)}) %reduce-scatter.23.cloned.1.call-update) | async-done | bytes 619792
  2399.9 34.1 %reduce-scatter.25.cloned.1.call-done = bf16[288,1076]{1,0:T(8,128)(2,1)} async-done(((bf16[1152,1076]{1,0:T(8,128)(2,1)}), bf16[288,1076]{1,0:T(8,128)(2,1)}) %reduce-scatter.25.cloned.1.call-update) | async-done | bytes 619792
  (798 shorter events, 651.7 us)
Async XLA Ops:
  7.2 58.4 %all-gather.10.cloned.1.call-start = ((), (), s32[]{:S(2)}) async-start(), calls=%async_computation.6 | async-start | bytes 4423680 | tf_op jit(solution)/shard_map/all_gather | solution.py:230
  9.8 68.9 %all-gather.14.cloned.1.call-start = ((), (), s32[]{:S(2)}) async-start(), calls=%async_computation.8 | async-start | bytes 3317760 | tf_op jit(solution)/shard_map/all_gather | solution.py:233
  10.5 95.4 %all-gather.12.cloned.1.call-start = ((), (), s32[]{:S(2)}) async-start(), calls=%async_computation.7 | async-start | bytes 3317760 | tf_op jit(solution)/shard_map/all_gather | solution.py:232
  125.5 150.8 %all-reduce.6.cloned.1.call-start = ((), (), s32[]{:S(2)}) async-start(), calls=%async_computation.15 | async-start | bytes 6782976 | tf_op jit(solution)/shard_map/while/body/eval_jaxpr/psum | solution.py:88
  145.5 276.4 %all-reduce.8.cloned.1.call-start = ((), (), s32[]{:S(2)}) async-start(), calls=%async_computation.16 | async-start | bytes 6782976 | tf_op jit(solution)/shard_map/while/body/eval_jaxpr/psum | solution.py:95
  466.0 150.8 %all-reduce.6.cloned.1.call-start = ((), (), s32[]{:S(2)}) async-start(), calls=%async_computation.15 | async-start | bytes 6782976 | tf_op jit(solution)/shard_map/while/body/eval_jaxpr/psum | solution.py:88
  486.0 276.4 %all-reduce.8.cloned.1.call-start = ((), (), s32[]{:S(2)}) async-start(), calls=%async_computation.16 | async-start | bytes 6782976 | tf_op jit(solution)/shard_map/while/body/eval_jaxpr/psum | solution.py:95
  806.5 150.8 %all-reduce.6.cloned.1.call-start = ((), (), s32[]{:S(2)}) async-start(), calls=%async_computation.15 | async-start | bytes 6782976 | tf_op jit(solution)/shard_map/while/body/eval_jaxpr/psum | solution.py:88
  826.5 276.4 %all-reduce.8.cloned.1.call-start = ((), (), s32[]{:S(2)}) async-start(), calls=%async_computation.16 | async-start | bytes 6782976 | tf_op jit(solution)/shard_map/while/body/eval_jaxpr/psum | solution.py:95
  1171.3 144.9 %all-reduce.10.cloned.1.call-start = ((), (), s32[]{:S(2)}) async-start(), calls=%async_computation.17 | async-start | bytes 6782976 | tf_op jit(solution)/shard_map/while/body/eval_jaxpr/psum | solution.py:140
  1186.8 298.1 %all-reduce.12.cloned.1.call-start = ((), (), s32[]{:S(2)}) async-start(), calls=%async_computation.18 | async-start | bytes 6782976 | tf_op jit(solution)/shard_map/while/body/eval_jaxpr/psum | solution.py:198
  1492.7 40.5 %collective-permute-start.1 = (bf16[1,729,1152]{2,1,0:T(8,128)(2,1)S(1)}, bf16[1,729,1152]{2,1,0:T(8,128)(2,1)S(1)}, u32[]{:S(2)}, u32[]{:S(2)}) collective-permute-start(bf16[1,729,1152]{2,1,0:T(8,128)(2,1)S(1)} %bitcast.382), channel_id=1, source_target_pairs={{16,0},{17,1},{18,2},{19,3},{20,4},{21,5},{22,6},{23,7},{24,8},{25... | collective-permute-start | bytes 5038856 | tf_op jit(solution)/shard_map/while/body/eval_jaxpr/ppermute | solution.py:17
  1533.4 143.0 %all-reduce.10.cloned.1.call-start = ((), (), s32[]{:S(2)}) async-start(), calls=%async_computation.17 | async-start | bytes 6782976 | tf_op jit(solution)/shard_map/while/body/eval_jaxpr/psum | solution.py:140
  1548.9 296.2 %all-reduce.12.cloned.1.call-start = ((), (), s32[]{:S(2)}) async-start(), calls=%async_computation.18 | async-start | bytes 6782976 | tf_op jit(solution)/shard_map/while/body/eval_jaxpr/psum | solution.py:198
  1852.9 40.5 %collective-permute-start.1 = (bf16[1,729,1152]{2,1,0:T(8,128)(2,1)S(1)}, bf16[1,729,1152]{2,1,0:T(8,128)(2,1)S(1)}, u32[]{:S(2)}, u32[]{:S(2)}) collective-permute-start(bf16[1,729,1152]{2,1,0:T(8,128)(2,1)S(1)} %bitcast.382), channel_id=1, source_target_pairs={{16,0},{17,1},{18,2},{19,3},{20,4},{21,5},{22,6},{23,7},{24,8},{25... | collective-permute-start | bytes 5038856 | tf_op jit(solution)/shard_map/while/body/eval_jaxpr/ppermute | solution.py:17
  1893.6 143.0 %all-reduce.10.cloned.1.call-start = ((), (), s32[]{:S(2)}) async-start(), calls=%async_computation.17 | async-start | bytes 6782976 | tf_op jit(solution)/shard_map/while/body/eval_jaxpr/psum | solution.py:140
  1909.1 296.0 %all-reduce.12.cloned.1.call-start = ((), (), s32[]{:S(2)}) async-start(), calls=%async_computation.18 | async-start | bytes 6782976 | tf_op jit(solution)/shard_map/while/body/eval_jaxpr/psum | solution.py:198
  2212.9 40.5 %collective-permute-start.1 = (bf16[1,729,1152]{2,1,0:T(8,128)(2,1)S(1)}, bf16[1,729,1152]{2,1,0:T(8,128)(2,1)S(1)}, u32[]{:S(2)}, u32[]{:S(2)}) collective-permute-start(bf16[1,729,1152]{2,1,0:T(8,128)(2,1)S(1)} %bitcast.382), channel_id=1, source_target_pairs={{16,0},{17,1},{18,2},{19,3},{20,4},{21,5},{22,6},{23,7},{24,8},{25... | collective-permute-start | bytes 5038856 | tf_op jit(solution)/shard_map/while/body/eval_jaxpr/ppermute | solution.py:17
  2254.0 87.3 %reduce-scatter.27.cloned.1.call-start = ((), (), s32[]{:S(2)}) async-start(), calls=%async_computation.13 | async-start | bytes 368640
  2255.0 87.9 %reduce-scatter.29.cloned.1.call-start = ((), (), s32[]{:S(2)}) async-start(), calls=%async_computation.14 | async-start | bytes 368640
  2256.0 88.4 %reduce-scatter.21.cloned.1.call-start = ((), (), s32[]{:S(2)}) async-start(), calls=%async_computation.10 | async-start | bytes 1105920
  2258.7 100.9 %reduce-scatter.19.cloned.1.call-start = ((), (), s32[]{:S(2)}) async-start(), calls=%async_computation.9 | async-start | bytes 2580480
  2272.6 124.2 %reduce-scatter.23.cloned.1.call-start = ((), (), s32[]{:S(2)}) async-start(), calls=%async_computation.11 | async-start | bytes 3317760
  2278.6 155.4 %reduce-scatter.25.cloned.1.call-start = ((), (), s32[]{:S(2)}) async-start(), calls=%async_computation.12 | async-start | bytes 3317760
  (210 other events, 2190.6 us)
Sparse Core Ops, SparseCore 0:
  10.1 40.3 all-gather.9
  52.1 26.5 all-gather.13
  80.2 25.7 all-gather.11
  145.7 130.6 all-reduce.5
  293.7 128.1 all-reduce.7
  486.1 130.6 all-reduce.5
  634.2 128.1 all-reduce.7
  826.7 130.6 all-reduce.5
  974.8 128.1 all-reduce.7
  1186.9 129.2 all-reduce.9
  1357.6 127.2 all-reduce.11
  1549.1 127.3 all-reduce.9
  1717.8 127.2 all-reduce.11
  1909.2 127.3 all-reduce.9
  2077.8 127.2 all-reduce.11
  2257.6 18.3 reduce-scatter.26
  2278.9 20.2 reduce-scatter.28
  2302.2 23.7 reduce-scatter.20
  2328.6 30.9 reduce-scatter.18
  2362.0 34.7 reduce-scatter.22
  2399.3 34.7 reduce-scatter.24
where the time goes:
time: 2450 us; the launch traced here: 2440 us
  waiting for transfers between devices  1730 us (71%)
  matrix products  218 us (9%)
  other arithmetic  196 us (8%)
  local copies, waits for them, and re-layouts  184 us (8%)
  blocking collectives  46.4 us (2%)
  loops' own time  41.8 us (2%)
    psum x3, waiting for transfers between devices, layer_forward(): hidden = token_rows + lax.psum(attn_term, 'tensor') + shift_rows[1]  392 us
    psum x3, waiting for transfers between devices, layer_forward(): lax.psum(mlp_term, 'tensor')  373 us
    psum x3, waiting for transfers between devices, layer_backward(): grad_normed_two = lax.psum(two_term, 'tensor')  343 us
    psum x3, waiting for transfers between devices, layer_backward(): grad_normed_one = lax.psum(one_term, 'tensor')  315 us
    ppermute x6, waiting for transfers between devices, from_behind(): lax.ppermute(value, axis, [(source, source + steps) for source in range(l...  193 us
    unnamed x15, waiting for transfers between devices  80.8 us
    dynamic_update_slice x27, other arithmetic, per_device(): lax.scan(forward_tick, jnp.zeros_like(images[0]), ticks)[1]  69.8 us
  transfers between devices with their start and end apart: 27, of which 23 were waited for; matrix products, arithmetic and copies ran while one was open for 11% of the time, Pallas kernels for 0%

commit v1 on v0

v1 whole, which is shorter than its diff:
```python
import functools

import jax
import jax.numpy as jnp
from jax import lax
from jax.experimental import pallas as pl
from jax.experimental.pallas import tpu as pltpu
from jax.sharding import PartitionSpec as P

HD = 72


NORM_EPS = 1e-06
GELU_ROOT = 0.7978845608028654
GELU_CUBIC = 0.044715
F32 = jnp.float32
BF16 = jnp.bfloat16


MESH = pl.DeviceIdType.MESH
TILE = 16


def greet(me, count):
    barrier = pltpu.get_barrier_semaphore()
    for there, other in ((me > 0, me - 1), (me < count - 1, me + 1)):
        @pl.when(there)
        def _():
            pl.semaphore_signal(barrier, inc=1, device_id={"tensor": other}, device_id_type=MESH)
    peers = (me > 0).astype(jnp.int32) + (me < count - 1).astype(jnp.int32)
    pl.semaphore_wait(barrier, peers)

def line_sum_kernel(count, rows, lag, x_ref, o_ref, come, gone, red_send, red_recv, out_send, out_recv):
    me = lax.axis_index("tensor")
    greet(me, count)
    pieces = x_ref.shape[0] // rows

    def span(piece):
        return pl.ds(pl.multiple_of(piece * rows, rows), rows)

    def send(piece, source, target, step, out):
        sems = (out_send, out_recv) if out else (red_send, red_recv)
        return pltpu.make_async_remote_copy(
            src_ref=source.at[span(piece)],
            dst_ref=target.at[span(piece)],
            send_sem=sems[0].at[piece],
            recv_sem=sems[1].at[piece],
            device_id={"tensor": me + step},
            device_id_type=MESH,
        )

    def place(step):
        return me if step > 0 else count - 1 - me

    def reduce_step(index, step):
        piece = 2 * index + (step < 0)
        ok = (index >= 0) & (piece < pieces)
        pos = place(step)

        @pl.when(ok & (pos == 0))
        def _():
            send(piece, x_ref, come, step, False).start()

        def add():
            send(piece, come, come, step, False).wait_recv()
            return (x_ref[span(piece), :].astype(F32) + come[span(piece), :].astype(F32)).astype(BF16)

        @pl.when(ok & (pos > 0) & (pos < count - 1))
        def _():
            gone[span(piece), :] = add()
            send(piece, gone, come, step, False).start()

        @pl.when(ok & (pos == count - 1))
        def _():
            o_ref[span(piece), :] = add()
            send(piece, o_ref, o_ref, -step, True).start()

    def out_step(index, step):
        piece = 2 * index + (step < 0)
        ok = (index >= 0) & (piece < pieces)
        pos = place(step)

        @pl.when(ok & (pos < count - 1))
        def _():
            send(piece, o_ref, o_ref, -step, True).wait_recv()

        @pl.when(ok & (pos > 0) & (pos < count - 1))
        def _():
            send(piece, o_ref, o_ref, -step, True).start()

    pairs = (pieces + 1) // 2

    def turn(s, _):
        for step in (1, -1):
            reduce_step(s - lag * place(step), step)
        for step in (1, -1):
            out_step(s - lag * (count - 1) - lag * (count - 1 - place(step)), step)
        return 0

    lax.fori_loop(0, pairs + 2 * lag * (count - 1), turn, 0)

    def end_steps(i, _):
        for step in (1, -1):
            piece = 2 * i + (step < 0)
            pos = place(step)

            @pl.when((piece < pieces) & (pos < count - 1))
            def _():
                send(piece, x_ref, come, step, False).wait_send()

            @pl.when((piece < pieces) & (pos > 0))
            def _():
                send(piece, o_ref, o_ref, -step, True).wait_send()
        return 0

    lax.fori_loop(0, pairs, end_steps, 0)


def line_sum(x, cid, rows=16, lag=4):
    count = lax.axis_size("tensor")
    pieces = x.shape[0] // rows
    return pl.pallas_call(
        functools.partial(line_sum_kernel, count, rows, lag),
        out_shape=jax.ShapeDtypeStruct(x.shape, BF16),
        in_specs=[pl.BlockSpec(memory_space=pltpu.VMEM)],
        out_specs=pl.BlockSpec(memory_space=pltpu.VMEM),
        scratch_shapes=[
            pltpu.VMEM(x.shape, BF16),
            pltpu.VMEM(x.shape, BF16),
        ] + [pltpu.SemaphoreType.DMA((pieces,))] * 4,
        compiler_params=pltpu.CompilerParams(collective_id=cid, has_side_effects=True),
        name="line_sum",
        cost_estimate=pl.CostEstimate(flops=0, bytes_accessed=120_000_000, transcendentals=0),
    )(x)


def tensor_sum(value):
    return line_sum(value.astype(BF16), 0).astype(F32)


def gelu_value(value):
    return 0.5 * value * (1.0 + jnp.tanh(GELU_ROOT * (value + GELU_CUBIC * value * value * value)))


def gelu_slope(value):
    inner = jnp.tanh(GELU_ROOT * (value + GELU_CUBIC * value * value * value))
    return 0.5 * (1.0 + inner) + 0.5 * value * (1.0 - inner * inner) * GELU_ROOT * (
        1.0 + 3.0 * GELU_CUBIC * value * value
    )


def norm_forward(token_rows, gain, shift):
    mean_row = jnp.mean(token_rows, axis=-1, keepdims=True)
    centred = token_rows - mean_row
    inverse = lax.rsqrt(jnp.mean(centred * centred, axis=-1, keepdims=True) + NORM_EPS)
    normed = centred * inverse
    return (normed * gain + shift, normed, inverse)


def norm_backward(grad_normed, normed, inverse, gain):
    scaled = grad_normed * gain
    inner = (
        scaled
        - jnp.mean(scaled, axis=-1, keepdims=True)
        - normed * jnp.mean(scaled * normed, axis=-1, keepdims=True)
    )
    return (inverse * inner, jnp.sum(grad_normed * normed, axis=0), jnp.sum(grad_normed, axis=0))


def dot_nn(left, right):
    return jnp.dot(left, right, preferred_element_type=F32)


def dot_nt(left, right):
    return lax.dot_general(left, right, (((1,), (1,)), ((), ())), preferred_element_type=F32)


def dot_tn(left, right):
    return lax.dot_general(left, right, (((0,), (0,)), ((), ())), preferred_element_type=F32)


def layer_forward(inputs, weights, qv_bias, up_bias, gains, shifts, cuts, real):
    qkv, out_t, up, down_t = weights
    width = qkv.shape[1] // 3
    heads = width // HD
    scale = HD ** (-0.5)
    seq_len = cuts[-1][1]
    normed_one = []
    parts = []
    for part in inputs:
        normed = norm_forward(part.astype(F32), gains[0], shifts[0])[0].astype(BF16)
        normed_one.append(normed)
        parts.append(dot_nn(normed, qkv))
    normed_one = jnp.concatenate(normed_one)
    projected = jnp.concatenate(parts)
    queries = (projected[:, :width] + qv_bias[0]).astype(BF16).reshape(seq_len, heads, HD)
    key_rows = projected[:, width : 2 * width].astype(BF16).reshape(seq_len, heads, HD)
    values = (projected[:, 2 * width :] + qv_bias[1]).astype(BF16).reshape(seq_len, heads, HD)
    context, hidden, normed_two, pre_act, active, outputs, log_total = [], [], [], [], [], [], []
    for (first, last), part in zip(cuts, inputs):
        scores = (
            jnp.einsum("qhd,khd->hqk", queries[first:last], key_rows, preferred_element_type=F32)
            * scale
        )
        scores = jnp.where(lax.broadcasted_iota(jnp.int32, scores.shape, 2) < real, scores, -1e30)
        row_max = jnp.max(scores, axis=-1, keepdims=True)
        exp_scores = jnp.exp(scores - row_max)
        row_total = jnp.sum(exp_scores, axis=-1, keepdims=True)
        probs = (exp_scores / row_total).astype(BF16)
        log_total.append(row_max + jnp.log(row_total))
        mixed = jnp.einsum("hqk,khd->qhd", probs, values, preferred_element_type=F32)
        context.append(mixed.astype(BF16).reshape(last - first, width))
        attn_term = tensor_sum(dot_nt(context[-1], out_t))
        hidden.append(part.astype(F32) + attn_term + shifts[1])
    for rows in hidden:
        normed = norm_forward(rows, gains[1], shifts[2])[0].astype(BF16)
        normed_two.append(normed)
        pre_act.append(dot_nn(normed, up) + up_bias)
        active.append(gelu_value(pre_act[-1]).astype(BF16))
        mlp_term = tensor_sum(dot_nt(active[-1], down_t))
        outputs.append((rows + mlp_term + shifts[3]).astype(BF16))
    stored = (
        inputs,
        normed_one,
        queries,
        key_rows,
        values,
        log_total,
        context,
        hidden,
        normed_two,
        pre_act,
        active,
    )
    return outputs, stored


def layer_backward(grads, stored, weights, gains, shifts, cuts, real):
    qkv, out_t, up, down_t = weights
    (
        inputs,
        normed_one,
        queries,
        key_rows,
        values,
        log_total,
        context,
        hidden,
        normed_two,
        pre_act,
        active,
    ) = stored
    width = qkv.shape[1] // 3
    scale = HD ** (-0.5)
    grad_mix = [part.astype(BF16) for part in grads]
    grad_pre = []
    two_terms = []
    for part, pre in zip(grad_mix, pre_act):
        grad_active = dot_nn(part, down_t)
        grad_pre.append((grad_active * gelu_slope(pre)).astype(BF16))
        two_terms.append(tensor_sum(dot_nt(grad_pre[-1], up)))
    mix_all = jnp.concatenate(grad_mix)
    pre_all = jnp.concatenate(grad_pre)
    grad_down = dot_tn(mix_all, jnp.concatenate(active))
    grad_up = dot_tn(jnp.concatenate(normed_two), pre_all)
    up_bias_grad = jnp.sum(pre_all.astype(F32), axis=0)
    mix_shift = jnp.sum(mix_all.astype(F32), axis=0)
    grad_hidden, grad_attn, gain_two, shift_two, attn_shift = [], [], 0.0, 0.0, 0.0
    grad_q = []
    grad_k = 0.0
    grad_v = 0.0
    for (first, last), part, two, rows, logs in zip(cuts, grads, two_terms, hidden, log_total):
        normed, inverse = norm_forward(rows, gains[1], shifts[2])[1:]
        moved, gain_part, shift_part = norm_backward(two, normed, inverse, gains[1])
        gain_two += gain_part
        shift_two += shift_part
        grad_hidden.append(part.astype(F32) + moved)
        grad_attn.append(grad_hidden[-1].astype(BF16))
        attn_shift += jnp.sum(grad_attn[-1].astype(F32), axis=0)
        grad_context = dot_nn(grad_attn[-1], out_t).astype(BF16).reshape(last - first, -1, HD)
        scores = (
            jnp.einsum("qhd,khd->hqk", queries[first:last], key_rows, preferred_element_type=F32)
            * scale
        )
        probs = jnp.exp(scores - logs)
        probs = jnp.where(lax.broadcasted_iota(jnp.int32, scores.shape, 2) < real, probs, 0.0)
        mixed = jnp.einsum("qhd,khd->hqk", grad_context, values, preferred_element_type=F32)
        row_delta = jnp.sum(mixed * probs, axis=-1, keepdims=True)
        grad_scores = (probs * (mixed - row_delta)).astype(BF16)
        grad_v += jnp.einsum("hqk,qhd->khd", probs.astype(BF16), grad_context, preferred_element_type=F32)
        grad_q.append(
            (jnp.einsum("hqk,khd->qhd", grad_scores, key_rows, preferred_element_type=F32) * scale).astype(BF16)
        )
        grad_k += jnp.einsum("hqk,qhd->khd", grad_scores, queries[first:last], preferred_element_type=F32)
    grad_proj = jnp.concatenate(
        [
            jnp.concatenate(grad_q).reshape(-1, width),
            (grad_k * scale).astype(BF16).reshape(-1, width),
            grad_v.astype(BF16).reshape(-1, width),
        ],
        axis=1,
    )
    context_all = jnp.concatenate(context)
    attn_all = jnp.concatenate(grad_attn)
    grad_out = dot_tn(attn_all, context_all)
    grad_qkv = dot_tn(normed_one, grad_proj)
    bias_sums = jnp.sum(grad_proj.astype(F32), axis=0)
    grad_inputs = []
    gain_one, shift_one = 0.0, 0.0
    one_terms = [tensor_sum(dot_nt(grad_proj[first:last], qkv)) for first, last in cuts]
    for one, part, rows in zip(one_terms, inputs, grad_hidden):
        normed, inverse = norm_forward(part.astype(F32), gains[0], shifts[0])[1:]
        moved, gain_part, shift_part = norm_backward(one, normed, inverse, gains[0])
        gain_one += gain_part
        shift_one += shift_part
        grad_inputs.append((rows + moved).astype(BF16))
    gain_grads = [gain_one, gain_two, shift_one, attn_shift, shift_two, mix_shift]
    bias_grads = jnp.concatenate([bias_sums[:width], bias_sums[2 * width :], up_bias_grad])
    return grad_inputs, (grad_qkv, grad_out, grad_up, grad_down), (jnp.concatenate(gain_grads), bias_grads)


def per_device(
    images,
    cotangent,
    qkv_weight,
    qv_bias,
    out_weight,
    up_weight,
    up_bias,
    down_weight,
    gains,
    shifts,
):
    image_count, seq_len, model_width = images.shape[1:]
    rows_here = qkv_weight.shape[2]
    width = qkv_weight.shape[3]
    units = up_weight.shape[2]
    section = lax.axis_index("section")
    fsdp = lax.axis_index("fsdp")
    is_first = section == 0
    every = ("section", "fsdp")
    padded = -(-seq_len // TILE) * TILE
    cuts = [(0, padded)]

    def gathered(piece):
        whole = lax.all_gather(piece, every, axis=0, tiled=True)
        return whole.reshape(2, -1, piece.shape[1])

    qkv = gathered(qkv_weight[0].transpose(1, 0, 2).reshape(rows_here, 3 * width))
    out_t = gathered(out_weight[0].T)
    up = gathered(up_weight[0])
    down_t = gathered(down_weight[0].T)
    scales = lax.all_gather(
        jnp.concatenate([gains[0], shifts[0]]), every, axis=0, tiled=False
    )
    scales = scales.reshape(2, -1, 6, rows_here).transpose(0, 2, 1, 3).reshape(2, 6, model_width)
    scales = scales.astype(F32)
    biases = lax.all_gather(
        jnp.concatenate([qv_bias.reshape(-1), up_bias.reshape(-1)]), "section", axis=0
    ).astype(F32)

    def padded_rows(array):
        rows = lax.dynamic_index_in_dim(array, section, 0, keepdims=False)[0]
        return jnp.pad(rows, ((0, padded - seq_len), (0, 0)))

    def layer_args(index):
        return (qkv[index], out_t[index], up[index], down_t[index])

    own = padded_rows(images)
    own_grad = padded_rows(cotangent)
    rows = [own[first:last] for first, last in cuts]
    outputs, stored = [], []
    for index in range(2):
        qv = biases[index, : 2 * width].reshape(2, width)
        rows, kept = layer_forward(
            rows, layer_args(index), qv, biases[index, 2 * width :], scales[index, :2], scales[index, 2:], cuts, seq_len
        )
        outputs.append(jnp.concatenate(rows))
        stored.append(kept)

    def swapped(pair):
        pair = [item[:seq_len] for item in pair]
        mine = jnp.where(is_first, pair[0], pair[1])
        other = lax.ppermute(jnp.where(is_first, pair[1], pair[0]), "section", [(0, 1), (1, 0)])
        return jnp.where(
            is_first, jnp.stack([mine, other]), jnp.stack([other, mine])
        )[None, :, None]

    section_outputs = swapped(outputs)
    grads = [own_grad[first:last] for first, last in cuts]
    input_grads = [None, None]
    weight_grads = [None, None]
    small = [None, None]
    for index in (1, 0):
        grads, weight_grads[index], small[index] = layer_backward(
            grads, stored[index], layer_args(index), scales[index, :2], scales[index, 2:], cuts, seq_len
        )
        input_grads[index] = jnp.concatenate(grads)
    input_grads = swapped(input_grads)

    def scattered(pair):
        pieces = [
            lax.psum_scatter(item.astype(BF16), "fsdp", scatter_dimension=0, tiled=True) for item in pair
        ]
        mine = jnp.where(is_first, pieces[0], pieces[1])
        other = lax.ppermute(jnp.where(is_first, pieces[1], pieces[0]), "section", [(0, 1), (1, 0)])
        return mine.astype(F32) + other.astype(F32)

    grad_qkv, grad_out, grad_up, grad_down = [
        scattered([weight_grads[0][place], weight_grads[1][place]]) for place in range(4)
    ]
    packed = jnp.stack([jnp.concatenate(small[0]), jnp.concatenate(small[1])])
    packed = lax.psum(packed, every)
    packed = jnp.where(is_first, packed[0], packed[1])
    norm_part = packed[: 6 * model_width].reshape(6, model_width)
    norm_part = lax.dynamic_slice_in_dim(norm_part, fsdp * rows_here, rows_here, 1)
    bias_part = packed[6 * model_width :]
    return (
        section_outputs,
        input_grads,
        grad_qkv.reshape(rows_here, 3, width).transpose(1, 0, 2)[None],
        bias_part[: 2 * width].reshape(1, 2, width),
        grad_out.T[None],
        grad_up[None],
        bias_part[2 * width :][None],
        grad_down.T[None],
        norm_part[:2][None],
        norm_part[2:][None],
    )


def solution(mesh):
    return jax.shard_map(
        per_device,
        mesh=mesh,
        in_specs=(
            P(None, "fsdp", None, None),
            P(None, "fsdp", None, None),
            P("section", None, "fsdp", "tensor"),
            P("section", None, "tensor"),
            P("section", "tensor", "fsdp"),
            P("section", "fsdp", "tensor"),
            P("section", "tensor"),
            P("section", "tensor", "fsdp"),
            P("section", None, "fsdp"),
            P("section", None, "fsdp"),
        ),
        out_specs=(
            P("section", None, "fsdp", None, None),
            P("section", None, "fsdp", None, None),
            P("section", None, "fsdp", "tensor"),
            P("section", None, "tensor"),
            P("section", "tensor", "fsdp"),
            P("section", "fsdp", "tensor"),
            P("section", "tensor"),
            P("section", "tensor", "fsdp"),
            P("section", None, "fsdp"),
            P("section", None, "fsdp"),
        ),
        check_vma=False,
    )
```

time: 2450 us -> 952 us (0.39)
  waiting for transfers between devices: 1730 us -> 225 us
  Pallas kernels: 0 us -> 385 us
  local copies, waits for them, and re-layouts: 184 us -> 63.9 us
  other arithmetic: 196 us -> 84.8 us
  matrix products: 218 us -> 140 us
  loops' own time: 41.8 us -> 0 us
  blocking collectives: 46.4 us -> 15.8 us
    psum x12 -> x1, waiting for transfers between devices: 1420 us -> 0.02 us  [per_device(): packed = lax.psum(packed, every)]
    pallas_call x0 -> x8, Pallas kernels: none -> 385 us  [line_sum(): pl.pallas_call(functools.partial(line_sum_kernel, count, rows, lag), out_...]
    ppermute x6, waiting for transfers between devices: 193 us -> 45 us  [the longest x4 45 us: scattered(): lax.ppermute(jnp.where(is_first, pieces[1], pieces[0]), 'section', [(0, 1...]
    reduce_scatter x0 -> x8, waiting for transfers between devices: none -> 148 us  [scattered(): lax.psum_scatter(item.astype(BF16), 'fsdp', scatter_dimension=0, tiled=True)]
    unnamed x15 -> x13, waiting for transfers between devices: 80.8 us -> 1.38 us
    dot_general x57 -> x36, matrix products: 218 us -> 140 us  [the longest x8 43.2 us: dot_tn(): lax.dot_general(left, right, (((0,), (0,)), ((), ())), preferred_element_...]
    dynamic_update_slice x27 -> x0, other arithmetic: 69.8 us -> none  [per_device(): lax.scan(forward_tick, jnp.zeros_like(images[0]), ticks)[1]]
    while x394 -> x0, local copies, waits for them, and re-layouts: 54.1 us -> none
  transfers between devices with their start and end apart: 27 -> 19, of which waited for: 23 -> 10; matrix products, arithmetic and copies ran while one was open for 11% -> 15% of each run, Pallas kernels for 0% -> 10%
where the time goes in v1:
time: 952 us; the launch traced here: 941 us
  Pallas kernels  385 us (40%)
  waiting for transfers between devices  225 us (24%)
  matrix products  140 us (15%)
  other arithmetic  84.8 us (9%)
  local copies, waits for them, and re-layouts  63.9 us (7%)
  between operations  16.4 us (2%)
  blocking collectives  15.8 us (2%)
    pallas_call x8, Pallas kernels, line_sum(): pl.pallas_call(functools.partial(line_sum_kernel, count, rows, lag), out_...  385 us
    reduce_scatter x8, waiting for transfers between devices, scattered(): lax.psum_scatter(item.astype(BF16), 'fsdp', scatter_dimension=0, tiled=True)  148 us
    ppermute x4, waiting for transfers between devices, scattered(): lax.ppermute(jnp.where(is_first, pieces[1], pieces[0]), 'section', [(0, 1...  45 us
    dot_general x8, matrix products, dot_tn(): lax.dot_general(left, right, (((0,), (0,)), ((), ())), preferred_element_...  43.2 us
    unnamed x182, local copies, waits for them, and re-layouts  39.6 us
    dot_general x8, matrix products, dot_nt(): lax.dot_general(left, right, (((1,), (1,)), ((), ())), preferred_element_...  36.8 us
    all_gather x4, waiting for transfers between devices, gathered(): whole = lax.all_gather(piece, every, axis=0, tiled=True)  30.5 us
    dot_general x8, matrix products, dot_nn(): return jnp.dot(left, right, preferred_element_type=F32)  28 us
  transfers between devices with their start and end apart: 19, of which 10 were waited for; matrix products, arithmetic and copies ran while one was open for 15% of the time, Pallas kernels for 10%

profile of v1, /device:TPU:0, one launch (start us, length us, event | category | flops | bytes accessed | tf_op | source)
XLA Modules:
  0.0 940.8 jit_solution(7313544489070119081)
XLA Ops:
  22.8 9.9 %all-gather.3 = bf16[8,6,288]{2,1,0:T(8,128)(2,1)S(1)} all-gather(bf16[1,6,288]{2,1,0:T(8,128)(2,1)S(1)} %maximum_bitcast_fusion), channel_id=2, replica_groups=mesh['section'=2,'tensor'=4,'fsdp'=4] {'section','fsdp'}, dimensions={0}, use_global_device_ids=true | all-gather | bytes 31104 | tf_op jit(solution)/shard_map/all_gather | solution.py:353
  83.5 53.7 %line_sum.8 = bf16[736,1152]{1,0:T(8,128)(2,1)} custom-call(bf16[736,1152]{1,0:T(8,128)(2,1)} %convolution_convert_fusion.7.x_ref), custom_call_target="tpu_custom_call" | custom-call | bytes 120000000 | tf_op jit(solution)/shard_map/line_sum/pallas_call | solution.py:122
  140.4 6.7 convolution_add_fusion.1
  147.0 19.2 %all-gather.13.cloned.1.call-done = bf16[2304,1076]{1,0:T(8,128)(2,1)} async-done(((bf16[288,1076]{1,0:T(8,128)(2,1)}), bf16[2304,1076]{1,0:T(8,128)(2,1)}) %all-gather.13.cloned.1.call-update) | async-done | bytes 4958224 | tf_op jit(solution)/shard_map/all_gather | solution.py:346
  166.2 7.2 convolution_convert_fusion.13.x_ref
  173.4 53.7 %line_sum.9 = bf16[736,1152]{1,0:T(8,128)(2,1)} custom-call(bf16[736,1152]{1,0:T(8,128)(2,1)} %convolution_convert_fusion.13.x_ref), custom_call_target="tpu_custom_call" | custom-call | bytes 120000000 | tf_op jit(solution)/shard_map/line_sum/pallas_call | solution.py:122
  253.4 52.5 %line_sum.10 = bf16[736,1152]{1,0:T(8,128)(2,1)} custom-call(bf16[736,1152]{1,0:T(8,128)(2,1)} %convolution_convert_fusion.6.x_ref), custom_call_target="tpu_custom_call" | custom-call | bytes 120000000 | tf_op jit(solution)/shard_map/line_sum/pallas_call | solution.py:122
  322.3 52.0 %line_sum.12 = bf16[736,1152]{1,0:T(8,128)(2,1)} custom-call(bf16[736,1152]{1,0:T(8,128)(2,1)} %convolution_convert_fusion.11.x_ref), custom_call_target="tpu_custom_call" | custom-call | bytes 120000000 | tf_op jit(solution)/shard_map/line_sum/pallas_call | solution.py:122
  402.7 49.1 %line_sum.13 = bf16[736,1152]{1,0:T(8,128)(2,1)} custom-call(bf16[736,1152]{1,0:T(8,128)(2,1)} %convolution_convert_fusion.10.x_ref), custom_call_target="tpu_custom_call" | custom-call | bytes 120000000 | tf_op jit(solution)/shard_map/line_sum/pallas_call | solution.py:122
  458.8 6.7 convert_reduce_fusion.11
  470.6 44.4 %line_sum.14 = bf16[736,1152]{1,0:T(8,128)(2,1)} custom-call(bf16[736,1152]{1,0:T(8,128)(2,1)} %convolution_convert_fusion.9.x_ref), custom_call_target="tpu_custom_call" | custom-call | bytes 120000000 | tf_op jit(solution)/shard_map/line_sum/pallas_call | solution.py:122
  524.1 6.2 fusion.83
  546.3 40.1 %line_sum.15 = bf16[736,1152]{1,0:T(8,128)(2,1)} custom-call(bf16[736,1152]{1,0:T(8,128)(2,1)} %convolution_convert_fusion.8.x_ref), custom_call_target="tpu_custom_call" | custom-call | bytes 120000000 | tf_op jit(solution)/shard_map/line_sum/pallas_call | solution.py:122
  611.6 6.6 convolution_convert_fusion
  618.3 6.7 convolution_convert_fusion.1
  625.0 6.9 convolution_convert_fusion.2
  632.4 7.2 convolution_convert_fusion.12.x_ref
  639.6 39.7 %line_sum.11 = bf16[736,1152]{1,0:T(8,128)(2,1)} custom-call(bf16[736,1152]{1,0:T(8,128)(2,1)} %convolution_convert_fusion.12.x_ref), custom_call_target="tpu_custom_call" | custom-call | bytes 120000000 | tf_op jit(solution)/shard_map/line_sum/pallas_call | solution.py:122
  703.9 37.1 %collective-permute-done.3 = bf16[288,288]{1,0:T(8,128)(2,1)S(1)} collective-permute-done((bf16[288,288]{1,0:T(8,128)(2,1)S(1)}, bf16[288,288]{1,0:T(8,128)(2,1)S(1)}, u32[]{:S(2)}, u32[]{:S(2)}) %collective-permute-start.3) | collective-permute-done | bytes 165920 | tf_op jit(solution)/shard_map/ppermute | solution.py:406
  766.7 34.4 %reduce-scatter.23.cloned.1.call-done = bf16[288,1076]{1,0:T(8,128)(2,1)} async-done(((bf16[1152,1076]{1,0:T(8,128)(2,1)}), bf16[288,1076]{1,0:T(8,128)(2,1)}) %reduce-scatter.23.cloned.1.call-update) | async-done | bytes 619792 | tf_op jit(solution)/shard_map/reduce_scatter | solution.py:403
  801.2 37.3 %reduce-scatter.21.cloned.1.call-done = bf16[288,1076]{1,0:T(8,128)(2,1)} async-done(((bf16[1152,1076]{1,0:T(8,128)(2,1)}), bf16[288,1076]{1,0:T(8,128)(2,1)}) %reduce-scatter.21.cloned.1.call-update) | async-done | bytes 619792 | tf_op jit(solution)/shard_map/reduce_scatter | solution.py:403
  842.0 33.7 %reduce-scatter.19.cloned.1.call-done = bf16[288,1076]{1,0:T(8,128)(2,1)} async-done(((bf16[1152,1076]{1,0:T(8,128)(2,1)}), bf16[288,1076]{1,0:T(8,128)(2,1)}) %reduce-scatter.19.cloned.1.call-update) | async-done | bytes 619792 | tf_op jit(solution)/shard_map/reduce_scatter | solution.py:403
  875.6 37.3 %reduce-scatter.17.cloned.1.call-done = bf16[288,1076]{1,0:T(8,128)(2,1)} async-done(((bf16[1152,1076]{1,0:T(8,128)(2,1)}), bf16[288,1076]{1,0:T(8,128)(2,1)}) %reduce-scatter.17.cloned.1.call-update) | async-done | bytes 619792 | tf_op jit(solution)/shard_map/reduce_scatter | solution.py:403
  923.8 7.9 collective-permute-done.4
  (353 shorter events, 268.3 us)
Async XLA Ops:
  7.2 43.9 %all-gather.9.cloned.1.call-start = ((), (), s32[]{:S(2)}) async-start(), calls=%async_computation.8 | async-start | bytes 4644864 | tf_op jit(solution)/shard_map/all_gather | solution.py:346
  11.8 68.2 %all-gather.11.cloned.1.call-start = ((), (), s32[]{:S(2)}) async-start(), calls=%async_computation.9 | async-start | bytes 1990656 | tf_op jit(solution)/shard_map/all_gather | solution.py:346
  13.6 126.7 %all-gather.15.cloned.1.call-start = ((), (), s32[]{:S(2)}) async-start(), calls=%async_computation.20 | async-start | bytes 5971968 | tf_op jit(solution)/shard_map/all_gather | solution.py:346
  14.4 151.8 %all-gather.13.cloned.1.call-start = ((), (), s32[]{:S(2)}) async-start(), calls=%async_computation.10 | async-start | bytes 5971968 | tf_op jit(solution)/shard_map/all_gather | solution.py:346
  15.0 682.7 %all-reduce.5.cloned.1.call-start = ((), (), s32[]{:S(2)}) async-start(), calls=%async_computation.13 | async-start | bytes 137216 | tf_op jit(solution)/shard_map/psum | solution.py:413
  44.3 96.0 %copy-start.56 = (f32[1152]{0:T(1024)}, f32[1152]{0:T(1024)S(1)}, u32[]{:S(2)}) copy-start(f32[1152]{0:T(1024)S(1)} %get-tuple-element.73) | copy-start | bytes 13828
  74.8 64.6 %copy-start.45 = (bf16[4,72,736]{2,1,0:T(8,128)(2,1)}, bf16[4,72,736]{2,1,0:T(8,128)(2,1)S(1)}, u32[]{:S(2)}) copy-start(bf16[4,72,736]{2,1,0:T(8,128)(2,1)S(1)} %fusion.87) | copy-start | bytes 1271812
  592.7 106.3 %reduce-scatter.15.cloned.1.call-start = ((), (), s32[]{:S(2)}) async-start(), calls=%async_computation.15 | async-start | bytes 1105920 | tf_op jit(solution)/shard_map/reduce_scatter | solution.py:403
  596.8 102.2 %reduce-scatter.13.cloned.1.call-start = ((), (), s32[]{:S(2)}) async-start(), calls=%async_computation.14 | async-start | bytes 1105920 | tf_op jit(solution)/shard_map/reduce_scatter | solution.py:403
  601.0 157.7 %reduce-scatter.11.cloned.1.call-start = ((), (), s32[]{:S(2)}) async-start(), calls=%async_computation.12 | async-start | bytes 2580480 | tf_op jit(solution)/shard_map/reduce_scatter | solution.py:403
  606.4 157.6 %reduce-scatter.9.cloned.1.call-start = ((), (), s32[]{:S(2)}) async-start(), calls=%async_computation.11 | async-start | bytes 2580480 | tf_op jit(solution)/shard_map/reduce_scatter | solution.py:403
  611.5 189.6 %reduce-scatter.23.cloned.1.call-start = ((), (), s32[]{:S(2)}) async-start(), calls=%async_computation.19 | async-start | bytes 3317760 | tf_op jit(solution)/shard_map/reduce_scatter | solution.py:403
  618.2 220.3 %reduce-scatter.21.cloned.1.call-start = ((), (), s32[]{:S(2)}) async-start(), calls=%async_computation.18 | async-start | bytes 3317760 | tf_op jit(solution)/shard_map/reduce_scatter | solution.py:403
  624.9 250.7 %reduce-scatter.19.cloned.1.call-start = ((), (), s32[]{:S(2)}) async-start(), calls=%async_computation.17 | async-start | bytes 3317760 | tf_op jit(solution)/shard_map/reduce_scatter | solution.py:403
  631.9 281.0 %reduce-scatter.17.cloned.1.call-start = ((), (), s32[]{:S(2)}) async-start(), calls=%async_computation.16 | async-start | bytes 3317760 | tf_op jit(solution)/shard_map/reduce_scatter | solution.py:403
  685.9 57.1 %collective-permute-start = (bf16[729,1152]{1,0:T(8,128)(2,1)}, bf16[729,1152]{1,0:T(8,128)(2,1)}, u32[]{:S(2)}, u32[]{:S(2)}) collective-permute-start(bf16[729,1152]{1,0:T(8,128)(2,1)} %broadcast_select_fusion.1), channel_id=1, source_target_pairs={{0,16},{16,0},{1,17},{17,1},{2,18},{18,2},{3,19},{19,3},{4,20},{20... | collective-permute-start | bytes 5038856 | tf_op jit(solution)/shard_map/ppermute | solution.py:384
  691.6 59.1 %collective-permute-start.1 = (bf16[729,1152]{1,0:T(8,128)(2,1)}, bf16[729,1152]{1,0:T(8,128)(2,1)}, u32[]{:S(2)}, u32[]{:S(2)}) collective-permute-start(bf16[729,1152]{1,0:T(8,128)(2,1)} %broadcast_select_fusion), channel_id=1, source_target_pairs={{0,16},{16,0},{1,17},{17,1},{2,18},{18,2},{3,19},{19,3},{4,20},{20... | collective-permute-start | bytes 5038856 | tf_op jit(solution)/shard_map/ppermute | solution.py:384
  697.6 45.4 %copy-start.25 = (bf16[1,1,1,729,1152]{4,3,2,1,0:T(8,128)(2,1)S(1)}, bf16[1,1,1,729,1152]{4,3,2,1,0:T(8,128)(2,1)}, u32[]{:S(2)}) copy-start(bf16[1,1,1,729,1152]{4,3,2,1,0:T(8,128)(2,1)} %get-tuple-element.92) | copy-start | bytes 5038852
  699.9 41.0 %collective-permute-start.3 = (bf16[288,288]{1,0:T(8,128)(2,1)S(1)}, bf16[288,288]{1,0:T(8,128)(2,1)S(1)}, u32[]{:S(2)}, u32[]{:S(2)}) collective-permute-start(bf16[288,288]{1,0:T(8,128)(2,1)S(1)} %broadcast_select_fusion.5), channel_id=1, source_target_pairs={{0,16},{16,0},{1,17},{17,1},{2,18},{18,2},{3,19},{19,3},{4,20},{20... | collective-permute-start | bytes 497672 | tf_op jit(solution)/shard_map/ppermute | solution.py:406
  758.7 157.7 %copy-start.34 = (bf16[288,864]{1,0:T(8,128)(2,1)S(1)}, bf16[288,864]{1,0:T(8,128)(2,1)}, u32[]{:S(2)}) copy-start(bf16[288,864]{1,0:T(8,128)(2,1)} %reduce-scatter.11.cloned.1.call-done) | copy-start | bytes 1492996
  764.0 152.4 %copy-start.35 = (bf16[288,864]{1,0:T(8,128)(2,1)S(1)}, bf16[288,864]{1,0:T(8,128)(2,1)}, u32[]{:S(2)}) copy-start(bf16[288,864]{1,0:T(8,128)(2,1)} %reduce-scatter.9.cloned.1.call-done) | copy-start | bytes 1492996
  765.2 151.2 %collective-permute-start.2 = (bf16[288,864]{1,0:T(8,128)(2,1)S(1)}, bf16[288,864]{1,0:T(8,128)(2,1)S(1)}, u32[]{:S(2)}, u32[]{:S(2)}) collective-permute-start(bf16[288,864]{1,0:T(8,128)(2,1)S(1)} %broadcast_select_fusion.4), channel_id=1, source_target_pairs={{0,16},{16,0},{1,17},{17,1},{2,18},{18,2},{3,19},{19,3},{4,20},{20... | collective-permute-start | bytes 1493000 | tf_op jit(solution)/shard_map/ppermute | solution.py:406
  840.5 80.7 %collective-permute-start.5 = (bf16[288,1076]{1,0:T(8,128)(2,1)}, bf16[288,1076]{1,0:T(8,128)(2,1)}, u32[]{:S(2)}, u32[]{:S(2)}) collective-permute-start(bf16[288,1076]{1,0:T(8,128)(2,1)} %broadcast_select_fusion.2), channel_id=1, source_target_pairs={{0,16},{16,0},{1,17},{17,1},{2,18},{18,2},{3,19},{19,3},{4,20},{20... | collective-permute-start | bytes 1859336 | tf_op jit(solution)/shard_map/ppermute | solution.py:406
  915.0 16.8 %collective-permute-start.4 = (bf16[288,1076]{1,0:T(8,128)(2,1)}, bf16[288,1076]{1,0:T(8,128)(2,1)}, u32[]{:S(2)}, u32[]{:S(2)}) collective-permute-start(bf16[288,1076]{1,0:T(8,128)(2,1)} %broadcast_select_fusion.3), channel_id=1, source_target_pairs={{0,16},{16,0},{1,17},{17,1},{2,18},{18,2},{3,19},{19,3},{4,20},{20... | collective-permute-start | bytes 1859336 | tf_op jit(solution)/shard_map/ppermute | solution.py:406
  (79 other events, 603.4 us)
Sparse Core Ops, SparseCore 0:
  11.9 39.1 all-gather.8
  53.6 26.3 all-gather.10
  81.9 41.2 all-gather.14
  124.9 41.2 all-gather.12
  592.8 49.0 all-reduce.4
  644.9 24.9 reduce-scatter.14
  673.0 23.7 reduce-scatter.12
  699.4 30.9 reduce-scatter.10
  733.0 30.9 reduce-scatter.8
  766.4 34.7 reduce-scatter.22
  803.7 34.7 reduce-scatter.20
  840.9 34.7 reduce-scatter.18
  878.2 34.7 reduce-scatter.16

commit v2 on v1

--- a/solution.py
+++ b/solution.py
@@ -6,6 +6,7 @@
 from jax.experimental import pallas as pl
 from jax.experimental.pallas import tpu as pltpu
 from jax.sharding import PartitionSpec as P
+from jax.experimental.layout import Layout, with_layout_constraint
 
 HD = 72
 
@@ -21,117 +22,312 @@
 TILE = 16
 
 
-def greet(me, count):
+def greet(me, count, others=()):
     barrier = pltpu.get_barrier_semaphore()
     for there, other in ((me > 0, me - 1), (me < count - 1, me + 1)):
         @pl.when(there)
         def _():
             pl.semaphore_signal(barrier, inc=1, device_id={"tensor": other}, device_id_type=MESH)
+    for other in others:
+        pl.semaphore_signal(barrier, inc=1, device_id=other, device_id_type=MESH)
     peers = (me > 0).astype(jnp.int32) + (me < count - 1).astype(jnp.int32)
-    pl.semaphore_wait(barrier, peers)
-
-def line_sum_kernel(count, rows, lag, x_ref, o_ref, come, gone, red_send, red_recv, out_send, out_recv):
-    me = lax.axis_index("tensor")
-    greet(me, count)
-    pieces = x_ref.shape[0] // rows
-
-    def span(piece):
-        return pl.ds(pl.multiple_of(piece * rows, rows), rows)
-
-    def send(piece, source, target, step, out):
-        sems = (out_send, out_recv) if out else (red_send, red_recv)
+    pl.semaphore_wait(barrier, peers + len(others))
+
+
+class Line:
+    def __init__(self, count, rows, lag, x_ref, o_ref, come, gone, sems):
+        self.count, self.rows, self.lag = count, rows, lag
+        self.x, self.o, self.come, self.gone = x_ref, o_ref, come, gone
+        self.red, self.out = sems[:2], sems[2:]
+        self.me = lax.axis_index("tensor")
+        self.pieces = x_ref.shape[0] // rows
+        self.pairs = (self.pieces + 1) // 2
+        self.turns = self.pairs + 2 * lag * (count - 1)
+
+    def span(self, piece):
+        return pl.ds(pl.multiple_of(piece * self.rows, self.rows), self.rows)
+
+    def send(self, piece, source, target, step, sems):
         return pltpu.make_async_remote_copy(
-            src_ref=source.at[span(piece)],
-            dst_ref=target.at[span(piece)],
+            src_ref=source.at[self.span(piece)],
+            dst_ref=target.at[self.span(piece)],
             send_sem=sems[0].at[piece],
             recv_sem=sems[1].at[piece],
-            device_id={"tensor": me + step},
+            device_id={"tensor": self.me + step},
             device_id_type=MESH,
         )
 
-    def place(step):
-        return me if step > 0 else count - 1 - me
-
-    def reduce_step(index, step):
+    def place(self, step):
+        return self.me if step > 0 else self.count - 1 - self.me
+
+    def reduce_step(self, index, step):
         piece = 2 * index + (step < 0)
-        ok = (index >= 0) & (piece < pieces)
-        pos = place(step)
+        ok = (index >= 0) & (piece < self.pieces)
+        pos = self.place(step)
+        end = self.count - 1
+        span = self.span(piece)
 
         @pl.when(ok & (pos == 0))
         def _():
-            send(piece, x_ref, come, step, False).start()
+            self.send(piece, self.x, self.come, step, self.red).start()
 
         def add():
-            send(piece, come, come, step, False).wait_recv()
-            return (x_ref[span(piece), :].astype(F32) + come[span(piece), :].astype(F32)).astype(BF16)
-
-        @pl.when(ok & (pos > 0) & (pos < count - 1))
+            self.send(piece, self.come, self.come, step, self.red).wait_recv()
+            return (self.x[span, :].astype(F32) + self.come[span, :].astype(F32)).astype(BF16)
+
+        @pl.when(ok & (pos > 0) & (pos < end))
         def _():
-            gone[span(piece), :] = add()
-            send(piece, gone, come, step, False).start()
-
-        @pl.when(ok & (pos == count - 1))
+            self.gone[span, :] = add()
+            self.send(piece, self.gone, self.come, step, self.red).start()
+
+        @pl.when(ok & (pos == end))
         def _():
-            o_ref[span(piece), :] = add()
-            send(piece, o_ref, o_ref, -step, True).start()
-
-    def out_step(index, step):
+            self.o[span, :] = add()
+            self.send(piece, self.o, self.o, -step, self.out).start()
+
+    def out_step(self, index, step):
         piece = 2 * index + (step < 0)
-        ok = (index >= 0) & (piece < pieces)
-        pos = place(step)
-
-        @pl.when(ok & (pos < count - 1))
+        ok = (index >= 0) & (piece < self.pieces)
+        pos = self.place(step)
+
+        @pl.when(ok & (pos < self.count - 1))
         def _():
-            send(piece, o_ref, o_ref, -step, True).wait_recv()
-
-        @pl.when(ok & (pos > 0) & (pos < count - 1))
+            self.send(piece, self.o, self.o, -step, self.out).wait_recv()
+
+        @pl.when(ok & (pos > 0) & (pos < self.count - 1))
         def _():
-            send(piece, o_ref, o_ref, -step, True).start()
-
-    pairs = (pieces + 1) // 2
-
-    def turn(s, _):
+            self.send(piece, self.o, self.o, -step, self.out).start()
+
+    def turn(self, s):
         for step in (1, -1):
-            reduce_step(s - lag * place(step), step)
+            self.reduce_step(s - self.lag * self.place(step), step)
+        back = self.lag * (self.count - 1)
         for step in (1, -1):
-            out_step(s - lag * (count - 1) - lag * (count - 1 - place(step)), step)
-        return 0
-
-    lax.fori_loop(0, pairs + 2 * lag * (count - 1), turn, 0)
-
-    def end_steps(i, _):
-        for step in (1, -1):
-            piece = 2 * i + (step < 0)
-            pos = place(step)
-
-            @pl.when((piece < pieces) & (pos < count - 1))
+            self.out_step(s - back - self.lag * (self.count - 1 - self.place(step)), step)
+
+    def finish(self):
+        def end_steps(i, _):
+            for step in (1, -1):
+                piece = 2 * i + (step < 0)
+                pos = self.place(step)
+
+                @pl.when((piece < self.pieces) & (pos < self.count - 1))
+                def _():
+                    self.send(piece, self.x, self.come, step, self.red).wait_send()
+
+                @pl.when((piece < self.pieces) & (pos > 0))
+                def _():
+                    self.send(piece, self.o, self.o, -step, self.out).wait_send()
+            return 0
+
+        lax.fori_loop(0, self.pairs, end_steps, 0)
+
+    @staticmethod
+    def scratch(x, rows):
+        return [pltpu.VMEM(x.shape, BF16)] * 2 + [pltpu.SemaphoreType.DMA((x.shape[0] // rows,))] * 4
+
+
+class Share:
+    def __init__(self, ways, layer, cuts, g_ref, o_ref, bufs):
+        self.ways, self.layer, self.cuts = ways, layer, cuts
+        self.levels = ways.bit_length() - 1
+        self.g, self.o = g_ref, o_ref
+        n = self.levels
+        self.recv, self.stage = bufs[:n], [None] + list(bufs[n : 2 * n - 1])
+        bufs = bufs[2 * n - 1 :]
+        self.last_recv, self.last_stage = bufs[:2]
+        sems = bufs[2:]
+        self.sems = [(sems[2 * j], sems[2 * j + 1]) for j in range(n + 1)]
+        self.me = lax.axis_index("fsdp")
+        self.owner = lax.axis_index("section") == layer
+        self.height = o_ref.shape[0]
+        self.rows = self.height // cuts
+
+    def others(self):
+        return [{"fsdp": self.flip(j)} for j in range(self.levels)] + [
+            {"section": 1 - lax.axis_index("section")}
+        ]
+
+    def flip(self, level):
+        bit = self.me // (1 << level) % 2
+        return self.me + (1 - 2 * bit) * (1 << level)
+
+    def blocks(self, level):
+        low = self.flip(level) % (1 << (level + 1))
+        return [low + (high << (level + 1)) for high in range(self.ways >> (level + 1))]
+
+    def span(self, piece):
+        return pl.ds(pl.multiple_of(piece * self.rows, self.rows), self.rows)
+
+    def own(self, block, piece):
+        if len(self.g.shape) == 3:
+            return self.g.at[block, self.span(piece)]
+        return self.g.at[pl.ds(pl.multiple_of(block * self.height + piece * self.rows, self.rows), self.rows)]
+
+    def copy(self, level, block, piece):
+        place = block // (1 << (level + 1))
+        return pltpu.make_async_remote_copy(
+            src_ref=self.own(block, piece) if level == 0 else self.stage[level].at[place, self.span(piece)],
+            dst_ref=self.recv[level].at[place, self.span(piece)],
+            send_sem=self.sems[level][0].at[place * self.cuts + piece],
+            recv_sem=self.sems[level][1].at[place * self.cuts + piece],
+            device_id={"fsdp": self.flip(level)},
+            device_id_type=MESH,
+        )
+
+    def last_copy(self, piece):
+        return pltpu.make_async_remote_copy(
+            src_ref=self.last_stage.at[self.span(piece)],
+            dst_ref=self.last_recv.at[self.span(piece)],
+            send_sem=self.sems[-1][0].at[piece],
+            recv_sem=self.sems[-1][1].at[piece],
+            device_id={"section": 1 - lax.axis_index("section")},
+            device_id_type=MESH,
+        )
+
+    def start(self):
+        for piece in range(self.cuts):
+            for block in self.blocks(0):
+                self.copy(0, block, piece).start()
+
+    def total(self, level, block, piece):
+        value = self.own(block, piece)[...].astype(F32)
+        for j in range(level):
+            self.copy(j, block, piece).wait_recv()
+            value += self.recv[j][block // (1 << (j + 1)), self.span(piece), :].astype(F32)
+        return value
+
+    def step(self, level, piece):
+        if level < self.levels:
+            for block in self.blocks(level):
+                self.stage[level][block // (1 << (level + 1)), self.span(piece), :] = self.total(
+                    level, block, piece
+                ).astype(BF16)
+                self.copy(level, block, piece).start()
+        elif level == self.levels:
+            value = self.total(level, self.me, piece)
+            self.o[self.span(piece), :] = value
+
+            @pl.when(jnp.logical_not(self.owner))
             def _():
-                send(piece, x_ref, come, step, False).wait_send()
-
-            @pl.when((piece < pieces) & (pos > 0))
+                self.last_stage[self.span(piece), :] = value.astype(BF16)
+                self.last_copy(piece).start()
+        else:
+
+            @pl.when(self.owner)
             def _():
-                send(piece, o_ref, o_ref, -step, True).wait_send()
-        return 0
-
-    lax.fori_loop(0, pairs, end_steps, 0)
+                self.last_copy(piece).wait_recv()
+                self.o[self.span(piece), :] += self.last_recv[self.span(piece), :].astype(F32)
+
+    def finish(self):
+        for piece in range(self.cuts):
+            for level in range(self.levels):
+                for block in self.blocks(level):
+                    self.copy(level, block, piece).wait_send()
+
+            @pl.when(jnp.logical_not(self.owner))
+            def _():
+                self.last_copy(piece).wait_send()
+
+    @staticmethod
+    def scratch(shape, ways, cuts):
+        levels = ways.bit_length() - 1
+        rows, width = shape
+        counts = [ways >> (j + 1) for j in range(levels)]
+        sems = []
+        for count in counts + [1]:
+            sems += [pltpu.SemaphoreType.DMA((count * cuts,))] * 2
+        return (
+            [pltpu.VMEM((count, rows, width), BF16) for count in counts + counts[1:]]
+            + [pltpu.VMEM((rows, width), BF16)] * 2
+            + sems
+        )
+
+
+def line_sum_kernel(count, rows, lag, x_ref, o_ref, come, gone, *sems):
+    line = Line(count, rows, lag, x_ref, o_ref, come, gone, sems)
+    greet(line.me, count)
+    lax.fori_loop(0, line.turns, lambda s, _: (line.turn(s), 0)[1], 0)
+    line.finish()
 
 
 def line_sum(x, cid, rows=16, lag=4):
     count = lax.axis_size("tensor")
-    pieces = x.shape[0] // rows
     return pl.pallas_call(
         functools.partial(line_sum_kernel, count, rows, lag),
         out_shape=jax.ShapeDtypeStruct(x.shape, BF16),
         in_specs=[pl.BlockSpec(memory_space=pltpu.VMEM)],
         out_specs=pl.BlockSpec(memory_space=pltpu.VMEM),
-        scratch_shapes=[
-            pltpu.VMEM(x.shape, BF16),
-            pltpu.VMEM(x.shape, BF16),
-        ] + [pltpu.SemaphoreType.DMA((pieces,))] * 4,
+        scratch_shapes=Line.scratch(x, rows),
         compiler_params=pltpu.CompilerParams(collective_id=cid, has_side_effects=True),
         name="line_sum",
         cost_estimate=pl.CostEstimate(flops=0, bytes_accessed=120_000_000, transcendentals=0),
     )(x)
+
+
+def line_share_kernel(count, rows, lag, ways, layer, cuts, k, *refs):
+    x_ref, g_refs = refs[0], refs[1 : 1 + k]
+    o_ref, go_refs = refs[1 + k], refs[2 + k : 2 + 2 * k]
+    scratch = refs[2 + 2 * k :]
+    line = Line(count, rows, lag, x_ref, o_ref, *scratch[:2], scratch[2:6])
+    scratch = scratch[6:]
+    each = len(scratch) // k
+    shares = [
+        Share(ways, layer, cuts, g_refs[i], go_refs[i], scratch[i * each : (i + 1) * each]) for i in range(k)
+    ]
+    levels = shares[0].levels
+    greet(line.me, count, shares[0].others())
+    for share in shares:
+        share.start()
+    steps = []
+    for level in range(1, levels + 2):
+        first, stride = (4, 1) if level == 1 else (3 + 6 * (level - 1), 5)
+        steps += [(first + i * cuts * stride, stride, level, share) for i, share in enumerate(shares)]
+    turns = max(line.turns, max(first + stride * (cuts - 1) + 1 for first, stride, _, _ in steps))
+
+    def turn(s, _):
+        line.turn(s)
+        for first, stride, level, share in steps:
+            past = s - first
+            piece = past // stride
+
+            @pl.when((past >= 0) & (past % stride == 0) & (piece < cuts))
+            def _():
+                share.step(level, piece)
+        return 0
+
+    lax.fori_loop(0, turns, turn, 0)
+    line.finish()
+    for share in shares:
+        share.finish()
+
+
+def line_share(x, grads, layer, cid, rows=16, lag=4):
+    count, ways = lax.axis_size("tensor"), lax.axis_size("fsdp")
+    height = grads[0].shape[0] // ways
+    shapes = [(height, g.shape[1]) for g in grads]
+    cuts = 3 if height % (3 * TILE) == 0 else 1
+    if height % TILE:
+        grads = [g.reshape(ways, height, g.shape[1]) for g in grads]
+    scratch = Line.scratch(x, rows)
+    for shape in shapes:
+        scratch += Share.scratch(shape, ways, cuts)
+    vmem = pl.BlockSpec(memory_space=pltpu.VMEM)
+    return pl.pallas_call(
+        functools.partial(
+            line_share_kernel, count, rows, lag, ways, layer, cuts, len(grads)
+        ),
+        out_shape=[jax.ShapeDtypeStruct(x.shape, BF16)]
+        + [jax.ShapeDtypeStruct(shape, F32) for shape in shapes],
+        in_specs=[vmem] * (1 + len(grads)),
+        out_specs=[vmem] * (1 + len(grads)),
+        scratch_shapes=scratch,
+        compiler_params=pltpu.CompilerParams(
+            collective_id=cid, has_side_effects=True, vmem_limit_bytes=56 * 1024 * 1024
+        ),
+        name="line_share",
+        cost_estimate=pl.CostEstimate(flops=0, bytes_accessed=120_000_000, transcendentals=0),
+    )(x, *grads)
 
 
 def tensor_sum(value):
@@ -176,10 +372,10 @@
 
 
 def dot_tn(left, right):
-    return lax.dot_general(left, right, (((0,), (0,)), ((), ())), preferred_element_type=F32)
-
-
-def layer_forward(inputs, weights, qv_bias, up_bias, gains, shifts, cuts, real):
+    return with_layout_constraint(lax.dot_general(left, right, (((0,), (0,)), ((), ())), preferred_element_type=F32), Layout((0,1)))
+
+
+def layer_forward(inputs, weights, qv_bias, up_bias, gains, shifts, cuts, real, is_last):
     qkv, out_t, up, down_t = weights
     width = qkv.shape[1] // 3
     heads = width // HD
@@ -217,8 +413,13 @@
         normed_two.append(normed)
         pre_act.append(dot_nn(normed, up) + up_bias)
         active.append(gelu_value(pre_act[-1]).astype(BF16))
-        mlp_term = tensor_sum(dot_nt(active[-1], down_t))
-        outputs.append((rows + mlp_term + shifts[3]).astype(BF16))
+        mlp_term = dot_nt(active[-1], down_t).astype(BF16)
+        if is_last:
+            outputs.append(lambda total, rows=rows: (rows + total.astype(F32) + shifts[3]).astype(BF16))
+            stored_term = mlp_term
+            continue
+        outputs.append((rows + line_sum(mlp_term, 0).astype(F32) + shifts[3]).astype(BF16))
+        stored_term = None
     stored = (
         inputs,
         normed_one,
@@ -232,10 +433,10 @@
         pre_act,
         active,
     )
-    return outputs, stored
-
-
-def layer_backward(grads, stored, weights, gains, shifts, cuts, real):
+    return outputs, stored, stored_term
+
+
+def layer_backward(grads, stored, weights, gains, shifts, cuts, real, layer, extra):
     qkv, out_t, up, down_t = weights
     (
         inputs,
@@ -258,11 +459,18 @@
     for part, pre in zip(grad_mix, pre_act):
         grad_active = dot_nn(part, down_t)
         grad_pre.append((grad_active * gelu_slope(pre)).astype(BF16))
-        two_terms.append(tensor_sum(dot_nt(grad_pre[-1], up)))
+        two_terms.append(dot_nt(grad_pre[-1], up).astype(BF16))
     mix_all = jnp.concatenate(grad_mix)
     pre_all = jnp.concatenate(grad_pre)
     grad_down = dot_tn(mix_all, jnp.concatenate(active))
     grad_up = dot_tn(jnp.concatenate(normed_two), pre_all)
+    count = two_terms[0].shape[0]
+    two = two_terms[0] if extra is None else jnp.concatenate([two_terms[0], extra])
+    two, grad_down, grad_up = line_share(
+        two, [grad_down.astype(BF16), grad_up.astype(BF16)], layer, 1 + 2 * layer
+    )
+    two_terms = [two[:count].astype(F32)]
+    extra = two[count:]
     up_bias_grad = jnp.sum(pre_all.astype(F32), axis=0)
     mix_shift = jnp.sum(mix_all.astype(F32), axis=0)
     grad_hidden, grad_attn, gain_two, shift_two, attn_shift = [], [], 0.0, 0.0, 0.0
@@ -307,16 +515,20 @@
     bias_sums = jnp.sum(grad_proj.astype(F32), axis=0)
     grad_inputs = []
     gain_one, shift_one = 0.0, 0.0
-    one_terms = [tensor_sum(dot_nt(grad_proj[first:last], qkv)) for first, last in cuts]
+    one, grad_qkv, grad_out = line_share(
+        dot_nt(grad_proj, qkv).astype(BF16), [grad_qkv.astype(BF16), grad_out.astype(BF16)], layer, 2 + 2 * layer
+    )
+    one_terms = [one.astype(F32)]
     for one, part, rows in zip(one_terms, inputs, grad_hidden):
         normed, inverse = norm_forward(part.astype(F32), gains[0], shifts[0])[1:]
         moved, gain_part, shift_part = norm_backward(one, normed, inverse, gains[0])
         gain_one += gain_part
         shift_one += shift_part
         grad_inputs.append((rows + moved).astype(BF16))
-    gain_grads = [gain_one, gain_two, shift_one, attn_shift, shift_two, mix_shift]
+    gain_grads = [gain_two, attn_shift, shift_two, mix_shift]
     bias_grads = jnp.concatenate([bias_sums[:width], bias_sums[2 * width :], up_bias_grad])
-    return grad_inputs, (grad_qkv, grad_out, grad_up, grad_down), (jnp.concatenate(gain_grads), bias_grads)
+    late = jnp.concatenate([gain_one, shift_one])
+    return grad_inputs, extra, (grad_qkv, grad_out, grad_up, grad_down), (jnp.concatenate(gain_grads + [bias_grads]), late)
 
 
 def per_device(
@@ -346,8 +558,19 @@
         whole = lax.all_gather(piece, every, axis=0, tiled=True)
         return whole.reshape(2, -1, piece.shape[1])
 
-    qkv = gathered(qkv_weight[0].transpose(1, 0, 2).reshape(rows_here, 3 * width))
-    out_t = gathered(out_weight[0].T)
+    gap = -3 * width % 128
+    mixer = gathered(
+        jnp.concatenate(
+            [
+                qkv_weight[0].transpose(1, 0, 2).reshape(rows_here, 3 * width),
+                jnp.zeros((rows_here, gap), BF16),
+                out_weight[0].T,
+            ],
+            axis=1,
+        )
+    )
+    qkv = mixer[:, :, : 3 * width]
+    out_t = mixer[:, :, 3 * width + gap :]
     up = gathered(up_weight[0])
     down_t = gathered(down_weight[0].T)
     scales = lax.all_gather(
@@ -372,10 +595,10 @@
     outputs, stored = [], []
     for index in range(2):
         qv = biases[index, : 2 * width].reshape(2, width)
-        rows, kept = layer_forward(
-            rows, layer_args(index), qv, biases[index, 2 * width :], scales[index, :2], scales[index, 2:], cuts, seq_len
-        )
-        outputs.append(jnp.concatenate(rows))
+        rows, kept, last_term = layer_forward(
+            rows, layer_args(index), qv, biases[index, 2 * width :], scales[index, :2], scales[index, 2:], cuts, seq_len, index == 1
+        )
+        outputs.append(rows[0])
         stored.append(kept)
 
     def swapped(pair):
@@ -386,35 +609,38 @@
             is_first, jnp.stack([mine, other]), jnp.stack([other, mine])
         )[None, :, None]
 
-    section_outputs = swapped(outputs)
     grads = [own_grad[first:last] for first, last in cuts]
     input_grads = [None, None]
     weight_grads = [None, None]
     small = [None, None]
     for index in (1, 0):
-        grads, weight_grads[index], small[index] = layer_backward(
-            grads, stored[index], layer_args(index), scales[index, :2], scales[index, 2:], cuts, seq_len
-        )
+        grads, total, weight_grads[index], small[index] = layer_backward(
+            grads,
+            stored[index],
+            layer_args(index),
+            scales[index, :2],
+            scales[index, 2:],
+            cuts,
+            seq_len,
+            index,
+            last_term if index == 1 else None,
+        )
+        if index == 1:
+            section_outputs = swapped([outputs[0], outputs[1](total)])
         input_grads[index] = jnp.concatenate(grads)
     input_grads = swapped(input_grads)
 
-    def scattered(pair):
-        pieces = [
-            lax.psum_scatter(item.astype(BF16), "fsdp", scatter_dimension=0, tiled=True) for item in pair
-        ]
-        mine = jnp.where(is_first, pieces[0], pieces[1])
-        other = lax.ppermute(jnp.where(is_first, pieces[1], pieces[0]), "section", [(0, 1), (1, 0)])
-        return mine.astype(F32) + other.astype(F32)
-
     grad_qkv, grad_out, grad_up, grad_down = [
-        scattered([weight_grads[0][place], weight_grads[1][place]]) for place in range(4)
+        jnp.where(is_first, first, second) for first, second in zip(*weight_grads)
     ]
-    packed = jnp.stack([jnp.concatenate(small[0]), jnp.concatenate(small[1])])
-    packed = lax.psum(packed, every)
+    packed = lax.psum(jnp.stack([small[0][0], small[1][0]]), every)
+    late = lax.psum(jnp.stack([small[0][1], small[1][1]]), every)
     packed = jnp.where(is_first, packed[0], packed[1])
-    norm_part = packed[: 6 * model_width].reshape(6, model_width)
+    late = jnp.where(is_first, late[0], late[1]).reshape(2, model_width)
+    norm_part = packed[: 4 * model_width].reshape(4, model_width)
+    norm_part = jnp.stack([late[0], norm_part[0], late[1], norm_part[1], norm_part[2], norm_part[3]])
     norm_part = lax.dynamic_slice_in_dim(norm_part, fsdp * rows_here, rows_here, 1)
-    bias_part = packed[6 * model_width :]
+    bias_part = packed[4 * model_width :]
     return (
         section_outputs,
         input_grads,

time: 952 us -> 803 us (0.84)
  waiting for transfers between devices: 225 us -> 59.9 us
  Pallas kernels: 385 us -> 445 us
  matrix products: 140 us -> 125 us
    pallas_call x0 -> x4, Pallas kernels: none -> 287 us  [line_share(): pl.pallas_call(functools.partial(line_share_kernel, count, rows, lag, way...]
    pallas_call x8 -> x3, Pallas kernels: 385 us -> 158 us  [line_sum(): pl.pallas_call(functools.partial(line_sum_kernel, count, rows, lag), out_...]
    reduce_scatter x8 -> x0, waiting for transfers between devices: 148 us -> none  [scattered(): lax.psum_scatter(item.astype(BF16), 'fsdp', scatter_dimension=0, tiled=True)]
    ppermute x4 -> x0, waiting for transfers between devices: 45 us -> none  [scattered(): lax.ppermute(jnp.where(is_first, pieces[1], pieces[0]), 'section', [(0, 1...]
    psum x1, waiting for transfers between devices: 0.02 us -> 44.6 us  [per_device(): packed = lax.psum(jnp.stack([small[0][0], small[1][0]]), every)]
    all_gather x4 -> x3, waiting for transfers between devices: 30.5 us -> 13.8 us  [gathered(): whole = lax.all_gather(piece, every, axis=0, tiled=True)]
    dot_general x8, matrix products: 43.2 us -> 29.6 us  [dot_tn(): lax.dot_general(left, right, (((0,), (0,)), ((), ())), preferred_element_...]
    unnamed x182 -> x171, local copies, waits for them, and re-layouts: 39.6 us -> 28.7 us
  transfers between devices with their start and end apart: 19 -> 6, of which waited for: 10 -> 2; matrix products, arithmetic and copies ran while one was open for 15% -> 10% of each run, Pallas kernels for 10% -> 16%
where the time goes in v2:
time: 803 us; the launch traced here: 799 us
  Pallas kernels  445 us (55%)
  matrix products  125 us (16%)
  other arithmetic  79 us (10%)
  waiting for transfers between devices  59.9 us (7%)
  local copies, waits for them, and re-layouts  57.5 us (7%)
  blocking collectives  16.1 us (2%)
  between operations  16.1 us (2%)
    pallas_call x4, Pallas kernels, line_share(): pl.pallas_call(functools.partial(line_share_kernel, count, rows, lag, way...  287 us
    pallas_call x3, Pallas kernels, line_sum(): pl.pallas_call(functools.partial(line_sum_kernel, count, rows, lag), out_...  158 us
    psum x1, waiting for transfers between devices, per_device(): packed = lax.psum(jnp.stack([small[0][0], small[1][0]]), every)  44.6 us
    dot_general x8, matrix products, dot_nt(): lax.dot_general(left, right, (((1,), (1,)), ((), ())), preferred_element_...  34.3 us
    dot_general x8, matrix products, dot_nn(): return jnp.dot(left, right, preferred_element_type=F32)  31.6 us
    dot_general x8, matrix products, dot_tn(): lax.dot_general(left, right, (((0,), (0,)), ((), ())), preferred_element_...  29.6 us
    unnamed x171, local copies, waits for them, and re-layouts  28.7 us
  transfers between devices with their start and end apart: 6, of which 2 were waited for; matrix products, arithmetic and copies ran while one was open for 10% of the time, Pallas kernels for 16%

profile of v2, /device:TPU:0, one launch (start us, length us, event | category | flops | bytes accessed | tf_op | source)
XLA Modules:
  0.0 798.9 jit_solution(16385510172198846416)
XLA Ops:
  15.9 10.7 %all-gather.3 = bf16[8,6,288]{2,1,0:T(8,128)(2,1)S(1)} all-gather(bf16[1,6,288]{2,1,0:T(8,128)(2,1)S(1)} %maximum_bitcast_fusion), channel_id=2, replica_groups=mesh['section'=2,'tensor'=4,'fsdp'=4] {'section','fsdp'}, dimensions={0}, use_global_device_ids=true | all-gather | bytes 31104 | tf_op jit(solution)/shard_map/all_gather | solution.py:576
  28.4 5.4 all-reduce.2
  47.3 13.8 %all-gather.8.cloned.1.call-done = bf16[2304,1184]{1,0:T(8,128)(2,1)} async-done(((bf16[288,1184]{1,0:T(8,128)(2,1)}), bf16[2304,1184]{1,0:T(8,128)(2,1)}) %all-gather.8.cloned.1.call-update) | async-done | bytes 5455888 | tf_op jit(solution)/shard_map/all_gather | solution.py:558
  86.3 54.0 %line_sum.3 = bf16[736,1152]{1,0:T(8,128)(2,1)} custom-call(bf16[736,1152]{1,0:T(8,128)(2,1)} %convolution_convert_fusion.7.x_ref), custom_call_target="tpu_custom_call" | custom-call | bytes 120000000 | tf_op jit(solution)/shard_map/line_sum/pallas_call | solution.py:256
  143.4 6.2 convolution_add_fusion.1
  149.7 7.2 convolution_convert_fusion.13.x_ref
  156.8 52.2 %line_sum.4 = bf16[736,1152]{1,0:T(8,128)(2,1)} custom-call(bf16[736,1152]{1,0:T(8,128)(2,1)} %convolution_convert_fusion.13.x_ref), custom_call_target="tpu_custom_call" | custom-call | bytes 120000000 | tf_op jit(solution)/shard_map/line_sum/pallas_call | solution.py:256
  241.5 51.8 %line_sum.5 = bf16[736,1152]{1,0:T(8,128)(2,1)} custom-call(bf16[736,1152]{1,0:T(8,128)(2,1)} %convolution_convert_fusion.6.x_ref), custom_call_target="tpu_custom_call" | custom-call | bytes 120000000 | tf_op jit(solution)/shard_map/line_sum/pallas_call | solution.py:256
  303.4 4.3 convert_reduce_fusion.10
  307.8 4.8 convolution_convert_fusion.2.refs_2_
  320.6 96.3 %line_share.4 = (bf16[1472,1152]{1,0:T(8,128)(2,1)}, f32[288,1076]{1,0:T(8,128)}, f32[288,1076]{1,0:T(8,128)}) custom-call(bf16[1472,1152]{1,0:T(8,128)(2,1)} %pad_maximum_fusion.refs_0_, bf16[1152,1076]{1,0:T(8,128)(2,1)} %convolution_convert_fusion.3.refs_1_, bf16[1152,1076]{1,0:T(8,128)(2,1)} %convolution_convert_fusion.2.refs_2_), custom_call_target="tpu_custom_call" | custom-call | bytes 120000000 | tf_op jit(solution)/shard_map/line_share/pallas_call | solution.py:316
  429.0 5.6 multiply_reduce_fusion.1
  434.6 5.3 multiply_convert_fusion.1
  442.3 5.2 convolution_convert_fusion.10.refs_0_
  453.3 55.5 %line_share.5 = (bf16[736,1152]{1,0:T(8,128)(2,1)}, f32[288,864]{1,0:T(8,128)}, f32[288,288]{1,0:T(8,128)}) custom-call(bf16[736,1152]{1,0:T(8,128)(2,1)} %convolution_convert_fusion.10.refs_0_, bf16[1152,864]{1,0:T(8,128)(2,1)} %convolution_convert_fusion.5.refs_1_, bf16[1152,288]{1,0:T(8,128)(2,1)} %convolution_convert_fusion.15.refs_2_), custom_call_target="tpu_custom_call" | custom-call | bytes 120000000 | tf_op jit(solution)/shard_map/line_share/pallas_call | solution.py:316
  519.1 5.4 convert_reduce_fusion.11
  524.6 4.7 convolution_convert_fusion.refs_2_
  533.3 58.3 %line_share.6 = (bf16[736,1152]{1,0:T(8,128)(2,1)}, f32[288,1076]{1,0:T(8,128)}, f32[288,1076]{1,0:T(8,128)}) custom-call(bf16[736,1152]{1,0:T(8,128)(2,1)} %convolution_convert_fusion.9.refs_0_, bf16[1152,1076]{1,0:T(8,128)(2,1)} %convolution_convert_fusion.1.refs_1_, bf16[1152,1076]{1,0:T(8,128)(2,1)} %convolution_convert_fusion.refs_2_), custom_call_target="tpu_custom_call" | custom-call | bytes 120000000 | tf_op jit(solution)/shard_map/line_share/pallas_call | solution.py:316
  602.4 5.5 multiply_reduce_fusion
  607.9 5.3 multiply_convert_fusion
  615.6 5.0 convolution_convert_fusion.8.refs_0_
  630.6 76.6 %line_share.7 = (bf16[736,1152]{1,0:T(8,128)(2,1)}, f32[288,864]{1,0:T(8,128)}, f32[288,288]{1,0:T(8,128)}) custom-call(bf16[736,1152]{1,0:T(8,128)(2,1)} %convolution_convert_fusion.8.refs_0_, bf16[1152,864]{1,0:T(8,128)(2,1)} %convolution_convert_fusion.4.refs_1_, bf16[1152,288]{1,0:T(8,128)(2,1)} %convolution_convert_fusion.14.refs_2_), custom_call_target="tpu_custom_call" | custom-call | bytes 120000000 | tf_op jit(solution)/shard_map/line_share/pallas_call | solution.py:316
  727.3 44.6 %all-reduce.6.cloned.1.call-done = (f32[2,6260]{1,0:T(2,128)}, f32[2,2304]{1,0:T(2,128)}) async-done(((f32[2,6260]{1,0:T(2,128)}, f32[2,2304]{1,0:T(2,128)}), (f32[2,6260]{1,0:T(2,128)}, f32[2,2304]{1,0:T(2,128)})) %all-reduce.6.cloned.1.call-update) | async-done | bytes 68528 | tf_op jit(solution)/shard_map/psum | solution.py:636
  787.7 4.3 copy.166
  (315 shorter events, 194.6 us)
Async XLA Ops:
  7.2 26.8 %copy-start = (bf16[2,1,729,1152]{3,0,2,1:T(2,128)(2,1)S(1)}, bf16[2,1,729,1152]{3,0,2,1:T(2,128)(2,1)}, u32[]{:S(2)}) copy-start(bf16[2,1,729,1152]{3,0,2,1:T(2,128)(2,1)} %param.10) | copy-start | bytes 10077700
  7.2 53.9 %all-gather.8.cloned.1.call-start = ((), (), s32[]{:S(2)}) async-start(), calls=%async_computation | async-start | bytes 6635520 | tf_op jit(solution)/shard_map/all_gather | solution.py:558
  7.2 8.6 %copy-start.60 = (bf16[1,4,288]{2,1,0:T(4,128)(2,1)S(1)}, bf16[1,4,288]{2,1,0:T(4,128)(2,1)}, u32[]{:S(2)}) copy-start(bf16[1,4,288]{2,1,0:T(4,128)(2,1)} %param.19) | copy-start | bytes 6916
  7.3 8.6 %copy-start.62 = (bf16[1,2,288]{2,1,0:T(2,128)(2,1)S(1)}, bf16[1,2,288]{2,1,0:T(2,128)(2,1)}, u32[]{:S(2)}) copy-start(bf16[1,2,288]{2,1,0:T(2,128)(2,1)} %param.18) | copy-start | bytes 3460
  7.3 19.5 %copy-start.61 = (bf16[1,2,288]{2,1,0:T(2,128)(2,1)S(1)}, bf16[1,2,288]{2,1,0:T(2,128)(2,1)}, u32[]{:S(2)}) copy-start(bf16[1,2,288]{2,1,0:T(2,128)(2,1)} %param.13) | copy-start | bytes 3460
  7.3 19.5 %copy-start.59 = (bf16[1,1076]{1,0:T(2,128)(2,1)S(1)}, bf16[1,1076]{1,0:T(2,128)(2,1)}, u32[]{:S(2)}) copy-start(bf16[1,1076]{1,0:T(2,128)(2,1)} %param.16) | copy-start | bytes 6460
  7.3 19.6 %copy-start.63 = (u32[32]{0:T(128)S(1)}, u32[32]{0:T(128)}, u32[]{:S(2)}) copy-start(u32[32]{0:T(128)} %constant.83) | copy-start | bytes 388
  14.3 129.1 %all-gather.12.cloned.1.call-start = ((), (), s32[]{:S(2)}) async-start(), calls=%async_computation.2 | async-start | bytes 5971968 | tf_op jit(solution)/shard_map/all_gather | solution.py:558
  15.1 134.6 %all-gather.10.cloned.1.call-start = ((), (), s32[]{:S(2)}) async-start(), calls=%async_computation.1 | async-start | bytes 5971968 | tf_op jit(solution)/shard_map/all_gather | solution.py:558
  15.8 756.1 %all-reduce.6.cloned.1.call-start = ((), (), s32[]{:S(2)}) async-start(), calls=%async_computation.3 | async-start | bytes 137216 | tf_op jit(solution)/shard_map/psum | solution.py:636
  46.7 18.2 %copy-start.51 = (f32[1152]{0:T(1024)}, f32[1152]{0:T(1024)S(1)}, u32[]{:S(2)}) copy-start(f32[1152]{0:T(1024)S(1)} %get-tuple-element.121) | copy-start | bytes 13828
  46.7 18.2 %copy-start.54 = (f32[1152]{0:T(1024)}, f32[1152]{0:T(1024)S(1)}, u32[]{:S(2)}) copy-start(f32[1152]{0:T(1024)S(1)} %get-tuple-element.120) | copy-start | bytes 13828
  46.7 18.2 %copy-start.49 = (f32[736]{0:T(1024)}, f32[736]{0:T(1024)S(1)}, u32[]{:S(2)}) copy-start(f32[736]{0:T(1024)S(1)} %broadcast_multiply_fusion.11) | copy-start | bytes 8836
  47.3 17.6 %copy-start.47 = (f32[736]{0:T(1024)}, f32[736]{0:T(1024)S(1)}, u32[]{:S(2)}) copy-start(f32[736]{0:T(1024)S(1)} %add_rsqrt_fusion.3) | copy-start | bytes 8836
  416.9 10.2 %slice-start.3 = ((s8[9043968]{0:T(1024)(128)(4,1)}), s8[4194304]{0:T(1024)(128)(4,1)S(1)}, s32[]{:S(2)}) async-start(s8[9043968]{0:T(1024)(128)(4,1)} %bitcast.157), calls=%async_computation.7 | async-start | bytes 8388608
  424.4 26.9 %copy-start.9 = (f32[736,1152]{1,0:T(8,128)}, f32[736,1152]{1,0:T(8,128)S(1)}, u32[]{:S(2)}) copy-start(f32[736,1152]{1,0:T(8,128)S(1)} %get-tuple-element.135) | copy-start | bytes 10174468
  429.0 18.5 %copy-start.45 = (bf16[4,72,736]{2,1,0:T(8,128)(2,1)}, bf16[4,72,736]{2,1,0:T(8,128)(2,1)S(1)}, u32[]{:S(2)}) copy-start(bf16[4,72,736]{2,1,0:T(8,128)(2,1)S(1)} %fusion.76) | copy-start | bytes 1271812
  519.1 10.2 %slice-start.8 = ((s8[5308416]{0:T(1024)(128)(4,1)}), s8[1114112]{0:T(1024)(128)(4,1)S(1)}, s32[]{:S(2)}) async-start(s8[5308416]{0:T(1024)(128)(4,1)} %bitcast.234), calls=%async_computation.12 | async-start | bytes 2228224
  533.3 67.3 %slice-start = ((s8[9043968]{0:T(1024)(128)(4,1)}), s8[655360]{0:T(1024)(128)(4,1)S(1)}, s32[]{:S(2)}) async-start(s8[9043968]{0:T(1024)(128)(4,1)} %bitcast.155), calls=%async_computation.4 | async-start | bytes 1310720
  591.6 8.9 %slice-start.1 = ((s8[9043968]{0:T(1024)(128)(4,1)}), s8[4194304]{0:T(1024)(128)(4,1)S(1)}, s32[]{:S(2)}) async-start(s8[9043968]{0:T(1024)(128)(4,1)} %bitcast.155), calls=%async_computation.5 | async-start | bytes 8388608
  597.9 26.4 %copy-start.7 = (f32[736,1152]{1,0:T(8,128)}, f32[736,1152]{1,0:T(8,128)S(1)}, u32[]{:S(2)}) copy-start(f32[736,1152]{1,0:T(8,128)S(1)} %get-tuple-element.133) | copy-start | bytes 10174468
  630.4 146.0 %collective-permute-start = (bf16[729,1152]{1,0:T(8,128)(2,1)}, bf16[729,1152]{1,0:T(8,128)(2,1)}, u32[]{:S(2)}, u32[]{:S(2)}) collective-permute-start(bf16[729,1152]{1,0:T(8,128)(2,1)} %broadcast_select_fusion.1), channel_id=1, source_target_pairs={{0,16},{16,0},{1,17},{17,1},{2,18},{18,2},{3,19},{19,3},{4,20},{20... | collective-permute-start | bytes 5038856 | tf_op jit(solution)/shard_map/ppermute | solution.py:607
  714.8 69.3 %collective-permute-start.1 = (bf16[729,1152]{1,0:T(8,128)(2,1)}, bf16[729,1152]{1,0:T(8,128)(2,1)}, u32[]{:S(2)}, u32[]{:S(2)}) collective-permute-start(bf16[729,1152]{1,0:T(8,128)(2,1)} %broadcast_select_fusion), channel_id=1, source_target_pairs={{0,16},{16,0},{1,17},{17,1},{2,18},{18,2},{3,19},{19,3},{4,20},{20... | collective-permute-start | bytes 5038856 | tf_op jit(solution)/shard_map/ppermute | solution.py:607
  722.9 53.5 %copy-start.19 = (bf16[1,1,1,729,1152]{4,3,2,1,0:T(8,128)(2,1)S(1)}, bf16[1,1,1,729,1152]{4,3,2,1,0:T(8,128)(2,1)}, u32[]{:S(2)}) copy-start(bf16[1,1,1,729,1152]{4,3,2,1,0:T(8,128)(2,1)} %get-tuple-element.138) | copy-start | bytes 5038852
  (61 other events, 253.2 us)
Sparse Core Ops, SparseCore 0:
  14.4 46.6 all-gather.7
  63.0 41.2 all-gather.11
  106.2 41.2 all-gather.9
  719.0 52.8 all-reduce.5

commit v3 on v2

--- a/solution.py
+++ b/solution.py
@@ -265,12 +265,187 @@
     )(x)
 
 
-def line_share_kernel(count, rows, lag, ways, layer, cuts, k, *refs):
-    x_ref, g_refs = refs[0], refs[1 : 1 + k]
-    o_ref, go_refs = refs[1 + k], refs[2 + k : 2 + 2 * k]
-    scratch = refs[2 + 2 * k :]
-    line = Line(count, rows, lag, x_ref, o_ref, *scratch[:2], scratch[2:6])
-    scratch = scratch[6:]
+class Swap:
+    def __init__(self, line, layer, refs, outs, bufs):
+        self.line, self.layer = line, layer
+        self.u, self.grad, self.gain, self.ready = refs
+        self.mine, self.got, self.late = outs
+        self.sems = bufs[:2]
+        self.small = Small(self.late, self.late, bufs[2:])
+        self.section = lax.axis_index("section")
+        self.first = 2 * line.lag * (line.count - 1)
+        self.steps = line.pieces // 2
+        self.rows = 2 * line.rows
+
+    def span(self, index):
+        return pl.ds(pl.multiple_of(index * self.rows, self.rows), self.rows)
+
+    def copy(self, source, index):
+        return pltpu.make_async_remote_copy(
+            src_ref=source.at[self.span(index)],
+            dst_ref=self.got.at[self.span(index)],
+            send_sem=self.sems[0].at[index],
+            recv_sem=self.sems[1].at[index],
+            device_id={"section": 1 - self.section},
+            device_id_type=MESH,
+        )
+
+    def start(self):
+        self.late[...] = jnp.zeros_like(self.late)
+
+    def step(self, index):
+        span = self.span(index)
+        one = self.line.o[span, :].astype(F32)
+        _, normed, inverse = norm_forward(self.u[span, :].astype(F32), 1.0, 0.0)
+        moved, gain_part, shift_part = norm_backward(one, normed, inverse, self.gain[...])
+        self.mine[span, :] = (self.grad[span, :] + moved).astype(BF16)
+        self.late[0:1, :] += gain_part.reshape(1, -1)
+        self.late[1:2, :] += shift_part.reshape(1, -1)
+
+        @pl.when(self.section == self.layer)
+        def _():
+            self.copy(self.ready, index).start()
+
+        @pl.when(self.section != self.layer)
+        def _():
+            self.copy(self.mine, index).start()
+
+    def finish(self):
+        for level in range(self.small.levels + 2):
+            self.small.step(level)
+
+        def end_steps(index, _):
+            @pl.when(self.section == self.layer)
+            def _():
+                self.copy(self.ready, index).wait_send()
+
+            @pl.when(self.section != self.layer)
+            def _():
+                self.copy(self.mine, index).wait_send()
+
+            self.copy(self.got, index).wait_recv()
+            return 0
+
+        lax.fori_loop(0, self.steps, end_steps, 0)
+        self.small.finish()
+
+    @staticmethod
+    def scratch(x, ways, rows):
+        return Pass.scratch(x, rows) + Small.scratch((8, x.shape[1]), ways)
+
+
+class Pass:
+    def __init__(self, line, pair, got, sems):
+        self.pair, self.got, self.sems = pair, got, sems
+        self.section = lax.axis_index("section")
+        self.rows = 2 * line.rows
+        self.steps = got.shape[0] // self.rows
+
+    def copy(self, source, index):
+        span = pl.ds(pl.multiple_of(index * self.rows, self.rows), self.rows)
+        return pltpu.make_async_remote_copy(
+            src_ref=source.at[span],
+            dst_ref=self.got.at[span],
+            send_sem=self.sems[0].at[index],
+            recv_sem=self.sems[1].at[index],
+            device_id={"section": 1 - self.section},
+            device_id_type=MESH,
+        )
+
+    def step(self, index):
+        for place in range(2):
+
+            @pl.when(self.section == 1 - place)
+            def _():
+                self.copy(self.pair[place], index).start()
+
+    def finish(self):
+        def end_steps(index, _):
+            for place in range(2):
+
+                @pl.when(self.section == 1 - place)
+                def _():
+                    self.copy(self.pair[place], index).wait_send()
+
+            self.copy(self.got, index).wait_recv()
+            return 0
+
+        lax.fori_loop(0, self.steps, end_steps, 0)
+
+    @staticmethod
+    def scratch(x, rows):
+        return [pltpu.SemaphoreType.DMA((x.shape[0] // (2 * rows),))] * 2
+
+
+class Small:
+    def __init__(self, value, total, bufs):
+        self.value, self.total = value, total
+        self.levels = lax.axis_size("fsdp").bit_length() - 1
+        n = self.levels + 1
+        self.away, self.near, self.sems = bufs[:n], bufs[n : 2 * n], bufs[2 * n :]
+
+    def copy(self, level):
+        me = lax.axis_index("fsdp")
+        if level < self.levels:
+            there = {"fsdp": me + (1 - 2 * (me // (1 << level) % 2)) * (1 << level)}
+        else:
+            there = {"section": 1 - lax.axis_index("section")}
+        return pltpu.make_async_remote_copy(
+            src_ref=self.away[level],
+            dst_ref=self.near[level],
+            send_sem=self.sems[0].at[level],
+            recv_sem=self.sems[1].at[level],
+            device_id=there,
+            device_id_type=MESH,
+        )
+
+    def step(self, level):
+        if level == 0:
+            now = self.value[...]
+        else:
+            self.copy(level - 1).wait_recv()
+            now = self.away[level - 1][...] + self.near[level - 1][...]
+        if level > self.levels:
+            self.total[...] = now
+        else:
+            self.away[level][...] = now
+            self.copy(level).start()
+
+    def finish(self):
+        for level in range(self.levels + 1):
+            self.copy(level).wait_send()
+
+    @staticmethod
+    def scratch(shape, ways):
+        n = ways.bit_length()
+        return [pltpu.VMEM(shape, F32)] * (2 * n) + [pltpu.SemaphoreType.DMA((n,))] * 2
+
+
+def line_share_kernel(count, rows, lag, ways, layer, cuts, k, trade, small, passing, *refs):
+    refs = list(refs)
+
+    def take(number):
+        taken, refs[:] = refs[:number], refs[number:]
+        return taken
+
+    x_ref, g_refs = take(1)[0], take(k)
+    swap_refs, small_ref, pair = take(4 * trade), take(small), take(2 * passing)
+    go_refs = take(k)
+    swap_outs, small_out, got = take(3 * trade), take(small), take(passing)
+    o_ref = take(1)[0]
+    line = Line(count, rows, lag, x_ref, o_ref, *take(2), take(4))
+    swap, extra = None, []
+    each = 2 * ways.bit_length() + 2
+    if trade:
+        swap = Swap(line, layer, swap_refs, swap_outs, take(2 + each))
+        swap.start()
+    if small:
+        sums = Small(small_ref[0], small_out[0], take(each))
+        extra.append(sums)
+    if passing:
+        pass_on = Pass(line, pair, got[0], take(2))
+        extra.append(pass_on)
+    scratch = refs
     each = len(scratch) // k
     shares = [
         Share(ways, layer, cuts, g_refs[i], go_refs[i], scratch[i * each : (i + 1) * each]) for i in range(k)
@@ -283,51 +458,109 @@
     for level in range(1, levels + 2):
         first, stride = (4, 1) if level == 1 else (3 + 6 * (level - 1), 5)
         steps += [(first + i * cuts * stride, stride, level, share) for i, share in enumerate(shares)]
-    turns = max(line.turns, max(first + stride * (cuts - 1) + 1 for first, stride, _, _ in steps))
+    if trade:
+        steps.append((swap.first, 1, 0, swap))
+    turns = max(line.turns, max(first + stride * (cuts - 1) + 1 for first, stride, _, item in steps if item is not swap))
 
     def turn(s, _):
         line.turn(s)
+        if small:
+            for level in range(levels + 2):
+
+                @pl.when(s == 6 * level + 2)
+                def _():
+                    sums.step(level)
+
+        if passing:
+
+            @pl.when((s % 2 == 0) & (s // 2 < pass_on.steps))
+            def _():
+                pass_on.step(s // 2)
+
         for first, stride, level, share in steps:
             past = s - first
             piece = past // stride
+
+            if share is swap:
+
+                @pl.when((past >= 0) & (past < swap.steps))
+                def _():
+                    swap.step(past)
+
+                continue
 
             @pl.when((past >= 0) & (past % stride == 0) & (piece < cuts))
             def _():
                 share.step(level, piece)
         return 0
 
+    if small:
+        turns = max(turns, 6 * (levels + 2) + 1)
+    if passing:
+        turns = max(turns, 2 * pass_on.steps)
     lax.fori_loop(0, turns, turn, 0)
+    if trade:
+        swap.finish()
+    for item in extra:
+        item.finish()
     line.finish()
     for share in shares:
         share.finish()
 
 
-def line_share(x, grads, layer, cid, rows=16, lag=4):
+def line_share(x, grads, layer, cid, trade=(), small=None, pair=(), rows=16, lag=4):
     count, ways = lax.axis_size("tensor"), lax.axis_size("fsdp")
     height = grads[0].shape[0] // ways
     shapes = [(height, g.shape[1]) for g in grads]
     cuts = 3 if height % (3 * TILE) == 0 else 1
     if height % TILE:
         grads = [g.reshape(ways, height, g.shape[1]) for g in grads]
+    total = jax.ShapeDtypeStruct(x.shape, BF16)
     scratch = Line.scratch(x, rows)
+    outs = [jax.ShapeDtypeStruct(shape, F32) for shape in shapes]
+    args = [x, *grads, *trade]
+    if trade:
+        outs += [total, total, jax.ShapeDtypeStruct((8, x.shape[1]), F32)]
+        scratch += Swap.scratch(x, ways, rows)
+    if small is not None:
+        args.append(small)
+        outs.append(jax.ShapeDtypeStruct(small.shape, F32))
+        scratch += Small.scratch(small.shape, ways)
+    if pair:
+        args += pair
+        outs.append(total)
+        scratch += Pass.scratch(x, rows)
+    if trade:
+        scratch = [pltpu.VMEM(x.shape, BF16)] + scratch
+    else:
+        outs.append(total)
     for shape in shapes:
         scratch += Share.scratch(shape, ways, cuts)
     vmem = pl.BlockSpec(memory_space=pltpu.VMEM)
     return pl.pallas_call(
         functools.partial(
-            line_share_kernel, count, rows, lag, ways, layer, cuts, len(grads)
+            line_share_kernel,
+            count,
+            rows,
+            lag,
+            ways,
+            layer,
+            cuts,
+            len(grads),
+            bool(trade),
+            small is not None,
+            bool(pair),
         ),
-        out_shape=[jax.ShapeDtypeStruct(x.shape, BF16)]
-        + [jax.ShapeDtypeStruct(shape, F32) for shape in shapes],
-        in_specs=[vmem] * (1 + len(grads)),
-        out_specs=[vmem] * (1 + len(grads)),
+        out_shape=outs,
+        in_specs=[vmem] * len(args),
+        out_specs=[vmem] * len(outs),
         scratch_shapes=scratch,
         compiler_params=pltpu.CompilerParams(
-            collective_id=cid, has_side_effects=True, vmem_limit_bytes=56 * 1024 * 1024
+            collective_id=cid, has_side_effects=True, vmem_limit_bytes=60 * 1024 * 1024
         ),
         name="line_share",
         cost_estimate=pl.CostEstimate(flops=0, bytes_accessed=120_000_000, transcendentals=0),
-    )(x, *grads)
+    )(*args)
 
 
 def tensor_sum(value):
@@ -415,7 +648,7 @@
         active.append(gelu_value(pre_act[-1]).astype(BF16))
         mlp_term = dot_nt(active[-1], down_t).astype(BF16)
         if is_last:
-            outputs.append(lambda total, rows=rows: (rows + total.astype(F32) + shifts[3]).astype(BF16))
+            outputs.append(None)
             stored_term = mlp_term
             continue
         outputs.append((rows + line_sum(mlp_term, 0).astype(F32) + shifts[3]).astype(BF16))
@@ -436,7 +669,7 @@
     return outputs, stored, stored_term
 
 
-def layer_backward(grads, stored, weights, gains, shifts, cuts, real, layer, extra):
+def layer_backward(grads, stored, weights, gains, shifts, cuts, real, layer, extra, ready, small):
     qkv, out_t, up, down_t = weights
     (
         inputs,
@@ -465,8 +698,9 @@
     grad_down = dot_tn(mix_all, jnp.concatenate(active))
     grad_up = dot_tn(jnp.concatenate(normed_two), pre_all)
     count = two_terms[0].shape[0]
+    extra_rows, last_shift = hidden[0], shifts[3]
     two = two_terms[0] if extra is None else jnp.concatenate([two_terms[0], extra])
-    two, grad_down, grad_up = line_share(
+    grad_down, grad_up, two = line_share(
         two, [grad_down.astype(BF16), grad_up.astype(BF16)], layer, 1 + 2 * layer
     )
     two_terms = [two[:count].astype(F32)]
@@ -513,22 +747,25 @@
     grad_out = dot_tn(attn_all, context_all)
     grad_qkv = dot_tn(normed_one, grad_proj)
     bias_sums = jnp.sum(grad_proj.astype(F32), axis=0)
-    grad_inputs = []
-    gain_one, shift_one = 0.0, 0.0
-    one, grad_qkv, grad_out = line_share(
-        dot_nt(grad_proj, qkv).astype(BF16), [grad_qkv.astype(BF16), grad_out.astype(BF16)], layer, 2 + 2 * layer
-    )
-    one_terms = [one.astype(F32)]
-    for one, part, rows in zip(one_terms, inputs, grad_hidden):
-        normed, inverse = norm_forward(part.astype(F32), gains[0], shifts[0])[1:]
-        moved, gain_part, shift_part = norm_backward(one, normed, inverse, gains[0])
-        gain_one += gain_part
-        shift_one += shift_part
-        grad_inputs.append((rows + moved).astype(BF16))
-    gain_grads = [gain_two, attn_shift, shift_two, mix_shift]
-    bias_grads = jnp.concatenate([bias_sums[:width], bias_sums[2 * width :], up_bias_grad])
-    late = jnp.concatenate([gain_one, shift_one])
-    return grad_inputs, extra, (grad_qkv, grad_out, grad_up, grad_down), (jnp.concatenate(gain_grads + [bias_grads]), late)
+    send = [dot_nt(grad_proj, qkv).astype(BF16), [grad_qkv.astype(BF16), grad_out.astype(BF16)], layer, 2 + 2 * layer]
+    sums = [gain_two, attn_shift, shift_two, mix_shift]
+    sums += [bias_sums[:width], bias_sums[2 * width :], up_bias_grad]
+    late = other = None
+    if ready is not None:
+        sums = jnp.concatenate(sums + small)
+        sums = jnp.pad(sums, (0, -sums.shape[0] % (8 * part.shape[1]))).reshape(-1, part.shape[1])
+        trade = (inputs[0], grad_hidden[0], gains[:1], ready)
+        grad_qkv, grad_out, mine, other, late, sums = line_share(*send, trade, sums)
+    else:
+        first = inputs[0]
+        last = (extra_rows + extra.astype(F32) + last_shift).astype(BF16)
+        grad_qkv, grad_out, other, one = line_share(*send, pair=(first, last))
+        other = (first, last, other)
+        normed, inverse = norm_forward(inputs[0].astype(F32), gains[0], shifts[0])[1:]
+        moved, gain_one, shift_one = norm_backward(one.astype(F32), normed, inverse, gains[0])
+        mine = (grad_hidden[0] + moved).astype(BF16)
+        sums += [gain_one, shift_one]
+    return mine, other, (grad_qkv, grad_out, grad_up, grad_down), sums, late
 
 
 def per_device(
@@ -601,20 +838,16 @@
         outputs.append(rows[0])
         stored.append(kept)
 
-    def swapped(pair):
-        pair = [item[:seq_len] for item in pair]
-        mine = jnp.where(is_first, pair[0], pair[1])
-        other = lax.ppermute(jnp.where(is_first, pair[1], pair[0]), "section", [(0, 1), (1, 0)])
-        return jnp.where(
-            is_first, jnp.stack([mine, other]), jnp.stack([other, mine])
-        )[None, :, None]
+    def placed(mine, other):
+        mine, other = mine[:seq_len], other[:seq_len]
+        return jnp.where(is_first, jnp.stack([mine, other]), jnp.stack([other, mine]))[None, :, None]
 
     grads = [own_grad[first:last] for first, last in cuts]
     input_grads = [None, None]
     weight_grads = [None, None]
-    small = [None, None]
+    small = ready = None
     for index in (1, 0):
-        grads, total, weight_grads[index], small[index] = layer_backward(
+        mine, other, weight_grads[index], small, late = layer_backward(
             grads,
             stored[index],
             layer_args(index),
@@ -624,19 +857,22 @@
             seq_len,
             index,
             last_term if index == 1 else None,
+            ready,
+            small,
         )
         if index == 1:
-            section_outputs = swapped([outputs[0], outputs[1](total)])
-        input_grads[index] = jnp.concatenate(grads)
-    input_grads = swapped(input_grads)
-
+            ready, grads = mine, [mine]
+            first, last, other = other
+            section_outputs = placed(jnp.where(is_first, first, last), other)
+        else:
+            input_grads = placed(jnp.where(is_first, mine, ready), other)
     grad_qkv, grad_out, grad_up, grad_down = [
         jnp.where(is_first, first, second) for first, second in zip(*weight_grads)
     ]
-    packed = lax.psum(jnp.stack([small[0][0], small[1][0]]), every)
-    late = lax.psum(jnp.stack([small[0][1], small[1][1]]), every)
-    packed = jnp.where(is_first, packed[0], packed[1])
-    late = jnp.where(is_first, late[0], late[1]).reshape(2, model_width)
+    each = 4 * model_width + 2 * width + units
+    small = small.reshape(-1)
+    packed = jnp.where(is_first, small[:each], small[each : 2 * each])
+    late = jnp.where(is_first, late[:2], small[2 * each : 2 * each + 2 * model_width].reshape(2, model_width))
     norm_part = packed[: 4 * model_width].reshape(4, model_width)
     norm_part = jnp.stack([late[0], norm_part[0], late[1], norm_part[1], norm_part[2], norm_part[3]])
     norm_part = lax.dynamic_slice_in_dim(norm_part, fsdp * rows_here, rows_here, 1)

time: 803 us -> 771 us (0.960)
  waiting for transfers between devices: 59.9 us -> 14.6 us
  Pallas kernels: 445 us -> 457 us
    psum x1 -> x0, waiting for transfers between devices: 44.6 us -> none  [per_device(): packed = lax.psum(jnp.stack([small[0][0], small[1][0]]), every)]
    pallas_call x4, Pallas kernels: 287 us -> 299 us  [line_share(): pl.pallas_call(functools.partial(line_share_kernel, count, rows, lag, way...]
    unnamed x171 -> x147, local copies, waits for them, and re-layouts: 28.7 us -> 26.1 us
  transfers between devices with their start and end apart: 6 -> 3, of which waited for: 2 -> 1; matrix products, arithmetic and copies ran while one was open for 10% -> 6% of each run, Pallas kernels for 16% -> 7%
where the time goes in v3:
time: 771 us; the launch traced here: 764 us
  Pallas kernels  457 us (59%)
  matrix products  127 us (16%)
  other arithmetic  76.2 us (10%)
  local copies, waits for them, and re-layouts  57.5 us (7%)
  blocking collectives  16 us (2%)
  between operations  15.9 us (2%)
  waiting for transfers between devices  14.6 us (2%)
    pallas_call x4, Pallas kernels, line_share(): pl.pallas_call(functools.partial(line_share_kernel, count, rows, lag, way...  299 us
    pallas_call x3, Pallas kernels, line_sum(): pl.pallas_call(functools.partial(line_sum_kernel, count, rows, lag), out_...  158 us
    dot_general x8, matrix products, dot_nt(): lax.dot_general(left, right, (((1,), (1,)), ((), ())), preferred_element_...  34.2 us
    dot_general x8, matrix products, dot_nn(): return jnp.dot(left, right, preferred_element_type=F32)  34.1 us
    dot_general x8, matrix products, dot_tn(): lax.dot_general(left, right, (((0,), (0,)), ((), ())), preferred_element_...  29.7 us
    unnamed x147, local copies, waits for them, and re-layouts  26.1 us
  transfers between devices with their start and end apart: 3, of which 1 were waited for; matrix products, arithmetic and copies ran while one was open for 6% of the time, Pallas kernels for 7%

profile of v3, /device:TPU:0, one launch (start us, length us, event | category | flops | bytes accessed | tf_op | source)
XLA Modules:
  0.0 764.3 jit_solution(7591112559184279616)
XLA Ops:
  19.9 10.8 %all-gather.3 = bf16[8,6,288]{2,1,0:T(8,128)(2,1)S(1)} all-gather(bf16[1,6,288]{2,1,0:T(8,128)(2,1)S(1)} %maximum_bitcast_fusion), channel_id=2, replica_groups=mesh['section'=2,'tensor'=4,'fsdp'=4] {'section','fsdp'}, dimensions={0}, use_global_device_ids=true | all-gather | bytes 31104 | tf_op jit(solution)/shard_map/all_gather | solution.py:813
  32.6 5.1 all-reduce.3
  37.9 5.4 constant_dynamic-slice_fusion
  47.8 13.2 %all-gather.8.cloned.1.call-done = bf16[2304,1184]{1,0:T(8,128)(2,1)} async-done(((bf16[288,1184]{1,0:T(8,128)(2,1)}), bf16[2304,1184]{1,0:T(8,128)(2,1)}) %all-gather.8.cloned.1.call-update) | async-done | bytes 5455888 | tf_op jit(solution)/shard_map/all_gather | solution.py:795
  86.8 53.9 %line_sum.3 = bf16[736,1152]{1,0:T(8,128)(2,1)} custom-call(bf16[736,1152]{1,0:T(8,128)(2,1)} %convolution_convert_fusion.7.x_ref), custom_call_target="tpu_custom_call" | custom-call | bytes 120000000 | tf_op jit(solution)/shard_map/line_sum/pallas_call | solution.py:256
  143.9 6.7 convolution_add_fusion.1
  150.6 7.2 convolution_convert_fusion.13.x_ref
  157.7 52.5 %line_sum.4 = bf16[736,1152]{1,0:T(8,128)(2,1)} custom-call(bf16[736,1152]{1,0:T(8,128)(2,1)} %convolution_convert_fusion.13.x_ref), custom_call_target="tpu_custom_call" | custom-call | bytes 120000000 | tf_op jit(solution)/shard_map/line_sum/pallas_call | solution.py:256
  239.6 51.9 %line_sum.5 = bf16[736,1152]{1,0:T(8,128)(2,1)} custom-call(bf16[736,1152]{1,0:T(8,128)(2,1)} %convolution_convert_fusion.6.x_ref), custom_call_target="tpu_custom_call" | custom-call | bytes 120000000 | tf_op jit(solution)/shard_map/line_sum/pallas_call | solution.py:256
  294.6 5.1 convolution_add_fusion
  308.4 4.9 convolution_convert_fusion.2.refs_2_
  321.3 96.7 %line_share.4 = (f32[288,1076]{1,0:T(8,128)}, f32[288,1076]{1,0:T(8,128)}, bf16[1472,1152]{1,0:T(8,128)(2,1)}) custom-call(bf16[1472,1152]{1,0:T(8,128)(2,1)} %pad_maximum_fusion.refs_0_, bf16[1152,1076]{1,0:T(8,128)(2,1)} %convolution_convert_fusion.3.refs_1_, bf16[1152,1076]{1,0:T(8,128)(2,1)} %convolution_convert_fusion.2.refs_2_), custom_call_target="tpu_custom_call" | custom-call | bytes 120000000 | tf_op jit(solution)/shard_map/line_share/pallas_call | solution.py:540
  422.1 6.1 convert_reduce_fusion.7
  430.8 5.6 multiply_reduce_fusion.1
  436.4 5.2 multiply_convert_fusion.1
  452.0 5.0 convolution_convert_fusion.10.refs_0_
  457.0 62.2 %line_share.5 = (f32[288,864]{1,0:T(8,128)}, f32[288,288]{1,0:T(8,128)}, bf16[736,1152]{1,0:T(8,128)(2,1)}, bf16[736,1152]{1,0:T(8,128)(2,1)}) custom-call(bf16[736,1152]{1,0:T(8,128)(2,1)} %convolution_convert_fusion.10.refs_0_, bf16[1152,864]{1,0:T(8,128)(2,1)} %convolution_convert_fusion.5.refs_1_, bf16[1152,288]{1,0:T(8,128)(2,1)} %convolution_convert_fusion.15.refs_2_, ...), custom_call_target="tpu_custom_call" | custom-call | bytes 120000000 | tf_op jit(solution)/shard_map/line_share/pallas_call | solution.py:540
  529.5 5.1 convert_reduce_fusion.10
  543.4 59.4 %line_share.6 = (f32[288,1076]{1,0:T(8,128)}, f32[288,1076]{1,0:T(8,128)}, bf16[736,1152]{1,0:T(8,128)(2,1)}) custom-call(bf16[736,1152]{1,0:T(8,128)(2,1)} %convolution_convert_fusion.9.refs_0_, bf16[1152,1076]{1,0:T(8,128)(2,1)} %convolution_convert_fusion.1.refs_1_, bf16[1152,1076]{1,0:T(8,128)(2,1)} %convolution_convert_fusion.refs_2_), custom_call_target="tpu_custom_call" | custom-call | bytes 120000000 | tf_op jit(solution)/shard_map/line_share/pallas_call | solution.py:540
  602.8 4.8 fusion.49
  613.8 5.7 multiply_reduce_fusion
  619.4 5.5 multiply_convert_fusion
  635.5 5.0 convolution_convert_fusion.8.refs_0_
  641.4 80.6 %line_share.7 = (f32[288,864]{1,0:T(8,128)}, f32[288,288]{1,0:T(8,128)}, bf16[736,1152]{1,0:T(8,128)(2,1)}, bf16[736,1152]{1,0:T(8,128)(2,1)}, f32[8,1152]{1,0:T(8,128)}, /*index=5*/f32[16,1152]{1,0:T(8,128)}) custom-call(bf16[736,1152]{1,0:T(8,128)(2,1)} %convolution_convert_fusion.8.refs_0_, bf16[1152,864]{1,0:T(8,128)(2,1)} %convolution_convert_fusion.4.refs_1_, ...), custom_call_target="tpu_custom_call" | custom-call | bytes 120000000 | tf_op jit(solution)/shard_map/line_share/pallas_call | solution.py:540
  (282 shorter events, 184.7 us)
Async XLA Ops:
  7.2 53.8 %all-gather.8.cloned.1.call-start = ((), (), s32[]{:S(2)}) async-start(), calls=%async_computation | async-start | bytes 6635520 | tf_op jit(solution)/shard_map/all_gather | solution.py:795
  14.3 129.6 %all-gather.12.cloned.1.call-start = ((), (), s32[]{:S(2)}) async-start(), calls=%async_computation.2 | async-start | bytes 5971968 | tf_op jit(solution)/shard_map/all_gather | solution.py:795
  15.0 135.6 %all-gather.10.cloned.1.call-start = ((), (), s32[]{:S(2)}) async-start(), calls=%async_computation.1 | async-start | bytes 5971968 | tf_op jit(solution)/shard_map/all_gather | solution.py:795
  19.3 11.7 %copy-start.49 = (bf16[1,2,288]{2,1,0:T(2,128)(2,1)S(1)}, bf16[1,2,288]{2,1,0:T(2,128)(2,1)}, u32[]{:S(2)}) copy-start(bf16[1,2,288]{2,1,0:T(2,128)(2,1)} %param.13) | copy-start | bytes 3460
  19.3 11.8 %copy-start.51 = (u32[32]{0:T(128)S(1)}, u32[32]{0:T(128)}, u32[]{:S(2)}) copy-start(u32[32]{0:T(128)} %constant.84) | copy-start | bytes 388
  19.3 13.0 %copy-start.45 = (bf16[1,1076]{1,0:T(2,128)(2,1)S(1)}, bf16[1,1076]{1,0:T(2,128)(2,1)}, u32[]{:S(2)}) copy-start(bf16[1,1076]{1,0:T(2,128)(2,1)} %param.16) | copy-start | bytes 6460
  19.5 124.3 %copy-start.6 = (bf16[1,1,729,1152]{3,2,1,0:T(8,128)(2,1)}, bf16[1,1,729,1152]{3,2,1,0:T(8,128)(2,1)S(1)}, u32[]{:S(2)}) copy-start(bf16[1,1,729,1152]{3,2,1,0:T(8,128)(2,1)S(1)} %copy.204) | copy-start | bytes 5038852
  47.1 17.5 %copy-start.41 = (f32[1152]{0:T(1024)}, f32[1152]{0:T(1024)S(1)}, u32[]{:S(2)}) copy-start(f32[1152]{0:T(1024)S(1)} %get-tuple-element.124) | copy-start | bytes 13828
  47.1 17.5 %copy-start.43 = (f32[1152]{0:T(1024)}, f32[1152]{0:T(1024)S(1)}, u32[]{:S(2)}) copy-start(f32[1152]{0:T(1024)S(1)} %get-tuple-element.125) | copy-start | bytes 13828
  47.2 17.5 %copy-start.39 = (f32[736]{0:T(1024)}, f32[736]{0:T(1024)S(1)}, u32[]{:S(2)}) copy-start(f32[736]{0:T(1024)S(1)} %broadcast_multiply_fusion.9) | copy-start | bytes 8836
  47.8 16.9 %copy-start.46 = (f32[736]{0:T(1024)}, f32[736]{0:T(1024)S(1)}, u32[]{:S(2)}) copy-start(f32[736]{0:T(1024)S(1)} %add_rsqrt_fusion.3) | copy-start | bytes 8836
  83.1 59.8 %copy-start.34 = (bf16[4,72,736]{2,1,0:T(8,128)(2,1)}, bf16[4,72,736]{2,1,0:T(8,128)(2,1)S(1)}, u32[]{:S(2)}) copy-start(bf16[4,72,736]{2,1,0:T(8,128)(2,1)S(1)} %fusion.81) | copy-start | bytes 1271812
  213.8 234.5 %copy-start.2 = (bf16[736,1152]{1,0:T(8,128)(2,1)}, bf16[736,1152]{1,0:T(8,128)(2,1)S(1)}, u32[]{:S(2)}) copy-start(bf16[736,1152]{1,0:T(8,128)(2,1)S(1)} %get-tuple-element.139.refs_3_) | copy-start | bytes 5087236
  293.7 10.3 %slice-start.10 = ((s8[5308416]{0:T(1024)(128)(4,1)}), s8[4194304]{0:T(1024)(128)(4,1)S(1)}, s32[]{:S(2)}) async-start(s8[5308416]{0:T(1024)(128)(4,1)} %bitcast.234), calls=%async_computation.13 | async-start | bytes 8388608
  294.6 9.4 %slice-start.11 = ((s8[5308416]{0:T(1024)(128)(4,1)}), s8[1114112]{0:T(1024)(128)(4,1)S(1)}, s32[]{:S(2)}) async-start(s8[5308416]{0:T(1024)(128)(4,1)} %bitcast.234), calls=%async_computation.14 | async-start | bytes 2228224
  304.0 9.3 %slice-start.6 = ((s8[5308416]{0:T(1024)(128)(4,1)}), s8[1114112]{0:T(1024)(128)(4,1)S(1)}, s32[]{:S(2)}) async-start(s8[5308416]{0:T(1024)(128)(4,1)} %bitcast.230), calls=%async_computation.9 | async-start | bytes 2228224
  422.0 8.8 %slice-start.3 = ((s8[9043968]{0:T(1024)(128)(4,1)}), s8[4194304]{0:T(1024)(128)(4,1)S(1)}, s32[]{:S(2)}) async-start(s8[9043968]{0:T(1024)(128)(4,1)} %bitcast.158), calls=%async_computation.6 | async-start | bytes 8388608
  422.0 8.8 %slice-start.4 = ((s8[9043968]{0:T(1024)(128)(4,1)}), s8[4194304]{0:T(1024)(128)(4,1)S(1)}, s32[]{:S(2)}) async-start(s8[9043968]{0:T(1024)(128)(4,1)} %bitcast.158), calls=%async_computation.7 | async-start | bytes 8388608
  428.1 17.8 %copy-start.12 = (f32[736,1152]{1,0:T(8,128)}, f32[736,1152]{1,0:T(8,128)S(1)}, u32[]{:S(2)}) copy-start(f32[736,1152]{1,0:T(8,128)S(1)} %get-tuple-element.133) | copy-start | bytes 10174468
  457.0 62.2 %copy-start.3 = (bf16[736,1152]{1,0:T(8,128)(2,1)S(1)}, bf16[736,1152]{1,0:T(8,128)(2,1)}, u32[]{:S(2)}) copy-start(bf16[736,1152]{1,0:T(8,128)(2,1)} %copy-done.2) | copy-start | bytes 5087236
  529.5 9.9 %slice-start.8 = ((s8[5308416]{0:T(1024)(128)(4,1)}), s8[1114112]{0:T(1024)(128)(4,1)S(1)}, s32[]{:S(2)}) async-start(s8[5308416]{0:T(1024)(128)(4,1)} %bitcast.232), calls=%async_computation.11 | async-start | bytes 2228224
  543.4 70.4 %slice-start = ((s8[9043968]{0:T(1024)(128)(4,1)}), s8[655360]{0:T(1024)(128)(4,1)S(1)}, s32[]{:S(2)}) async-start(s8[9043968]{0:T(1024)(128)(4,1)} %bitcast.156), calls=%async_computation.3 | async-start | bytes 1310720
  602.8 10.9 %slice-start.1 = ((s8[9043968]{0:T(1024)(128)(4,1)}), s8[4194304]{0:T(1024)(128)(4,1)S(1)}, s32[]{:S(2)}) async-start(s8[9043968]{0:T(1024)(128)(4,1)} %bitcast.156), calls=%async_computation.4 | async-start | bytes 8388608
  611.0 18.4 %copy-start.14 = (f32[736,1152]{1,0:T(8,128)}, f32[736,1152]{1,0:T(8,128)S(1)}, u32[]{:S(2)}) copy-start(f32[736,1152]{1,0:T(8,128)S(1)} %get-tuple-element.137.refs_4_) | copy-start | bytes 10174468
  (46 other events, 180.8 us)
Sparse Core Ops, SparseCore 0:
  14.4 46.5 all-gather.7
  62.8 41.2 all-gather.11
  106.0 41.2 all-gather.9

commit v4 on v3

--- a/solution.py
+++ b/solution.py
@@ -131,7 +131,9 @@
     def __init__(self, ways, layer, cuts, g_ref, o_ref, bufs):
         self.ways, self.layer, self.cuts = ways, layer, cuts
         self.levels = ways.bit_length() - 1
-        self.g, self.o = g_ref, o_ref
+        self.home, self.o = g_ref, o_ref
+        self.g, self.load_sem = bufs[:2]
+        bufs = bufs[2:]
         n = self.levels
         self.recv, self.stage = bufs[:n], [None] + list(bufs[n : 2 * n - 1])
         bufs = bufs[2 * n - 1 :]
@@ -159,15 +161,18 @@
     def span(self, piece):
         return pl.ds(pl.multiple_of(piece * self.rows, self.rows), self.rows)
 
-    def own(self, block, piece):
-        if len(self.g.shape) == 3:
-            return self.g.at[block, self.span(piece)]
-        return self.g.at[pl.ds(pl.multiple_of(block * self.height + piece * self.rows, self.rows), self.rows)]
+    def load(self):
+        return pltpu.make_async_copy(self.home, self.g, self.load_sem)
+
+    def own(self, array, block, piece):
+        if len(array.shape) == 3:
+            return array.at[block, self.span(piece)]
+        return array.at[pl.ds(pl.multiple_of(block * self.height + piece * self.rows, self.rows), self.rows)]
 
     def copy(self, level, block, piece):
         place = block // (1 << (level + 1))
         return pltpu.make_async_remote_copy(
-            src_ref=self.own(block, piece) if level == 0 else self.stage[level].at[place, self.span(piece)],
+            src_ref=self.own(self.home, block, piece) if level == 0 else self.stage[level].at[place, self.span(piece)],
             dst_ref=self.recv[level].at[place, self.span(piece)],
             send_sem=self.sems[level][0].at[place * self.cuts + piece],
             recv_sem=self.sems[level][1].at[place * self.cuts + piece],
@@ -191,7 +196,7 @@
                 self.copy(0, block, piece).start()
 
     def total(self, level, block, piece):
-        value = self.own(block, piece)[...].astype(F32)
+        value = self.own(self.g, block, piece)[...].astype(F32)
         for j in range(level):
             self.copy(j, block, piece).wait_recv()
             value += self.recv[j][block // (1 << (j + 1)), self.span(piece), :].astype(F32)
@@ -230,7 +235,7 @@
                 self.last_copy(piece).wait_send()
 
     @staticmethod
-    def scratch(shape, ways, cuts):
+    def scratch(g, shape, ways, cuts):
         levels = ways.bit_length() - 1
         rows, width = shape
         counts = [ways >> (j + 1) for j in range(levels)]
@@ -238,7 +243,8 @@
         for count in counts + [1]:
             sems += [pltpu.SemaphoreType.DMA((count * cuts,))] * 2
         return (
-            [pltpu.VMEM((count, rows, width), BF16) for count in counts + counts[1:]]
+            [pltpu.VMEM(g.shape, BF16), pltpu.SemaphoreType.DMA]
+            + [pltpu.VMEM((count, rows, width), BF16) for count in counts + counts[1:]]
             + [pltpu.VMEM((rows, width), BF16)] * 2
             + sems
         )
@@ -265,17 +271,23 @@
     )(x)
 
 
-class Swap:
-    def __init__(self, line, layer, refs, outs, bufs):
-        self.line, self.layer = line, layer
-        self.u, self.grad, self.gain, self.ready = refs
-        self.mine, self.got, self.late = outs
-        self.sems = bufs[:2]
-        self.small = Small(self.late, self.late, bufs[2:])
+class Norm:
+    def __init__(self, line, layer, wide, trade, refs, outs, bufs):
+        self.line, self.layer, self.trade = line, layer, trade
+        self.home = refs[:2]
+        self.gain, self.ready = refs[2], refs[3] if trade else None
+        self.u, self.grad, self.load_sems = bufs[:3]
+        bufs = bufs[3:]
+        self.mine, self.late = outs[0], outs[-1]
+        self.wide = outs[1] if wide else None
+        self.got = outs[1] if trade else None
+        if trade:
+            self.sems = bufs[:2]
+            self.small = Small(self.late, self.late, bufs[2:])
         self.section = lax.axis_index("section")
         self.first = 2 * line.lag * (line.count - 1)
-        self.steps = line.pieces // 2
         self.rows = 2 * line.rows
+        self.steps = self.u.shape[0] // self.rows
 
     def span(self, index):
         return pl.ds(pl.multiple_of(index * self.rows, self.rows), self.rows)
@@ -290,7 +302,14 @@
             device_id_type=MESH,
         )
 
+    def loads(self):
+        return [
+            pltpu.make_async_copy(self.home[i], (self.u, self.grad)[i], self.load_sems.at[i]) for i in range(2)
+        ]
+
     def start(self):
+        for load in self.loads():
+            load.start()
         self.late[...] = jnp.zeros_like(self.late)
 
     def step(self, index):
@@ -298,9 +317,15 @@
         one = self.line.o[span, :].astype(F32)
         _, normed, inverse = norm_forward(self.u[span, :].astype(F32), 1.0, 0.0)
         moved, gain_part, shift_part = norm_backward(one, normed, inverse, self.gain[...])
-        self.mine[span, :] = (self.grad[span, :] + moved).astype(BF16)
+        moved = self.grad[span, :].astype(F32) + moved
+        self.mine[span, :] = moved.astype(BF16)
+        if self.wide is not None:
+            self.wide[span, :] = moved
         self.late[0:1, :] += gain_part.reshape(1, -1)
         self.late[1:2, :] += shift_part.reshape(1, -1)
+        self.late[2:3, :] += jnp.sum(moved.astype(BF16).astype(F32), axis=0, keepdims=True)
+        if not self.trade:
+            return
 
         @pl.when(self.section == self.layer)
         def _():
@@ -311,6 +336,8 @@
             self.copy(self.mine, index).start()
 
     def finish(self):
+        if not self.trade:
+            return
         for level in range(self.small.levels + 2):
             self.small.step(level)
 
@@ -330,8 +357,11 @@
         self.small.finish()
 
     @staticmethod
-    def scratch(x, ways, rows):
-        return Pass.scratch(x, rows) + Small.scratch((8, x.shape[1]), ways)
+    def scratch(x, refs, ways, rows):
+        loads = [pltpu.VMEM(ref.shape, ref.dtype) for ref in refs[:2]] + [pltpu.SemaphoreType.DMA((2,))]
+        if len(refs) == 3:
+            return loads
+        return loads + Pass.scratch(x, rows) + Small.scratch((8, x.shape[1]), ways)
 
 
 class Pass:
@@ -421,7 +451,7 @@
         return [pltpu.VMEM(shape, F32)] * (2 * n) + [pltpu.SemaphoreType.DMA((n,))] * 2
 
 
-def line_share_kernel(count, rows, lag, ways, layer, cuts, k, trade, small, passing, *refs):
+def line_share_kernel(count, rows, lag, ways, layer, cuts, k, wide, trade, small, passing, *refs):
     refs = list(refs)
 
     def take(number):
@@ -429,16 +459,15 @@
         return taken
 
     x_ref, g_refs = take(1)[0], take(k)
-    swap_refs, small_ref, pair = take(4 * trade), take(small), take(2 * passing)
+    swap_refs, small_ref, pair = take(3 + trade), take(small), take(2 * passing)
     go_refs = take(k)
-    swap_outs, small_out, got = take(3 * trade), take(small), take(passing)
+    swap_outs, small_out, got = take(2 + wide + trade), take(small), take(passing)
     o_ref = take(1)[0]
     line = Line(count, rows, lag, x_ref, o_ref, *take(2), take(4))
-    swap, extra = None, []
+    extra = []
     each = 2 * ways.bit_length() + 2
-    if trade:
-        swap = Swap(line, layer, swap_refs, swap_outs, take(2 + each))
-        swap.start()
+    swap = Norm(line, layer, wide, trade, swap_refs, swap_outs, take(5 + each if trade else 3))
+    swap.start()
     if small:
         sums = Small(small_ref[0], small_out[0], take(each))
         extra.append(sums)
@@ -451,6 +480,8 @@
         Share(ways, layer, cuts, g_refs[i], go_refs[i], scratch[i * each : (i + 1) * each]) for i in range(k)
     ]
     levels = shares[0].levels
+    for share in shares:
+        share.load().start()
     greet(line.me, count, shares[0].others())
     for share in shares:
         share.start()
@@ -458,12 +489,22 @@
     for level in range(1, levels + 2):
         first, stride = (4, 1) if level == 1 else (3 + 6 * (level - 1), 5)
         steps += [(first + i * cuts * stride, stride, level, share) for i, share in enumerate(shares)]
-    if trade:
-        steps.append((swap.first, 1, 0, swap))
+    steps.append((swap.first, 1, 0, swap))
     turns = max(line.turns, max(first + stride * (cuts - 1) + 1 for first, stride, _, item in steps if item is not swap))
 
     def turn(s, _):
         line.turn(s)
+
+        @pl.when(s == 3)
+        def _():
+            for share in shares:
+                share.load().wait()
+
+        @pl.when(s == swap.first)
+        def _():
+            for load in swap.loads():
+                load.wait()
+
         if small:
             for level in range(levels + 2):
 
@@ -499,8 +540,7 @@
     if passing:
         turns = max(turns, 2 * pass_on.steps)
     lax.fori_loop(0, turns, turn, 0)
-    if trade:
-        swap.finish()
+    swap.finish()
     for item in extra:
         item.finish()
     line.finish()
@@ -508,20 +548,25 @@
         share.finish()
 
 
-def line_share(x, grads, layer, cid, trade=(), small=None, pair=(), rows=16, lag=4):
+def line_share(x, grads, layer, cid, norm, wide=False, small=None, pair=(), rows=16, lag=4):
     count, ways = lax.axis_size("tensor"), lax.axis_size("fsdp")
     height = grads[0].shape[0] // ways
     shapes = [(height, g.shape[1]) for g in grads]
     cuts = 3 if height % (3 * TILE) == 0 else 1
     if height % TILE:
         grads = [g.reshape(ways, height, g.shape[1]) for g in grads]
-    total = jax.ShapeDtypeStruct(x.shape, BF16)
+    trade = len(norm) == 4
+    total = jax.ShapeDtypeStruct(norm[0].shape, BF16)
     scratch = Line.scratch(x, rows)
     outs = [jax.ShapeDtypeStruct(shape, F32) for shape in shapes]
-    args = [x, *grads, *trade]
+    args = [x, *grads, *norm]
+    outs.append(total)
+    if wide:
+        outs.append(jax.ShapeDtypeStruct(norm[0].shape, F32))
     if trade:
-        outs += [total, total, jax.ShapeDtypeStruct((8, x.shape[1]), F32)]
-        scratch += Swap.scratch(x, ways, rows)
+        outs.append(total)
+    outs.append(jax.ShapeDtypeStruct((8, x.shape[1]), F32))
+    scratch += Norm.scratch(x, norm, ways, rows)
     if small is not None:
         args.append(small)
         outs.append(jax.ShapeDtypeStruct(small.shape, F32))
@@ -530,13 +575,24 @@
         args += pair
         outs.append(total)
         scratch += Pass.scratch(x, rows)
+    more = x.shape != norm[0].shape
+    if more:
+        outs.append(jax.ShapeDtypeStruct(x.shape, BF16))
+    else:
+        scratch = [pltpu.VMEM(x.shape, BF16)] + scratch
+    for g, shape in zip(grads, shapes):
+        scratch += Share.scratch(g, shape, ways, cuts)
+    vmem = pl.BlockSpec(memory_space=pltpu.VMEM)
+    far = pl.BlockSpec(memory_space=pl.ANY)
+    ins = [vmem] + [far] * len(grads)
+    ins += [far, far, vmem, far] if trade else [far, far, vmem]
+    ins += [vmem] if small is not None else []
+    ins += [far, far] if pair else []
+    spots = [vmem] * len(outs)
     if trade:
-        scratch = [pltpu.VMEM(x.shape, BF16)] + scratch
-    else:
-        outs.append(total)
-    for shape in shapes:
-        scratch += Share.scratch(shape, ways, cuts)
-    vmem = pl.BlockSpec(memory_space=pltpu.VMEM)
+        spots[len(grads) + 1] = far
+    if pair:
+        spots[-1] = far
     return pl.pallas_call(
         functools.partial(
             line_share_kernel,
@@ -547,13 +603,14 @@
             layer,
             cuts,
             len(grads),
-            bool(trade),
+            wide,
+            trade,
             small is not None,
             bool(pair),
         ),
         out_shape=outs,
-        in_specs=[vmem] * len(args),
-        out_specs=[vmem] * len(outs),
+        in_specs=ins,
+        out_specs=spots,
         scratch_shapes=scratch,
         compiler_params=pltpu.CompilerParams(
             collective_id=cid, has_side_effects=True, vmem_limit_bytes=60 * 1024 * 1024
@@ -700,26 +757,25 @@
     count = two_terms[0].shape[0]
     extra_rows, last_shift = hidden[0], shifts[3]
     two = two_terms[0] if extra is None else jnp.concatenate([two_terms[0], extra])
-    grad_down, grad_up, two = line_share(
-        two, [grad_down.astype(BF16), grad_up.astype(BF16)], layer, 1 + 2 * layer
+    results = line_share(
+        two,
+        [grad_down.astype(BF16), grad_up.astype(BF16)],
+        layer,
+        1 + 2 * layer,
+        (hidden[0], grads[0], gains[1:]),
+        wide=True,
     )
-    two_terms = [two[:count].astype(F32)]
-    extra = two[count:]
+    grad_down, grad_up, grad_attn, grad_hidden, sums_two = results[:5]
+    extra = None if extra is None else results[5][count:]
     up_bias_grad = jnp.sum(pre_all.astype(F32), axis=0)
     mix_shift = jnp.sum(mix_all.astype(F32), axis=0)
-    grad_hidden, grad_attn, gain_two, shift_two, attn_shift = [], [], 0.0, 0.0, 0.0
+    gain_two, shift_two, attn_shift = sums_two[0], sums_two[1], sums_two[2]
     grad_q = []
     grad_k = 0.0
     grad_v = 0.0
-    for (first, last), part, two, rows, logs in zip(cuts, grads, two_terms, hidden, log_total):
-        normed, inverse = norm_forward(rows, gains[1], shifts[2])[1:]
-        moved, gain_part, shift_part = norm_backward(two, normed, inverse, gains[1])
-        gain_two += gain_part
-        shift_two += shift_part
-        grad_hidden.append(part.astype(F32) + moved)
-        grad_attn.append(grad_hidden[-1].astype(BF16))
-        attn_shift += jnp.sum(grad_attn[-1].astype(F32), axis=0)
-        grad_context = dot_nn(grad_attn[-1], out_t).astype(BF16).reshape(last - first, -1, HD)
+    part = grads[0]
+    for (first, last), logs in zip(cuts, log_total):
+        grad_context = dot_nn(grad_attn, out_t).astype(BF16).reshape(last - first, -1, HD)
         scores = (
             jnp.einsum("qhd,khd->hqk", queries[first:last], key_rows, preferred_element_type=F32)
             * scale
@@ -743,7 +799,7 @@
         axis=1,
     )
     context_all = jnp.concatenate(context)
-    attn_all = jnp.concatenate(grad_attn)
+    attn_all = grad_attn
     grad_out = dot_tn(attn_all, context_all)
     grad_qkv = dot_tn(normed_one, grad_proj)
     bias_sums = jnp.sum(grad_proj.astype(F32), axis=0)
@@ -754,17 +810,16 @@
     if ready is not None:
         sums = jnp.concatenate(sums + small)
         sums = jnp.pad(sums, (0, -sums.shape[0] % (8 * part.shape[1]))).reshape(-1, part.shape[1])
-        trade = (inputs[0], grad_hidden[0], gains[:1], ready)
-        grad_qkv, grad_out, mine, other, late, sums = line_share(*send, trade, sums)
+        grad_qkv, grad_out, mine, other, late, sums = line_share(
+            *send, (inputs[0], grad_hidden, gains[:1], ready), small=sums
+        )
     else:
         first = inputs[0]
         last = (extra_rows + extra.astype(F32) + last_shift).astype(BF16)
-        grad_qkv, grad_out, other, one = line_share(*send, pair=(first, last))
+        norm = (inputs[0], grad_hidden, gains[:1])
+        grad_qkv, grad_out, mine, late, other = line_share(*send, norm, pair=(first, last))
         other = (first, last, other)
-        normed, inverse = norm_forward(inputs[0].astype(F32), gains[0], shifts[0])[1:]
-        moved, gain_one, shift_one = norm_backward(one.astype(F32), normed, inverse, gains[0])
-        mine = (grad_hidden[0] + moved).astype(BF16)
-        sums += [gain_one, shift_one]
+        sums += [late[0], late[1]]
     return mine, other, (grad_qkv, grad_out, grad_up, grad_down), sums, late
 
 

time: 771 us -> 755 us (0.979)
  other arithmetic: 76.2 us -> 50.3 us
    reduce_sum x5 -> x0, other arithmetic: 21.3 us -> none  [the longest x3 11.9 us: norm_backward(): jnp.sum(grad_normed * normed, axis=0)]
    unnamed x147 -> x145, local copies, waits for them, and re-layouts: 26.1 us -> 30.8 us
  transfers between devices with their start and end apart: 3 -> 3, of which waited for: 1 -> 1; matrix products, arithmetic and copies ran while one was open for 6% -> 7% of each run, Pallas kernels for 7% -> 7%
where the time goes in v4:
time: 755 us; the launch traced here: 743 us
  Pallas kernels  452 us (60%)
  matrix products  133 us (18%)
  local copies, waits for them, and re-layouts  64.5 us (9%)
  other arithmetic  50.3 us (7%)
  between operations  16 us (2%)
  blocking collectives  15.9 us (2%)
  waiting for transfers between devices  11.7 us (2%)
    pallas_call x4, Pallas kernels, line_share(): pl.pallas_call(functools.partial(line_share_kernel, count, rows, lag, way...  294 us
    pallas_call x3, Pallas kernels, line_sum(): pl.pallas_call(functools.partial(line_sum_kernel, count, rows, lag), out_...  158 us
    dot_general x8, matrix products, dot_tn(): lax.dot_general(left, right, (((0,), (0,)), ((), ())), preferred_element_...  35.1 us
    dot_general x8, matrix products, dot_nt(): lax.dot_general(left, right, (((1,), (1,)), ((), ())), preferred_element_...  34.6 us
    dot_general x8, matrix products, dot_nn(): return jnp.dot(left, right, preferred_element_type=F32)  32.3 us
    unnamed x145, local copies, waits for them, and re-layouts  30.8 us
  transfers between devices with their start and end apart: 3, of which 1 were waited for; matrix products, arithmetic and copies ran while one was open for 7% of the time, Pallas kernels for 7%

profile of v4, /device:TPU:0, one launch (start us, length us, event | category | flops | bytes accessed | tf_op | source)
XLA Modules:
  0.0 742.9 jit_solution(8192316056809135695)
XLA Ops:
  17.5 5.9 all-reduce.3
  23.6 10.0 %all-gather.3 = bf16[8,6,288]{2,1,0:T(8,128)(2,1)S(1)} all-gather(bf16[1,6,288]{2,1,0:T(8,128)(2,1)S(1)} %maximum_bitcast_fusion), channel_id=2, replica_groups=mesh['section'=2,'tensor'=4,'fsdp'=4] {'section','fsdp'}, dimensions={0}, use_global_device_ids=true | all-gather | bytes 31104 | tf_op jit(solution)/shard_map/all_gather | solution.py:868
  50.8 10.3 %all-gather.8.cloned.1.call-done = bf16[2304,1184]{1,0:T(8,128)(2,1)} async-done(((bf16[288,1184]{1,0:T(8,128)(2,1)}), bf16[2304,1184]{1,0:T(8,128)(2,1)}) %all-gather.8.cloned.1.call-update) | async-done | bytes 5455888 | tf_op jit(solution)/shard_map/all_gather | solution.py:850
  88.8 53.7 %line_sum.3 = bf16[736,1152]{1,0:T(8,128)(2,1)} custom-call(bf16[736,1152]{1,0:T(8,128)(2,1)} %convolution_convert_fusion.7.x_ref), custom_call_target="tpu_custom_call" | custom-call | bytes 120000000 | tf_op jit(solution)/shard_map/line_sum/pallas_call | solution.py:262
  147.6 7.1 convolution_add_fusion.1
  154.7 7.2 convolution_convert_fusion.13.x_ref
  161.8 52.1 %line_sum.4 = bf16[736,1152]{1,0:T(8,128)(2,1)} custom-call(bf16[736,1152]{1,0:T(8,128)(2,1)} %convolution_convert_fusion.13.x_ref), custom_call_target="tpu_custom_call" | custom-call | bytes 120000000 | tf_op jit(solution)/shard_map/line_sum/pallas_call | solution.py:262
  242.8 52.1 %line_sum.5 = bf16[736,1152]{1,0:T(8,128)(2,1)} custom-call(bf16[736,1152]{1,0:T(8,128)(2,1)} %convolution_convert_fusion.6.x_ref), custom_call_target="tpu_custom_call" | custom-call | bytes 120000000 | tf_op jit(solution)/shard_map/line_sum/pallas_call | solution.py:262
  300.8 4.2 convolution_convert_fusion.3.refs_1_
  305.0 4.3 convert_reduce_fusion.4
  309.4 4.9 convolution_convert_fusion.2.refs_2_
  322.2 96.9 %line_share.4 = (f32[288,1076]{1,0:T(8,128)}, f32[288,1076]{1,0:T(8,128)}, bf16[736,1152]{1,0:T(8,128)(2,1)}, f32[736,1152]{1,0:T(8,128)}, f32[8,1152]{1,0:T(8,128)}, /*index=5*/bf16[1472,1152]{1,0:T(8,128)(2,1)}) custom-call(bf16[1472,1152]{1,0:T(8,128)(2,1)} %pad_maximum_fusion.refs_0_, bf16[1152,1076]{1,0:T(8,128)(2,1)} %convolution_convert_fusion.3.refs_1_, ...), custom_call_target="tpu_custom_call" | custom-call | bytes 120000000 | tf_op jit(solution)/shard_map/line_share/pallas_call | solution.py:596
  424.9 5.4 fusion.50
  439.0 5.0 convolution_convert_fusion.10.refs_0_
  449.4 60.9 %line_share.5 = (f32[288,864]{1,0:T(8,128)}, f32[288,288]{1,0:T(8,128)}, bf16[736,1152]{1,0:T(8,128)(2,1)}, f32[8,1152]{1,0:T(8,128)}, bf16[736,1152]{1,0:T(8,128)(2,1)}) custom-call(bf16[736,1152]{1,0:T(8,128)(2,1)} %convolution_convert_fusion.10.refs_0_, bf16[1152,864]{1,0:T(8,128)(2,1)} %convolution_convert_fusion.5.refs_1_, ...), custom_call_target="tpu_custom_call" | custom-call | bytes 120000000 | tf_op jit(solution)/shard_map/line_share/pallas_call | solution.py:596
  510.3 6.8 convolution_convert_fusion.1.refs_1_
  517.4 6.1 convert_reduce_fusion.5
  523.6 4.5 convolution_convert_fusion.refs_2_
  532.1 59.4 %line_share.6 = (f32[288,1076]{1,0:T(8,128)}, f32[288,1076]{1,0:T(8,128)}, bf16[736,1152]{1,0:T(8,128)(2,1)}, f32[736,1152]{1,0:T(8,128)}, f32[8,1152]{1,0:T(8,128)}) custom-call(bf16[736,1152]{1,0:T(8,128)(2,1)} %convolution_convert_fusion.9.refs_0_, bf16[1152,1076]{1,0:T(8,128)(2,1)} %convolution_convert_fusion.1.refs_1_, ...), custom_call_target="tpu_custom_call" | custom-call | bytes 120000000 | tf_op jit(solution)/shard_map/line_share/pallas_call | solution.py:596
  597.4 5.5 fusion.53
  611.4 5.1 convolution_convert_fusion.8.refs_0_
  625.6 76.6 %line_share.7 = (f32[288,864]{1,0:T(8,128)}, f32[288,288]{1,0:T(8,128)}, bf16[736,1152]{1,0:T(8,128)(2,1)}, bf16[736,1152]{1,0:T(8,128)(2,1)}, f32[8,1152]{1,0:T(8,128)}, /*index=5*/f32[16,1152]{1,0:T(8,128)}) custom-call(bf16[736,1152]{1,0:T(8,128)(2,1)} %convolution_convert_fusion.8.refs_0_, bf16[1152,864]{1,0:T(8,128)(2,1)} %convolution_convert_fusion.4.refs_1_, ...), custom_call_target="tpu_custom_call" | custom-call | bytes 120000000 | tf_op jit(solution)/shard_map/line_share/pallas_call | solution.py:596
  708.2 4.3 copy.165
  728.2 4.3 copy.166
  (274 shorter events, 174.3 us)
Async XLA Ops:
  7.2 26.6 %copy-start = (bf16[2,1,729,1152]{3,0,2,1:T(2,128)(2,1)S(1)}, bf16[2,1,729,1152]{3,0,2,1:T(2,128)(2,1)}, u32[]{:S(2)}) copy-start(bf16[2,1,729,1152]{3,0,2,1:T(2,128)(2,1)} %param.10) | copy-start | bytes 10077700
  7.2 53.9 %all-gather.8.cloned.1.call-start = ((), (), s32[]{:S(2)}) async-start(), calls=%async_computation | async-start | bytes 6635520 | tf_op jit(solution)/shard_map/all_gather | solution.py:850
  7.2 8.6 %copy-start.44 = (bf16[1,2,288]{2,1,0:T(2,128)(2,1)S(1)}, bf16[1,2,288]{2,1,0:T(2,128)(2,1)}, u32[]{:S(2)}) copy-start(bf16[1,2,288]{2,1,0:T(2,128)(2,1)} %param.13) | copy-start | bytes 3460
  7.3 8.7 %copy-start.52 = (u32[32]{0:T(128)S(1)}, u32[32]{0:T(128)}, u32[]{:S(2)}) copy-start(u32[32]{0:T(128)} %constant.78) | copy-start | bytes 388
  7.3 9.9 %copy-start.40 = (bf16[1,1076]{1,0:T(2,128)(2,1)S(1)}, bf16[1,1076]{1,0:T(2,128)(2,1)}, u32[]{:S(2)}) copy-start(bf16[1,1076]{1,0:T(2,128)(2,1)} %param.16) | copy-start | bytes 6460
  7.3 16.3 %copy-start.43 = (bf16[1,4,288]{2,1,0:T(4,128)(2,1)S(1)}, bf16[1,4,288]{2,1,0:T(4,128)(2,1)}, u32[]{:S(2)}) copy-start(bf16[1,4,288]{2,1,0:T(4,128)(2,1)} %param.19) | copy-start | bytes 6916
  7.3 16.2 %copy-start.45 = (bf16[1,2,288]{2,1,0:T(2,128)(2,1)S(1)}, bf16[1,2,288]{2,1,0:T(2,128)(2,1)}, u32[]{:S(2)}) copy-start(bf16[1,2,288]{2,1,0:T(2,128)(2,1)} %param.18) | copy-start | bytes 3460
  14.3 133.3 %all-gather.12.cloned.1.call-start = ((), (), s32[]{:S(2)}) async-start(), calls=%async_computation.2 | async-start | bytes 5971968 | tf_op jit(solution)/shard_map/all_gather | solution.py:850
  15.1 139.6 %all-gather.10.cloned.1.call-start = ((), (), s32[]{:S(2)}) async-start(), calls=%async_computation.1 | async-start | bytes 5971968 | tf_op jit(solution)/shard_map/all_gather | solution.py:850
  37.5 105.0 %copy-start.10 = (bf16[1,1,729,1152]{3,2,1,0:T(8,128)(2,1)}, bf16[1,1,729,1152]{3,2,1,0:T(8,128)(2,1)S(1)}, u32[]{:S(2)}) copy-start(bf16[1,1,729,1152]{3,2,1,0:T(8,128)(2,1)S(1)} %copy.204) | copy-start | bytes 5038852
  49.5 15.7 %copy-start.34 = (f32[736]{0:T(1024)}, f32[736]{0:T(1024)S(1)}, u32[]{:S(2)}) copy-start(f32[736]{0:T(1024)S(1)} %broadcast_multiply_fusion.3) | copy-start | bytes 8836
  50.1 15.1 %copy-start.41 = (f32[736]{0:T(1024)}, f32[736]{0:T(1024)S(1)}, u32[]{:S(2)}) copy-start(f32[736]{0:T(1024)S(1)} %add_rsqrt_fusion.3) | copy-start | bytes 8836
  50.8 14.4 %copy-start.36 = (f32[1152]{0:T(1024)}, f32[1152]{0:T(1024)S(1)}, u32[]{:S(2)}) copy-start(f32[1152]{0:T(1024)S(1)} %get-tuple-element.154) | copy-start | bytes 13828
  50.8 14.4 %copy-start.38 = (f32[1152]{0:T(1024)}, f32[1152]{0:T(1024)S(1)}, u32[]{:S(2)}) copy-start(f32[1152]{0:T(1024)S(1)} %get-tuple-element.155) | copy-start | bytes 13828
  67.2 9.7 %copy-start.17 = (bf16[736,288]{0,1:T(8,128)(2,1)}, bf16[736,288]{0,1:T(8,128)(2,1)S(1)}, u32[]{:S(2)}) copy-start(bf16[736,288]{0,1:T(8,128)(2,1)S(1)} %copy.151) | copy-start | bytes 1271812
  85.0 59.6 %copy-start.48 = (bf16[4,72,736]{2,1,0:T(8,128)(2,1)}, bf16[4,72,736]{2,1,0:T(8,128)(2,1)S(1)}, u32[]{:S(2)}) copy-start(bf16[4,72,736]{2,1,0:T(8,128)(2,1)S(1)} %fusion.57) | copy-start | bytes 1271812
  217.0 227.1 %copy-start.4 = (bf16[736,1152]{1,0:T(8,128)(2,1)}, bf16[736,1152]{1,0:T(8,128)(2,1)S(1)}, u32[]{:S(2)}) copy-start(bf16[736,1152]{1,0:T(8,128)(2,1)S(1)} %get-tuple-element.143.refs_3_.refs_6_) | copy-start | bytes 5087236
  297.2 12.2 %copy-start.8 = (f32[736,1152]{1,0:T(8,128)}, f32[736,1152]{1,0:T(8,128)S(1)}, u32[]{:S(2)}) copy-start(f32[736,1152]{1,0:T(8,128)S(1)} %get-tuple-element.141.refs_3_) | copy-start | bytes 10174468
  322.2 96.9 %copy-start.51 = (bf16[4,72,736]{2,1,0:T(8,128)(2,1)S(1)}, bf16[4,72,736]{2,1,0:T(8,128)(2,1)}, u32[]{:S(2)}) copy-start(bf16[4,72,736]{2,1,0:T(8,128)(2,1)} %copy-done.50) | copy-start | bytes 1271812
  419.1 11.2 %slice-start.3 = ((s8[9043968]{0:T(1024)(128)(4,1)}), s8[4194304]{0:T(1024)(128)(4,1)S(1)}, s32[]{:S(2)}) async-start(s8[9043968]{0:T(1024)(128)(4,1)} %bitcast.168), calls=%async_computation.6 | async-start | bytes 8388608
  510.3 17.7 %slice-start.8 = ((s8[5308416]{0:T(1024)(128)(4,1)}), s8[4194304]{0:T(1024)(128)(4,1)S(1)}, s32[]{:S(2)}) async-start(s8[5308416]{0:T(1024)(128)(4,1)} %bitcast.233), calls=%async_computation.11 | async-start | bytes 8388608
  517.4 10.6 %slice-start.9 = ((s8[5308416]{0:T(1024)(128)(4,1)}), s8[1114112]{0:T(1024)(128)(4,1)S(1)}, s32[]{:S(2)}) async-start(s8[5308416]{0:T(1024)(128)(4,1)} %bitcast.233), calls=%async_computation.12 | async-start | bytes 2228224
  532.1 59.4 %copy-start.49 = (bf16[4,72,736]{2,1,0:T(8,128)(2,1)S(1)}, bf16[4,72,736]{2,1,0:T(8,128)(2,1)}, u32[]{:S(2)}) copy-start(bf16[4,72,736]{2,1,0:T(8,128)(2,1)} %copy-done.48) | copy-start | bytes 1271812
  591.6 11.3 %slice-start = ((s8[9043968]{0:T(1024)(128)(4,1)}), s8[4194304]{0:T(1024)(128)(4,1)S(1)}, s32[]{:S(2)}) async-start(s8[9043968]{0:T(1024)(128)(4,1)} %bitcast.166), calls=%async_computation.3 | async-start | bytes 8388608
  (45 other events, 195.0 us)
Sparse Core Ops, SparseCore 0:
  14.4 46.6 all-gather.7
  63.0 41.2 all-gather.11
  106.2 41.2 all-gather.9

commit v5 on v4

--- a/solution.py
+++ b/solution.py
@@ -250,21 +250,38 @@
         )
 
 
-def line_sum_kernel(count, rows, lag, x_ref, o_ref, come, gone, *sems):
-    line = Line(count, rows, lag, x_ref, o_ref, come, gone, sems)
-    greet(line.me, count)
-    lax.fori_loop(0, line.turns, lambda s, _: (line.turn(s), 0)[1], 0)
+def line_sum_kernel(count, rows, lag, ahead, x_ref, o_ref, come, gone, *sems):
+    line = Line(count, rows, lag, x_ref, o_ref, come, gone, sems[:4])
+    fsdp = lax.axis_index("fsdp")
+    odd = fsdp % 2
+    greet(line.me, count, [{"fsdp": fsdp + 1 - 2 * odd}] if ahead else [])
+    if ahead:
+
+        @pl.when(odd == 1)
+        def _():
+            pl.semaphore_wait(sems[4], 1)
+
+    def turn(s, _):
+        line.turn(s)
+        if ahead:
+
+            @pl.when((s == min(ahead, line.turns - 1)) & (odd == 0))
+            def _():
+                pl.semaphore_signal(sems[4], inc=1, device_id={"fsdp": fsdp + 1}, device_id_type=MESH)
+        return 0
+
+    lax.fori_loop(0, line.turns, turn, 0)
     line.finish()
 
 
-def line_sum(x, cid, rows=16, lag=4):
+def line_sum(x, cid, ahead=0, rows=16, lag=4):
     count = lax.axis_size("tensor")
     return pl.pallas_call(
-        functools.partial(line_sum_kernel, count, rows, lag),
+        functools.partial(line_sum_kernel, count, rows, lag, ahead),
         out_shape=jax.ShapeDtypeStruct(x.shape, BF16),
         in_specs=[pl.BlockSpec(memory_space=pltpu.VMEM)],
         out_specs=pl.BlockSpec(memory_space=pltpu.VMEM),
-        scratch_shapes=Line.scratch(x, rows),
+        scratch_shapes=Line.scratch(x, rows) + ([pltpu.SemaphoreType.REGULAR] if ahead else []),
         compiler_params=pltpu.CompilerParams(collective_id=cid, has_side_effects=True),
         name="line_sum",
         cost_estimate=pl.CostEstimate(flops=0, bytes_accessed=120_000_000, transcendentals=0),
@@ -621,7 +638,7 @@
 
 
 def tensor_sum(value):
-    return line_sum(value.astype(BF16), 0).astype(F32)
+    return line_sum(value.astype(BF16), 5).astype(F32)
 
 
 def gelu_value(value):
@@ -696,7 +713,8 @@
         log_total.append(row_max + jnp.log(row_total))
         mixed = jnp.einsum("hqk,khd->qhd", probs, values, preferred_element_type=F32)
         context.append(mixed.astype(BF16).reshape(last - first, width))
-        attn_term = tensor_sum(dot_nt(context[-1], out_t))
+        attn_term = dot_nt(context[-1], out_t).astype(BF16)
+        attn_term = (line_sum(attn_term, 5) if is_last else line_sum(attn_term, 0, 46)).astype(F32)
         hidden.append(part.astype(F32) + attn_term + shifts[1])
     for rows in hidden:
         normed = norm_forward(rows, gains[1], shifts[2])[0].astype(BF16)
@@ -708,7 +726,7 @@
             outputs.append(None)
             stored_term = mlp_term
             continue
-        outputs.append((rows + line_sum(mlp_term, 0).astype(F32) + shifts[3]).astype(BF16))
+        outputs.append((rows + line_sum(mlp_term, 5).astype(F32) + shifts[3]).astype(BF16))
         stored_term = None
     stored = (
         inputs,

time: 755 us -> 741 us (0.981)
  Pallas kernels: 452 us -> 432 us
    pallas_call x3, Pallas kernels: 158 us -> 128 us  [line_sum(): pl.pallas_call(functools.partial(line_sum_kernel, count, rows, lag, ahead...]
    pallas_call x4, Pallas kernels: 294 us -> 304 us  [line_share(): pl.pallas_call(functools.partial(line_share_kernel, count, rows, lag, way...]
  transfers between devices with their start and end apart: 3 -> 3, of which waited for: 1 -> 2; matrix products, arithmetic and copies ran while one was open for 7% -> 7% of each run, Pallas kernels for 7% -> 6%
where the time goes in v5:
time: 741 us; the launch traced here: 729 us
  Pallas kernels  432 us (58%)
  matrix products  133 us (18%)
  local copies, waits for them, and re-layouts  64.5 us (9%)
  other arithmetic  50.2 us (7%)
  waiting for transfers between devices  17.4 us (2%)
  between operations  16 us (2%)
  blocking collectives  15.9 us (2%)
    pallas_call x4, Pallas kernels, line_share(): pl.pallas_call(functools.partial(line_share_kernel, count, rows, lag, way...  304 us
    pallas_call x3, Pallas kernels, line_sum(): pl.pallas_call(functools.partial(line_sum_kernel, count, rows, lag, ahead...  128 us
    dot_general x8, matrix products, dot_tn(): lax.dot_general(left, right, (((0,), (0,)), ((), ())), preferred_element_...  35.1 us
    dot_general x8, matrix products, dot_nt(): lax.dot_general(left, right, (((1,), (1,)), ((), ())), preferred_element_...  34.6 us
    dot_general x8, matrix products, dot_nn(): return jnp.dot(left, right, preferred_element_type=F32)  32.4 us
    unnamed x145, local copies, waits for them, and re-layouts  30.8 us
    all_gather x3, waiting for transfers between devices, gathered(): whole = lax.all_gather(piece, every, axis=0, tiled=True)  16 us
  transfers between devices with their start and end apart: 3, of which 2 were waited for; matrix products, arithmetic and copies ran while one was open for 7% of the time, Pallas kernels for 6%

profile of v5, /device:TPU:0, one launch (start us, length us, event | category | flops | bytes accessed | tf_op | source)
XLA Modules:
  0.0 729.3 jit_solution(7982615495525458122)
XLA Ops:
  17.5 5.9 all-reduce.3
  23.6 10.0 %all-gather.3 = bf16[8,6,288]{2,1,0:T(8,128)(2,1)S(1)} all-gather(bf16[1,6,288]{2,1,0:T(8,128)(2,1)S(1)} %maximum_bitcast_fusion), channel_id=2, replica_groups=mesh['section'=2,'tensor'=4,'fsdp'=4] {'section','fsdp'}, dimensions={0}, use_global_device_ids=true | all-gather | bytes 31104 | tf_op jit(solution)/shard_map/all_gather | solution.py:886
  50.8 10.3 %all-gather.8.cloned.1.call-done = bf16[2304,1184]{1,0:T(8,128)(2,1)} async-done(((bf16[288,1184]{1,0:T(8,128)(2,1)}), bf16[2304,1184]{1,0:T(8,128)(2,1)}) %all-gather.8.cloned.1.call-update) | async-done | bytes 5455888 | tf_op jit(solution)/shard_map/all_gather | solution.py:868
  88.8 40.8 %line_sum.3 = bf16[736,1152]{1,0:T(8,128)(2,1)} custom-call(bf16[736,1152]{1,0:T(8,128)(2,1)} %convolution_convert_fusion.7.x_ref), custom_call_target="tpu_custom_call" | custom-call | bytes 120000000 | tf_op jit(solution)/shard_map/line_sum/pallas_call | solution.py:279
  134.6 7.2 convolution_add_fusion.1
  141.8 5.7 all-gather.10.cloned.1.call-done
  147.5 7.2 convolution_convert_fusion.13.x_ref
  154.6 41.9 %line_sum.4 = bf16[736,1152]{1,0:T(8,128)(2,1)} custom-call(bf16[736,1152]{1,0:T(8,128)(2,1)} %convolution_convert_fusion.13.x_ref), custom_call_target="tpu_custom_call" | custom-call | bytes 120000000 | tf_op jit(solution)/shard_map/line_sum/pallas_call | solution.py:279
  225.4 45.7 %line_sum.5 = bf16[736,1152]{1,0:T(8,128)(2,1)} custom-call(bf16[736,1152]{1,0:T(8,128)(2,1)} %convolution_convert_fusion.6.x_ref), custom_call_target="tpu_custom_call" | custom-call | bytes 120000000 | tf_op jit(solution)/shard_map/line_sum/pallas_call | solution.py:279
  281.3 4.3 convert_reduce_fusion.4
  285.6 4.9 convolution_convert_fusion.2.refs_2_
  298.5 107.1 %line_share.4 = (f32[288,1076]{1,0:T(8,128)}, f32[288,1076]{1,0:T(8,128)}, bf16[736,1152]{1,0:T(8,128)(2,1)}, f32[736,1152]{1,0:T(8,128)}, f32[8,1152]{1,0:T(8,128)}, /*index=5*/bf16[1472,1152]{1,0:T(8,128)(2,1)}) custom-call(bf16[1472,1152]{1,0:T(8,128)(2,1)} %pad_maximum_fusion.refs_0_, bf16[1152,1076]{1,0:T(8,128)(2,1)} %convolution_convert_fusion.3.refs_1_, ...), custom_call_target="tpu_custom_call" | custom-call | bytes 120000000 | tf_op jit(solution)/shard_map/line_share/pallas_call | solution.py:613
  411.4 5.4 fusion.50
  425.5 5.0 convolution_convert_fusion.10.refs_0_
  435.9 60.3 %line_share.5 = (f32[288,864]{1,0:T(8,128)}, f32[288,288]{1,0:T(8,128)}, bf16[736,1152]{1,0:T(8,128)(2,1)}, f32[8,1152]{1,0:T(8,128)}, bf16[736,1152]{1,0:T(8,128)(2,1)}) custom-call(bf16[736,1152]{1,0:T(8,128)(2,1)} %convolution_convert_fusion.10.refs_0_, bf16[1152,864]{1,0:T(8,128)(2,1)} %convolution_convert_fusion.5.refs_1_, ...), custom_call_target="tpu_custom_call" | custom-call | bytes 120000000 | tf_op jit(solution)/shard_map/line_share/pallas_call | solution.py:613
  496.2 6.8 convolution_convert_fusion.1.refs_1_
  503.3 6.1 convert_reduce_fusion.5
  509.4 4.5 convolution_convert_fusion.refs_2_
  518.0 59.5 %line_share.6 = (f32[288,1076]{1,0:T(8,128)}, f32[288,1076]{1,0:T(8,128)}, bf16[736,1152]{1,0:T(8,128)(2,1)}, f32[736,1152]{1,0:T(8,128)}, f32[8,1152]{1,0:T(8,128)}) custom-call(bf16[736,1152]{1,0:T(8,128)(2,1)} %convolution_convert_fusion.9.refs_0_, bf16[1152,1076]{1,0:T(8,128)(2,1)} %convolution_convert_fusion.1.refs_1_, ...), custom_call_target="tpu_custom_call" | custom-call | bytes 120000000 | tf_op jit(solution)/shard_map/line_share/pallas_call | solution.py:613
  583.4 5.5 fusion.53
  597.3 5.1 convolution_convert_fusion.8.refs_0_
  611.6 77.0 %line_share.7 = (f32[288,864]{1,0:T(8,128)}, f32[288,288]{1,0:T(8,128)}, bf16[736,1152]{1,0:T(8,128)(2,1)}, bf16[736,1152]{1,0:T(8,128)(2,1)}, f32[8,1152]{1,0:T(8,128)}, /*index=5*/f32[16,1152]{1,0:T(8,128)}) custom-call(bf16[736,1152]{1,0:T(8,128)(2,1)} %convolution_convert_fusion.8.refs_0_, bf16[1152,864]{1,0:T(8,128)(2,1)} %convolution_convert_fusion.4.refs_1_, ...), custom_call_target="tpu_custom_call" | custom-call | bytes 120000000 | tf_op jit(solution)/shard_map/line_share/pallas_call | solution.py:613
  694.7 4.3 copy.165
  714.6 4.3 copy.166
  (274 shorter events, 178.5 us)
Async XLA Ops:
  7.2 26.6 %copy-start = (bf16[2,1,729,1152]{3,0,2,1:T(2,128)(2,1)S(1)}, bf16[2,1,729,1152]{3,0,2,1:T(2,128)(2,1)}, u32[]{:S(2)}) copy-start(bf16[2,1,729,1152]{3,0,2,1:T(2,128)(2,1)} %param.10) | copy-start | bytes 10077700
  7.2 53.9 %all-gather.8.cloned.1.call-start = ((), (), s32[]{:S(2)}) async-start(), calls=%async_computation | async-start | bytes 6635520 | tf_op jit(solution)/shard_map/all_gather | solution.py:868
  7.2 8.6 %copy-start.44 = (bf16[1,2,288]{2,1,0:T(2,128)(2,1)S(1)}, bf16[1,2,288]{2,1,0:T(2,128)(2,1)}, u32[]{:S(2)}) copy-start(bf16[1,2,288]{2,1,0:T(2,128)(2,1)} %param.13) | copy-start | bytes 3460
  7.3 8.7 %copy-start.52 = (u32[32]{0:T(128)S(1)}, u32[32]{0:T(128)}, u32[]{:S(2)}) copy-start(u32[32]{0:T(128)} %constant.78) | copy-start | bytes 388
  7.3 9.9 %copy-start.40 = (bf16[1,1076]{1,0:T(2,128)(2,1)S(1)}, bf16[1,1076]{1,0:T(2,128)(2,1)}, u32[]{:S(2)}) copy-start(bf16[1,1076]{1,0:T(2,128)(2,1)} %param.16) | copy-start | bytes 6460
  7.3 16.3 %copy-start.43 = (bf16[1,4,288]{2,1,0:T(4,128)(2,1)S(1)}, bf16[1,4,288]{2,1,0:T(4,128)(2,1)}, u32[]{:S(2)}) copy-start(bf16[1,4,288]{2,1,0:T(4,128)(2,1)} %param.19) | copy-start | bytes 6916
  7.3 16.2 %copy-start.45 = (bf16[1,2,288]{2,1,0:T(2,128)(2,1)S(1)}, bf16[1,2,288]{2,1,0:T(2,128)(2,1)}, u32[]{:S(2)}) copy-start(bf16[1,2,288]{2,1,0:T(2,128)(2,1)} %param.18) | copy-start | bytes 3460
  14.3 120.3 %all-gather.12.cloned.1.call-start = ((), (), s32[]{:S(2)}) async-start(), calls=%async_computation.2 | async-start | bytes 5971968 | tf_op jit(solution)/shard_map/all_gather | solution.py:868
  15.1 132.4 %all-gather.10.cloned.1.call-start = ((), (), s32[]{:S(2)}) async-start(), calls=%async_computation.1 | async-start | bytes 5971968 | tf_op jit(solution)/shard_map/all_gather | solution.py:868
  37.5 92.1 %copy-start.10 = (bf16[1,1,729,1152]{3,2,1,0:T(8,128)(2,1)}, bf16[1,1,729,1152]{3,2,1,0:T(8,128)(2,1)S(1)}, u32[]{:S(2)}) copy-start(bf16[1,1,729,1152]{3,2,1,0:T(8,128)(2,1)S(1)} %copy.204) | copy-start | bytes 5038852
  49.5 15.7 %copy-start.34 = (f32[736]{0:T(1024)}, f32[736]{0:T(1024)S(1)}, u32[]{:S(2)}) copy-start(f32[736]{0:T(1024)S(1)} %broadcast_multiply_fusion.3) | copy-start | bytes 8836
  50.1 15.1 %copy-start.41 = (f32[736]{0:T(1024)}, f32[736]{0:T(1024)S(1)}, u32[]{:S(2)}) copy-start(f32[736]{0:T(1024)S(1)} %add_rsqrt_fusion.3) | copy-start | bytes 8836
  50.8 14.4 %copy-start.36 = (f32[1152]{0:T(1024)}, f32[1152]{0:T(1024)S(1)}, u32[]{:S(2)}) copy-start(f32[1152]{0:T(1024)S(1)} %get-tuple-element.154) | copy-start | bytes 13828
  50.8 14.4 %copy-start.38 = (f32[1152]{0:T(1024)}, f32[1152]{0:T(1024)S(1)}, u32[]{:S(2)}) copy-start(f32[1152]{0:T(1024)S(1)} %get-tuple-element.155) | copy-start | bytes 13828
  67.2 9.7 %copy-start.17 = (bf16[736,288]{0,1:T(8,128)(2,1)}, bf16[736,288]{0,1:T(8,128)(2,1)S(1)}, u32[]{:S(2)}) copy-start(bf16[736,288]{0,1:T(8,128)(2,1)S(1)} %copy.151) | copy-start | bytes 1271812
  85.0 46.6 %copy-start.48 = (bf16[4,72,736]{2,1,0:T(8,128)(2,1)}, bf16[4,72,736]{2,1,0:T(8,128)(2,1)S(1)}, u32[]{:S(2)}) copy-start(bf16[4,72,736]{2,1,0:T(8,128)(2,1)S(1)} %fusion.57) | copy-start | bytes 1271812
  199.6 230.9 %copy-start.4 = (bf16[736,1152]{1,0:T(8,128)(2,1)}, bf16[736,1152]{1,0:T(8,128)(2,1)S(1)}, u32[]{:S(2)}) copy-start(bf16[736,1152]{1,0:T(8,128)(2,1)S(1)} %get-tuple-element.143.refs_3_.refs_6_) | copy-start | bytes 5087236
  273.4 12.2 %copy-start.8 = (f32[736,1152]{1,0:T(8,128)}, f32[736,1152]{1,0:T(8,128)S(1)}, u32[]{:S(2)}) copy-start(f32[736,1152]{1,0:T(8,128)S(1)} %get-tuple-element.141.refs_3_) | copy-start | bytes 10174468
  298.5 107.1 %copy-start.51 = (bf16[4,72,736]{2,1,0:T(8,128)(2,1)S(1)}, bf16[4,72,736]{2,1,0:T(8,128)(2,1)}, u32[]{:S(2)}) copy-start(bf16[4,72,736]{2,1,0:T(8,128)(2,1)} %copy-done.50) | copy-start | bytes 1271812
  405.6 11.2 %slice-start.3 = ((s8[9043968]{0:T(1024)(128)(4,1)}), s8[4194304]{0:T(1024)(128)(4,1)S(1)}, s32[]{:S(2)}) async-start(s8[9043968]{0:T(1024)(128)(4,1)} %bitcast.168), calls=%async_computation.6 | async-start | bytes 8388608
  496.2 17.7 %slice-start.8 = ((s8[5308416]{0:T(1024)(128)(4,1)}), s8[4194304]{0:T(1024)(128)(4,1)S(1)}, s32[]{:S(2)}) async-start(s8[5308416]{0:T(1024)(128)(4,1)} %bitcast.233), calls=%async_computation.11 | async-start | bytes 8388608
  503.3 10.6 %slice-start.9 = ((s8[5308416]{0:T(1024)(128)(4,1)}), s8[1114112]{0:T(1024)(128)(4,1)S(1)}, s32[]{:S(2)}) async-start(s8[5308416]{0:T(1024)(128)(4,1)} %bitcast.233), calls=%async_computation.12 | async-start | bytes 2228224
  518.0 59.5 %copy-start.49 = (bf16[4,72,736]{2,1,0:T(8,128)(2,1)S(1)}, bf16[4,72,736]{2,1,0:T(8,128)(2,1)}, u32[]{:S(2)}) copy-start(bf16[4,72,736]{2,1,0:T(8,128)(2,1)} %copy-done.48) | copy-start | bytes 1271812
  577.6 11.3 %slice-start = ((s8[9043968]{0:T(1024)(128)(4,1)}), s8[4194304]{0:T(1024)(128)(4,1)S(1)}, s32[]{:S(2)}) async-start(s8[9043968]{0:T(1024)(128)(4,1)} %bitcast.166), calls=%async_computation.3 | async-start | bytes 8388608
  (45 other events, 195.0 us)
Sparse Core Ops, SparseCore 0:
  14.4 46.6 all-gather.7
  63.0 41.2 all-gather.11
  106.2 41.2 all-gather.9

commit v6 on v5

--- a/solution.py
+++ b/solution.py
@@ -297,10 +297,10 @@
         bufs = bufs[3:]
         self.mine, self.late = outs[0], outs[-1]
         self.wide = outs[1] if wide else None
-        self.got = outs[1] if trade else None
+        self.both = outs[0] if trade else None
         if trade:
-            self.sems = bufs[:2]
-            self.small = Small(self.late, self.late, bufs[2:])
+            self.mine, self.sems = bufs[0], bufs[1:4]
+            self.small = Small(self.late, self.late, bufs[4:])
         self.section = lax.axis_index("section")
         self.first = 2 * line.lag * (line.count - 1)
         self.rows = 2 * line.rows
@@ -309,10 +309,13 @@
     def span(self, index):
         return pl.ds(pl.multiple_of(index * self.rows, self.rows), self.rows)
 
-    def copy(self, source, index):
+    def keep(self, source):
+        return pltpu.make_async_copy(source, self.both.at[self.section], self.sems[2].at[0])
+
+    def copy(self, source, index, slot=None):
         return pltpu.make_async_remote_copy(
             src_ref=source.at[self.span(index)],
-            dst_ref=self.got.at[self.span(index)],
+            dst_ref=self.both.at[self.section if slot is None else slot, self.span(index)],
             send_sem=self.sems[0].at[index],
             recv_sem=self.sems[1].at[index],
             device_id={"section": 1 - self.section},
@@ -327,6 +330,12 @@
     def start(self):
         for load in self.loads():
             load.start()
+        if self.trade:
+
+            @pl.when(self.section != self.layer)
+            def _():
+                self.keep(self.ready).start()
+
         self.late[...] = jnp.zeros_like(self.late)
 
     def step(self, index):
@@ -355,6 +364,11 @@
     def finish(self):
         if not self.trade:
             return
+
+        @pl.when(self.section == self.layer)
+        def _():
+            self.keep(self.mine).start()
+
         for level in range(self.small.levels + 2):
             self.small.step(level)
 
@@ -367,10 +381,19 @@
             def _():
                 self.copy(self.mine, index).wait_send()
 
-            self.copy(self.got, index).wait_recv()
+            self.copy(self.mine, index, 1 - self.section).wait_recv()
             return 0
 
         lax.fori_loop(0, self.steps, end_steps, 0)
+
+        @pl.when(self.section == self.layer)
+        def _():
+            self.keep(self.mine).wait()
+
+        @pl.when(self.section != self.layer)
+        def _():
+            self.keep(self.ready).wait()
+
         self.small.finish()
 
     @staticmethod
@@ -378,27 +401,40 @@
         loads = [pltpu.VMEM(ref.shape, ref.dtype) for ref in refs[:2]] + [pltpu.SemaphoreType.DMA((2,))]
         if len(refs) == 3:
             return loads
-        return loads + Pass.scratch(x, rows) + Small.scratch((8, x.shape[1]), ways)
+        return loads + [pltpu.VMEM(refs[0].shape, BF16)] + Pass.scratch(x, rows) + Small.scratch((8, x.shape[1]), ways)
 
 
 class Pass:
-    def __init__(self, line, pair, got, sems):
-        self.pair, self.got, self.sems = pair, got, sems
+    def __init__(self, line, pair, both, sems):
+        self.pair, self.both, self.sems = pair, both, sems
         self.section = lax.axis_index("section")
         self.rows = 2 * line.rows
-        self.steps = got.shape[0] // self.rows
-
-    def copy(self, source, index):
-        span = pl.ds(pl.multiple_of(index * self.rows, self.rows), self.rows)
+        self.steps = both.shape[1] // self.rows
+
+    def span(self, index):
+        return pl.ds(pl.multiple_of(index * self.rows, self.rows), self.rows)
+
+    def keep(self, source):
+        return pltpu.make_async_copy(source, self.both.at[self.section], self.sems[2].at[0])
+
+    def copy(self, source, index, slot=None):
+        span = self.span(index)
         return pltpu.make_async_remote_copy(
             src_ref=source.at[span],
-            dst_ref=self.got.at[span],
+            dst_ref=self.both.at[self.section if slot is None else slot, span],
             send_sem=self.sems[0].at[index],
             recv_sem=self.sems[1].at[index],
             device_id={"section": 1 - self.section},
             device_id_type=MESH,
         )
 
+    def start(self):
+        for place in range(2):
+
+            @pl.when(self.section == place)
+            def _():
+                self.keep(self.pair[place]).start()
+
     def step(self, index):
         for place in range(2):
 
@@ -414,14 +450,19 @@
                 def _():
                     self.copy(self.pair[place], index).wait_send()
 
-            self.copy(self.got, index).wait_recv()
+            self.copy(self.pair[0], index, 1 - self.section).wait_recv()
             return 0
 
         lax.fori_loop(0, self.steps, end_steps, 0)
+        for place in range(2):
+
+            @pl.when(self.section == place)
+            def _():
+                self.keep(self.pair[place]).wait()
 
     @staticmethod
     def scratch(x, rows):
-        return [pltpu.SemaphoreType.DMA((x.shape[0] // (2 * rows),))] * 2
+        return [pltpu.SemaphoreType.DMA((x.shape[0] // (2 * rows),))] * 3
 
 
 class Small:
@@ -478,18 +519,19 @@
     x_ref, g_refs = take(1)[0], take(k)
     swap_refs, small_ref, pair = take(3 + trade), take(small), take(2 * passing)
     go_refs = take(k)
-    swap_outs, small_out, got = take(2 + wide + trade), take(small), take(passing)
+    swap_outs, small_out, got = take(2 + wide), take(small), take(passing)
     o_ref = take(1)[0]
     line = Line(count, rows, lag, x_ref, o_ref, *take(2), take(4))
     extra = []
     each = 2 * ways.bit_length() + 2
-    swap = Norm(line, layer, wide, trade, swap_refs, swap_outs, take(5 + each if trade else 3))
+    swap = Norm(line, layer, wide, trade, swap_refs, swap_outs, take(7 + each if trade else 3))
     swap.start()
     if small:
         sums = Small(small_ref[0], small_out[0], take(each))
         extra.append(sums)
     if passing:
-        pass_on = Pass(line, pair, got[0], take(2))
+        pass_on = Pass(line, pair, got[0], take(3))
+        pass_on.start()
         extra.append(pass_on)
     scratch = refs
     each = len(scratch) // k
@@ -577,11 +619,10 @@
     scratch = Line.scratch(x, rows)
     outs = [jax.ShapeDtypeStruct(shape, F32) for shape in shapes]
     args = [x, *grads, *norm]
-    outs.append(total)
+    two = jax.ShapeDtypeStruct((2, *norm[0].shape), BF16)
+    outs.append(two if trade else total)
     if wide:
         outs.append(jax.ShapeDtypeStruct(norm[0].shape, F32))
-    if trade:
-        outs.append(total)
     outs.append(jax.ShapeDtypeStruct((8, x.shape[1]), F32))
     scratch += Norm.scratch(x, norm, ways, rows)
     if small is not None:
@@ -590,7 +631,7 @@
         scratch += Small.scratch(small.shape, ways)
     if pair:
         args += pair
-        outs.append(total)
+        outs.append(two)
         scratch += Pass.scratch(x, rows)
     more = x.shape != norm[0].shape
     if more:
@@ -607,7 +648,7 @@
     ins += [far, far] if pair else []
     spots = [vmem] * len(outs)
     if trade:
-        spots[len(grads) + 1] = far
+        spots[len(grads)] = far
     if pair:
         spots[-1] = far
     return pl.pallas_call(
@@ -828,7 +869,8 @@
     if ready is not None:
         sums = jnp.concatenate(sums + small)
         sums = jnp.pad(sums, (0, -sums.shape[0] % (8 * part.shape[1]))).reshape(-1, part.shape[1])
-        grad_qkv, grad_out, mine, other, late, sums = line_share(
+        mine = None
+        grad_qkv, grad_out, other, late, sums = line_share(
             *send, (inputs[0], grad_hidden, gains[:1], ready), small=sums
         )
     else:
@@ -836,7 +878,6 @@
         last = (extra_rows + extra.astype(F32) + last_shift).astype(BF16)
         norm = (inputs[0], grad_hidden, gains[:1])
         grad_qkv, grad_out, mine, late, other = line_share(*send, norm, pair=(first, last))
-        other = (first, last, other)
         sums += [late[0], late[1]]
     return mine, other, (grad_qkv, grad_out, grad_up, grad_down), sums, late
 
@@ -911,9 +952,8 @@
         outputs.append(rows[0])
         stored.append(kept)
 
-    def placed(mine, other):
-        mine, other = mine[:seq_len], other[:seq_len]
-        return jnp.where(is_first, jnp.stack([mine, other]), jnp.stack([other, mine]))[None, :, None]
+    def placed(both):
+        return both[None, :, None, :seq_len]
 
     grads = [own_grad[first:last] for first, last in cuts]
     input_grads = [None, None]
@@ -935,10 +975,9 @@
         )
         if index == 1:
             ready, grads = mine, [mine]
-            first, last, other = other
-            section_outputs = placed(jnp.where(is_first, first, last), other)
+            section_outputs = placed(other)
         else:
-            input_grads = placed(jnp.where(is_first, mine, ready), other)
+            input_grads = placed(other)
     grad_qkv, grad_out, grad_up, grad_down = [
         jnp.where(is_first, first, second) for first, second in zip(*weight_grads)
     ]

time: 741 us -> 731 us (0.987)
  other arithmetic: 50.2 us -> 40.9 us
    unnamed x145 -> x137, local copies, waits for them, and re-layouts: 30.8 us -> 29.8 us
where the time goes in v6:
time: 731 us; the launch traced here: 720 us
  Pallas kernels  432 us (59%)
  matrix products  133 us (18%)
  local copies, waits for them, and re-layouts  64.7 us (9%)
  other arithmetic  40.9 us (6%)
  waiting for transfers between devices  17.5 us (2%)
  blocking collectives  15.9 us (2%)
  between operations  15.9 us (2%)
    pallas_call x4, Pallas kernels, line_share(): pl.pallas_call(functools.partial(line_share_kernel, count, rows, lag, way...  304 us
    pallas_call x3, Pallas kernels, line_sum(): pl.pallas_call(functools.partial(line_sum_kernel, count, rows, lag, ahead...  128 us
    dot_general x8, matrix products, dot_tn(): lax.dot_general(left, right, (((0,), (0,)), ((), ())), preferred_element_...  35.1 us
    dot_general x8, matrix products, dot_nt(): lax.dot_general(left, right, (((1,), (1,)), ((), ())), preferred_element_...  34.6 us
    dot_general x8, matrix products, dot_nn(): return jnp.dot(left, right, preferred_element_type=F32)  32.4 us
    unnamed x137, local copies, waits for them, and re-layouts  29.8 us
    all_gather x3, waiting for transfers between devices, gathered(): whole = lax.all_gather(piece, every, axis=0, tiled=True)  16.1 us
  transfers between devices with their start and end apart: 3, of which 2 were waited for; matrix products, arithmetic and copies ran while one was open for 7% of the time, Pallas kernels for 6%

profile of v6, /device:TPU:0, one launch (start us, length us, event | category | flops | bytes accessed | tf_op | source)
XLA Modules:
  0.0 719.9 jit_solution(15713435338209443812)
XLA Ops:
  17.5 5.9 all-reduce.3
  23.6 10.0 %all-gather.3 = bf16[8,6,288]{2,1,0:T(8,128)(2,1)S(1)} all-gather(bf16[1,6,288]{2,1,0:T(8,128)(2,1)S(1)} %maximum_bitcast_fusion), channel_id=2, replica_groups=mesh['section'=2,'tensor'=4,'fsdp'=4] {'section','fsdp'}, dimensions={0}, use_global_device_ids=true | all-gather | bytes 31104 | tf_op jit(solution)/shard_map/all_gather | solution.py:927
  50.8 10.3 %all-gather.8.cloned.1.call-done = bf16[2304,1184]{1,0:T(8,128)(2,1)} async-done(((bf16[288,1184]{1,0:T(8,128)(2,1)}), bf16[2304,1184]{1,0:T(8,128)(2,1)}) %all-gather.8.cloned.1.call-update) | async-done | bytes 5455888 | tf_op jit(solution)/shard_map/all_gather | solution.py:909
  88.8 40.7 %line_sum.3 = bf16[736,1152]{1,0:T(8,128)(2,1)} custom-call(bf16[736,1152]{1,0:T(8,128)(2,1)} %convolution_convert_fusion.7.x_ref), custom_call_target="tpu_custom_call" | custom-call | bytes 120000000 | tf_op jit(solution)/shard_map/line_sum/pallas_call | solution.py:279
  134.5 7.2 convolution_add_fusion.1
  141.7 5.8 all-gather.10.cloned.1.call-done
  147.5 7.2 convolution_convert_fusion.13.x_ref
  154.6 41.9 %line_sum.4 = bf16[736,1152]{1,0:T(8,128)(2,1)} custom-call(bf16[736,1152]{1,0:T(8,128)(2,1)} %convolution_convert_fusion.13.x_ref), custom_call_target="tpu_custom_call" | custom-call | bytes 120000000 | tf_op jit(solution)/shard_map/line_sum/pallas_call | solution.py:279
  225.4 45.7 %line_sum.5 = bf16[736,1152]{1,0:T(8,128)(2,1)} custom-call(bf16[736,1152]{1,0:T(8,128)(2,1)} %convolution_convert_fusion.6.x_ref), custom_call_target="tpu_custom_call" | custom-call | bytes 120000000 | tf_op jit(solution)/shard_map/line_sum/pallas_call | solution.py:279
  281.2 4.3 convert_reduce_fusion.4
  285.6 4.9 convolution_convert_fusion.2.refs_2_
  298.4 107.1 %line_share.4 = (f32[288,1076]{1,0:T(8,128)}, f32[288,1076]{1,0:T(8,128)}, bf16[736,1152]{1,0:T(8,128)(2,1)}, f32[736,1152]{1,0:T(8,128)}, f32[8,1152]{1,0:T(8,128)}, /*index=5*/bf16[1472,1152]{1,0:T(8,128)(2,1)}) custom-call(bf16[1472,1152]{1,0:T(8,128)(2,1)} %pad_maximum_fusion.refs_0_, bf16[1152,1076]{1,0:T(8,128)(2,1)} %convolution_convert_fusion.3.refs_1_, ...), custom_call_target="tpu_custom_call" | custom-call | bytes 120000000 | tf_op jit(solution)/shard_map/line_share/pallas_call | solution.py:654
  411.4 5.4 fusion.48
  425.5 5.1 convolution_convert_fusion.10.refs_0_
  436.0 60.3 %line_share.5 = (f32[288,864]{1,0:T(8,128)}, f32[288,288]{1,0:T(8,128)}, bf16[736,1152]{1,0:T(8,128)(2,1)}, f32[8,1152]{1,0:T(8,128)}, bf16[2,736,1152]{2,1,0:T(8,128)(2,1)}) custom-call(bf16[736,1152]{1,0:T(8,128)(2,1)} %convolution_convert_fusion.10.refs_0_, bf16[1152,864]{1,0:T(8,128)(2,1)} %convolution_convert_fusion.5.refs_1_, ...), custom_call_target="tpu_custom_call" | custom-call | bytes 120000000 | tf_op jit(solution)/shard_map/line_share/pallas_call | solution.py:654
  496.3 6.8 convolution_convert_fusion.1.refs_1_
  503.4 6.1 convert_reduce_fusion.5
  509.5 4.5 convolution_convert_fusion.refs_2_
  518.1 59.4 %line_share.6 = (f32[288,1076]{1,0:T(8,128)}, f32[288,1076]{1,0:T(8,128)}, bf16[736,1152]{1,0:T(8,128)(2,1)}, f32[736,1152]{1,0:T(8,128)}, f32[8,1152]{1,0:T(8,128)}) custom-call(bf16[736,1152]{1,0:T(8,128)(2,1)} %convolution_convert_fusion.9.refs_0_, bf16[1152,1076]{1,0:T(8,128)(2,1)} %convolution_convert_fusion.1.refs_1_, ...), custom_call_target="tpu_custom_call" | custom-call | bytes 120000000 | tf_op jit(solution)/shard_map/line_share/pallas_call | solution.py:654
  583.4 5.5 fusion.51
  597.3 5.1 convolution_convert_fusion.8.refs_0_
  610.1 76.8 %line_share.7 = (f32[288,864]{1,0:T(8,128)}, f32[288,288]{1,0:T(8,128)}, bf16[2,736,1152]{2,1,0:T(8,128)(2,1)}, f32[8,1152]{1,0:T(8,128)}, f32[16,1152]{1,0:T(8,128)}) custom-call(bf16[736,1152]{1,0:T(8,128)(2,1)} %convolution_convert_fusion.8.refs_0_, bf16[1152,864]{1,0:T(8,128)(2,1)} %convolution_convert_fusion.4.refs_1_, ...), custom_call_target="tpu_custom_call" | custom-call | bytes 120000000 | tf_op jit(solution)/shard_map/line_share/pallas_call | solution.py:654
  690.3 4.3 copy.165
  697.9 4.3 copy.166
  (262 shorter events, 169.4 us)
Async XLA Ops:
  7.2 26.6 %copy-start = (bf16[2,1,729,1152]{3,0,2,1:T(2,128)(2,1)S(1)}, bf16[2,1,729,1152]{3,0,2,1:T(2,128)(2,1)}, u32[]{:S(2)}) copy-start(bf16[2,1,729,1152]{3,0,2,1:T(2,128)(2,1)} %param.10) | copy-start | bytes 10077700
  7.2 53.9 %all-gather.8.cloned.1.call-start = ((), (), s32[]{:S(2)}) async-start(), calls=%async_computation | async-start | bytes 6635520 | tf_op jit(solution)/shard_map/all_gather | solution.py:909
  7.2 8.6 %copy-start.40 = (bf16[1,2,288]{2,1,0:T(2,128)(2,1)S(1)}, bf16[1,2,288]{2,1,0:T(2,128)(2,1)}, u32[]{:S(2)}) copy-start(bf16[1,2,288]{2,1,0:T(2,128)(2,1)} %param.13) | copy-start | bytes 3460
  7.3 8.7 %copy-start.48 = (u32[32]{0:T(128)S(1)}, u32[32]{0:T(128)}, u32[]{:S(2)}) copy-start(u32[32]{0:T(128)} %constant.78) | copy-start | bytes 388
  7.3 9.9 %copy-start.36 = (bf16[1,1076]{1,0:T(2,128)(2,1)S(1)}, bf16[1,1076]{1,0:T(2,128)(2,1)}, u32[]{:S(2)}) copy-start(bf16[1,1076]{1,0:T(2,128)(2,1)} %param.16) | copy-start | bytes 6460
  7.3 16.3 %copy-start.39 = (bf16[1,4,288]{2,1,0:T(4,128)(2,1)S(1)}, bf16[1,4,288]{2,1,0:T(4,128)(2,1)}, u32[]{:S(2)}) copy-start(bf16[1,4,288]{2,1,0:T(4,128)(2,1)} %param.19) | copy-start | bytes 6916
  7.3 16.2 %copy-start.41 = (bf16[1,2,288]{2,1,0:T(2,128)(2,1)S(1)}, bf16[1,2,288]{2,1,0:T(2,128)(2,1)}, u32[]{:S(2)}) copy-start(bf16[1,2,288]{2,1,0:T(2,128)(2,1)} %param.18) | copy-start | bytes 3460
  14.3 120.2 %all-gather.12.cloned.1.call-start = ((), (), s32[]{:S(2)}) async-start(), calls=%async_computation.2 | async-start | bytes 5971968 | tf_op jit(solution)/shard_map/all_gather | solution.py:909
  15.1 132.4 %all-gather.10.cloned.1.call-start = ((), (), s32[]{:S(2)}) async-start(), calls=%async_computation.1 | async-start | bytes 5971968 | tf_op jit(solution)/shard_map/all_gather | solution.py:909
  37.5 92.0 %copy-start.8 = (bf16[1,1,729,1152]{3,2,1,0:T(8,128)(2,1)}, bf16[1,1,729,1152]{3,2,1,0:T(8,128)(2,1)S(1)}, u32[]{:S(2)}) copy-start(bf16[1,1,729,1152]{3,2,1,0:T(8,128)(2,1)S(1)} %copy.204) | copy-start | bytes 5038852
  49.5 15.7 %copy-start.30 = (f32[736]{0:T(1024)}, f32[736]{0:T(1024)S(1)}, u32[]{:S(2)}) copy-start(f32[736]{0:T(1024)S(1)} %broadcast_multiply_fusion.3) | copy-start | bytes 8836
  50.1 15.1 %copy-start.37 = (f32[736]{0:T(1024)}, f32[736]{0:T(1024)S(1)}, u32[]{:S(2)}) copy-start(f32[736]{0:T(1024)S(1)} %add_rsqrt_fusion.3) | copy-start | bytes 8836
  50.8 14.4 %copy-start.32 = (f32[1152]{0:T(1024)}, f32[1152]{0:T(1024)S(1)}, u32[]{:S(2)}) copy-start(f32[1152]{0:T(1024)S(1)} %get-tuple-element.152) | copy-start | bytes 13828
  50.8 14.4 %copy-start.34 = (f32[1152]{0:T(1024)}, f32[1152]{0:T(1024)S(1)}, u32[]{:S(2)}) copy-start(f32[1152]{0:T(1024)S(1)} %get-tuple-element.153) | copy-start | bytes 13828
  67.2 9.7 %copy-start.14 = (bf16[736,288]{0,1:T(8,128)(2,1)}, bf16[736,288]{0,1:T(8,128)(2,1)S(1)}, u32[]{:S(2)}) copy-start(bf16[736,288]{0,1:T(8,128)(2,1)S(1)} %copy.151) | copy-start | bytes 1271812
  85.0 46.6 %copy-start.44 = (bf16[4,72,736]{2,1,0:T(8,128)(2,1)}, bf16[4,72,736]{2,1,0:T(8,128)(2,1)S(1)}, u32[]{:S(2)}) copy-start(bf16[4,72,736]{2,1,0:T(8,128)(2,1)S(1)} %fusion.55) | copy-start | bytes 1271812
  199.6 231.0 %copy-start.10 = (bf16[736,1152]{1,0:T(8,128)(2,1)}, bf16[736,1152]{1,0:T(8,128)(2,1)S(1)}, u32[]{:S(2)}) copy-start(bf16[736,1152]{1,0:T(8,128)(2,1)S(1)} %get-tuple-element.141.refs_3_.refs_6_) | copy-start | bytes 5087236
  273.3 12.2 %copy-start.6 = (f32[736,1152]{1,0:T(8,128)}, f32[736,1152]{1,0:T(8,128)S(1)}, u32[]{:S(2)}) copy-start(f32[736,1152]{1,0:T(8,128)S(1)} %get-tuple-element.139.refs_3_) | copy-start | bytes 10174468
  298.4 107.2 %copy-start.47 = (bf16[4,72,736]{2,1,0:T(8,128)(2,1)S(1)}, bf16[4,72,736]{2,1,0:T(8,128)(2,1)}, u32[]{:S(2)}) copy-start(bf16[4,72,736]{2,1,0:T(8,128)(2,1)} %copy-done.46) | copy-start | bytes 1271812
  405.6 11.2 %slice-start.3 = ((s8[9043968]{0:T(1024)(128)(4,1)}), s8[4194304]{0:T(1024)(128)(4,1)S(1)}, s32[]{:S(2)}) async-start(s8[9043968]{0:T(1024)(128)(4,1)} %bitcast.164), calls=%async_computation.6 | async-start | bytes 8388608
  496.3 17.7 %slice-start.8 = ((s8[5308416]{0:T(1024)(128)(4,1)}), s8[4194304]{0:T(1024)(128)(4,1)S(1)}, s32[]{:S(2)}) async-start(s8[5308416]{0:T(1024)(128)(4,1)} %bitcast.229), calls=%async_computation.11 | async-start | bytes 8388608
  503.4 10.6 %slice-start.9 = ((s8[5308416]{0:T(1024)(128)(4,1)}), s8[1114112]{0:T(1024)(128)(4,1)S(1)}, s32[]{:S(2)}) async-start(s8[5308416]{0:T(1024)(128)(4,1)} %bitcast.229), calls=%async_computation.12 | async-start | bytes 2228224
  518.1 59.4 %copy-start.45 = (bf16[4,72,736]{2,1,0:T(8,128)(2,1)S(1)}, bf16[4,72,736]{2,1,0:T(8,128)(2,1)}, u32[]{:S(2)}) copy-start(bf16[4,72,736]{2,1,0:T(8,128)(2,1)} %copy-done.44) | copy-start | bytes 1271812
  577.6 11.3 %slice-start = ((s8[9043968]{0:T(1024)(128)(4,1)}), s8[4194304]{0:T(1024)(128)(4,1)S(1)}, s32[]{:S(2)}) async-start(s8[9043968]{0:T(1024)(128)(4,1)} %bitcast.162), calls=%async_computation.3 | async-start | bytes 8388608
  (41 other events, 183.5 us)
Sparse Core Ops, SparseCore 0:
  14.4 46.6 all-gather.7
  63.0 41.2 all-gather.11
  106.2 41.2 all-gather.9
